TPU v7x, 512 devices: a whole 4x8x8 slice. The times are simulated.
512 devices in a mesh: depth: 64 (over z, y), strip: 8 (over x, core).
Axes of the slice: x: 4, y: 8, z: 8, core: 2. Of those that a mesh axis runs over, the one named last changes fastest.
Arguments:
- volume: float32 [128, 512, 1024], P('strip', 'depth'), may hold values from -4.5 to 6.5
- extinction: float32 [1], replicated, may hold values from 0.0005859375 to 0.001953125
- color_map: float32 [3, 2], replicated, may hold values from -3 to 3
- light_direction: float32 [3], replicated, may hold values from -4 to 4
Outputs:
- image: float32 [4, 128, 1024], P(None, 'strip', 'depth')
All inputs are finite; a program needn't handle non-finite values.
Results may differ from a plain program's by a relative error of at most 0.000034.
Values sent between devices are 32-bit elements; how exact they have to be, the bound alone decides.
No kernel may reach another device: no remote copies, remote signals or barrier semaphores. Data moves between devices by JAX's collectives and lax.ppermute only.
A program may use at most 64 MiB of HBM per device.

v0:
```python
import jax
import jax.numpy as jnp
from jax import lax
from jax.sharding import PartitionSpec as P


def extended_2(block, sides, width):
    for axis, dim in sides:
        count = lax.axis_size(axis)
        forward = [(i, i + 1) for i in range(count - 1)]
        backward = [(target, source) for source, target in forward]
        low = lax.ppermute(
            lax.slice_in_dim(block, block.shape[dim] - width, None, axis=dim), axis, forward
        )
        high = lax.ppermute(lax.slice_in_dim(block, 0, width, axis=dim), axis, backward)
        block = jnp.concatenate([low, block, high], axis=dim)
    return block


def blur_valid(field_in, along):
    extent = field_in.shape[along]
    lower_cells = lax.slice_in_dim(field_in, 0, extent - 2, axis=along)
    middle = lax.slice_in_dim(field_in, 1, extent - 1, axis=along)
    upper_cells = lax.slice_in_dim(field_in, 2, extent, axis=along)
    return 0.25 * lower_cells + 0.5 * middle + 0.25 * upper_cells


def slope_valid(field_in, along):
    extent = field_in.shape[along]
    lower_cells = lax.slice_in_dim(field_in, 0, extent - 2, axis=along)
    upper_cells = lax.slice_in_dim(field_in, 2, extent, axis=along)
    return 0.5 * (upper_cells - lower_cells)


def smooth_all(padded):
    return blur_valid(blur_valid(blur_valid(padded, 0), 1), 2)


def gradients(padded):
    first = blur_valid(blur_valid(slope_valid(padded, 0), 1), 2)
    second = blur_valid(blur_valid(slope_valid(padded, 1), 0), 2)
    third = blur_valid(blur_valid(slope_valid(padded, 2), 0), 1)
    return (first, second, third)


def pad_columns(field_in):
    return jnp.pad(field_in, ((0, 0), (0, 0), (1, 1)))


def render_slab(smoothed, gradient, extinction, color_map, light_direction):
    facing = (
        gradient[0] * light_direction[0]
        + gradient[1] * light_direction[1]
        + gradient[2] * light_direction[2]
    )
    shading = 0.3 + 0.7 * facing * facing / (1.0 + facing * facing)
    optical = extinction[0] * jax.nn.softplus(2.0 * smoothed)
    opacity = 1.0 - jnp.exp(-optical)
    prior_depth = jnp.cumsum(optical, axis=1) - optical
    weights = jnp.exp(-prior_depth) * opacity * shading
    colors = jnp.stack(
        [
            jnp.sum(
                weights * jax.nn.sigmoid(color_map[channel, 0] * smoothed + color_map[channel, 1]),
                axis=1,
            )
            for channel in range(3)
        ],
        0,
    )
    transmit = jnp.exp(-jnp.sum(optical, axis=1))
    return jnp.concatenate([colors, transmit[None]], 0)


def local(volume, extinction, color_map, light_direction):
    row_count, slab_count, column_count = volume.shape
    groups = lax.axis_size("depth")
    extended = extended_2(volume, (("depth", 1), ("strip", 0)), 2)
    filtered = smooth_all(pad_columns(extended))
    row_global = lax.axis_index("strip") * row_count + jnp.arange(row_count + 2) - 1
    slab_global = lax.axis_index("depth") * slab_count + jnp.arange(slab_count + 2) - 1
    row_inside = (row_global >= 0) & (row_global < row_count * lax.axis_size("strip"))
    slab_inside = (slab_global >= 0) & (slab_global < slab_count * groups)
    inside = (row_inside[:, None] & slab_inside[None, :]).astype(jnp.float32)
    filtered = filtered * inside[:, :, None]
    smoothed = filtered[1:-1, 1:-1]
    gradient = gradients(pad_columns(filtered))
    partial_value = render_slab(smoothed, gradient, extinction, color_map, light_direction)
    layers = lax.all_to_all(
        partial_value[:, :, None, :], "depth", split_axis=3, concat_axis=2, tiled=True
    )
    through = jnp.cumprod(layers[3], axis=1)
    prior_pass = jnp.concatenate([jnp.ones_like(through[:, :1]), through[:, :-1]], 1)
    colors = jnp.sum(prior_pass[None] * layers[:3], axis=2)
    transmit = through[:, -1]
    return jnp.concatenate([colors, 1.0 - transmit[None]], 0)


def solution(mesh):
    in_specs = (P("strip", "depth", None), P(), P(), P())
    out_specs = P(None, "strip", "depth")
    return jax.shard_map(local, mesh=mesh, in_specs=in_specs, out_specs=out_specs, check_vma=False)
```

profile of v0, /device:TPU:3, one launch (start us, length us, event | category | flops | bytes accessed | tf_op | source)
XLA Modules:
  0.0 90.2 jit_solution(13778293491945401389)
XLA Ops:
  0.0 1.4 %fusion.38 = (f32[16,2,1024]{2,1,0:T(2,128)S(1)}, f32[16,2,1024]{2,1,0:T(2,128)S(1)}) fusion(f32[16,8,1024]{2,1,0:T(8,128)} %param.4), kind=kLoop, calls=%fused_computation.92 | loop fusion | bytes 524288 | tf_op jit(solution)/shard_map/slice | solution.py:13
  1.4 3.2 %collective-permute-start = (f32[16,2,1024]{2,1,0:T(2,128)S(1)}, f32[16,2,1024]{2,1,0:T(2,128)S(1)}, u32[]{:S(2)}, u32[]{:S(2)}) collective-permute-start(f32[16,2,1024]{2,1,0:T(2,128)S(1)} %get-tuple-element.12), channel_id=1, source_target_pairs={{0,8},{8,16},{16,24},{24,32},{32,40},{40,48},{48,56},{56,64},{64,7... | collective-permute-start | bytes 393224 | tf_op jit(solution)/shard_map/ppermute | solution.py:12
  4.6 1.3 %collective-permute-start.1 = (f32[16,2,1024]{2,1,0:T(2,128)S(1)}, f32[16,2,1024]{2,1,0:T(2,128)S(1)}, u32[]{:S(2)}, u32[]{:S(2)}) collective-permute-start(f32[16,2,1024]{2,1,0:T(2,128)S(1)} %get-tuple-element.13), channel_id=1, source_target_pairs={{8,0},{16,8},{24,16},{32,24},{40,32},{48,40},{56,48},{64,56},{72,6... | collective-permute-start | bytes 393224 | tf_op jit(solution)/shard_map/ppermute | solution.py:15
  6.7 1.6 %fusion.39 = (f32[1,1]{0,1:T(1,128)}, f32[1,1]{0,1:T(1,128)}, f32[1,1]{0,1:T(1,128)}, f32[1,1]{0,1:T(1,128)}, f32[1,1]{0,1:T(1,128)}, /*index=5*/f32[1,1]{0,1:T(1,128)}) fusion(f32[3,2]{0,1:T(2,128)} %param.6), kind=kLoop, calls=%fused_computation.93 | loop fusion | bytes 48 | tf_op jit(solution)/shard_map/slice | solution.py:64
  8.2 2.1 %collective-permute-done.1 = f32[16,2,1024]{2,1,0:T(2,128)S(1)} collective-permute-done((f32[16,2,1024]{2,1,0:T(2,128)S(1)}, f32[16,2,1024]{2,1,0:T(2,128)S(1)}, u32[]{:S(2)}, u32[]{:S(2)}) %collective-permute-start.1) | collective-permute-done | bytes 131104 | tf_op jit(solution)/shard_map/ppermute | solution.py:15
  10.3 0.9 %pad_maximum_fusion.3 = (f32[2,12,1024]{2,1,0:T(8,128)S(1)}, f32[2,12,1024]{2,1,0:T(8,128)S(1)}) fusion(f32[16,2,1024]{2,1,0:T(2,128)S(1)} %collective-permute-done.1, f32[16,8,1024]{2,1,0:T(8,128)} %param.4, f32[16,2,1024]{2,1,0:T(2,128)S(1)} %collective-permute-done), kind=kLoop, calls=%fused_computation.83 | loop fusion | flops 98304 | bytes 983040 | tf_op jit(solution)/shard_map/slice | solution.py:13
  11.2 5.1 %collective-permute-start.2 = (f32[2,12,1024]{2,1,0:T(8,128)S(1)}, f32[2,12,1024]{2,1,0:T(8,128)S(1)}, u32[]{:S(2)}, u32[]{:S(2)}) collective-permute-start(f32[2,12,1024]{2,1,0:T(8,128)S(1)} %get-tuple-element.10), channel_id=1, source_target_pairs={{0,1},{1,2},{2,3},{3,4},{4,5},{5,6},{6,7},{8,9},{9,10},{10,11},{11... | collective-permute-start | bytes 294920 | tf_op jit(solution)/shard_map/ppermute | solution.py:12
  16.3 1.9 %collective-permute-start.3 = (f32[2,12,1024]{2,1,0:T(8,128)S(1)}, f32[2,12,1024]{2,1,0:T(8,128)S(1)}, u32[]{:S(2)}, u32[]{:S(2)}) collective-permute-start(f32[2,12,1024]{2,1,0:T(8,128)S(1)} %get-tuple-element.11), channel_id=1, source_target_pairs={{1,0},{2,1},{3,2},{4,3},{5,4},{6,5},{7,6},{9,8},{10,9},{11,10},{12... | collective-permute-start | bytes 294920 | tf_op jit(solution)/shard_map/ppermute | solution.py:15
  18.9 3.7 %collective-permute-done.3 = f32[2,12,1024]{2,1,0:T(8,128)S(1)} collective-permute-done((f32[2,12,1024]{2,1,0:T(8,128)S(1)}, f32[2,12,1024]{2,1,0:T(8,128)S(1)}, u32[]{:S(2)}, u32[]{:S(2)}) %collective-permute-start.3) | collective-permute-done | bytes 98336 | tf_op jit(solution)/shard_map/ppermute | solution.py:15
  22.6 0.8 select_maximum_fusion
  24.0 0.7 fusion.10
  24.7 0.7 fusion.6
  26.5 1.1 %fusion.36 = (f32[16,1024]{1,0:T(8,128)S(1)}, f32[16,8,1024]{2,1,0:T(8,128)}) fusion(f32[18,10,1024]{2,1,0:T(8,128)S(1)} %fusion.10, f32[]{:T(128)} %bitcast.26), kind=kLoop, calls=%fused_computation.91 | loop fusion | flops 1163264 | bytes 1114116 | tf_op jit(solution)/shard_map/reduce_sum | solution.py:71
  28.1 2.3 %reduce_window_sum.11 = f32[16,8,1024]{2,1,0:T(8,128)} reduce-window(f32[16,8,1024]{2,1,0:T(8,128)} %get-tuple-element.9, f32[]{:T(128)} %constant.16.clone.1), window={size=1x8x1 pad=0_0x7_0x0_0}, to_apply=%region_0.1 | reduce-window | flops 917504 | bytes 1048580 | tf_op jit(solution)/shard_map/jit(cumsum)/reduce_window_sum | solution.py:59
  30.4 8.3 %multiply_reduce_fusion.3 = (f32[16,1024]{1,0:T(8,128)S(1)}, f32[16,1024]{1,0:T(8,128)S(1)}, f32[16,1024]{1,0:T(8,128)S(1)}) fusion(f32[18,10,1024]{2,1,0:T(8,128)S(1)} %fusion.10, f32[]{:T(128)} %bitcast.5, f32[]{:T(128)} %bitcast.4, f32[]{:T(128)} %bitcast.11, f32[]{:T(128)} %bitcast.10, f32[]{:T(128)} %bitcast.8, f32[]{:T(128)} %bitcast.7, f32[]{:T(128)} %bitcast.3, ...), kind=kLoop, calls=%fused_computation.79 | loop fusion | flops 6897664 | bytes 6488100 | tf_op jit(solution)/shard_map/reduce_sum | solution.py:63
  38.8 0.8 copy.12
  39.6 1.5 %bitcast_bitcast_fusion = f32[1024,1,4,16]{3,2,1,0:T(4,128)} fusion(f32[4,16,1024]{1,0,2:T(4,128)S(1)} %copy.12), kind=kLoop, calls=%fused_computation.95 | loop fusion | bytes 524288
  41.1 3.2 %reshape.83 = f32[64,1,1024]{2,1,0:T(1,128)S(1)} reshape(f32[1024,1,4,16]{3,2,1,0:T(4,128)} %bitcast_bitcast_fusion) | data formatting | bytes 524288
  44.3 30.7 %all_to_all.4 = f32[64,1,1024]{2,1,0:T(1,128)S(1)} all-to-all(f32[64,1,1024]{2,1,0:T(1,128)S(1)} %reshape.83), channel_id=1, replica_groups=mesh['depth'=64,'strip'=8] {'depth'}, dimensions={0} | all-to-all | bytes 524288 | tf_op jit(solution)/shard_map/all_to_all | solution.py:89
  75.5 1.3 %reduce = f32[64,1024]{1,0:T(8,128)S(1)} reduce(f32[64,1,1024]{2,1,0:T(1,128)S(1)} %all_to_all.4, f32[]{:T(128)} %broadcast.177), dimensions={1}, to_apply=%all_to_all.2.reduce_sub_computation | reduce | bytes 524292 | tf_op jit(solution)/shard_map/all_to_all | solution.py:89
  76.8 1.5 %reshape.84 = f32[1024,1,4,16]{3,2,1,0:T(4,128)S(1)} reshape(f32[64,1024]{1,0:T(8,128)S(1)} %reduce) | data formatting | bytes 524288
  79.0 6.3 %fusion.41 = f32[16,64,16]{2,0,1:T(8,128)S(1)} fusion(f32[16,64,16]{2,0,1:T(8,128)S(1)} %copy.14), kind=kOutput, calls=%fused_computation.96 | output fusion | flops 1032192 | bytes 131072 | tf_op jit(solution)/shard_map/jit(cumprod)/reduce_window | solution.py:92
  85.6 2.2 %copy.19 = f32[3,16,64,16]{3,2,1,0:T(8,128)} copy(f32[3,16,64,16]{1,0,3,2:T(4,128)S(1)} %bitcast.28) | data formatting | bytes 393216 | tf_op jit(solution)/shard_map/slice | solution.py:94
  87.9 1.7 %multiply_reduce_fusion = f32[3,16,16]{2,1,0:T(8,128)S(1)} fusion(f32[3,16,64,16]{3,2,1,0:T(8,128)} %copy.19, f32[16,64,16]{2,1,0:T(8,128)S(1)} %concatenate.18.clone), kind=kLoop, calls=%fused_computation.2 | loop fusion | flops 97536 | bytes 265216 | tf_op jit(solution)/shard_map/reduce_sum | solution.py:94
  (26 shorter events, 5.0 us)
Async XLA Ops:
  0.0 22.6 %copy-start = (f32[16,8,1024]{2,1,0:T(8,128)S(1)}, f32[16,8,1024]{2,1,0:T(8,128)}, u32[]{:S(2)}) copy-start(f32[16,8,1024]{2,1,0:T(8,128)} %param.4) | copy-start | bytes 1572868
  0.0 18.3 %copy-start.1 = (f32[3]{0:T(128)S(1)}, f32[3]{0:T(128)}, u32[]{:S(2)}) copy-start(f32[3]{0:T(128)} %param.7) | copy-start | bytes 40
  1.4 6.9 %collective-permute-start = (f32[16,2,1024]{2,1,0:T(2,128)S(1)}, f32[16,2,1024]{2,1,0:T(2,128)S(1)}, u32[]{:S(2)}, u32[]{:S(2)}) collective-permute-start(f32[16,2,1024]{2,1,0:T(2,128)S(1)} %get-tuple-element.12), channel_id=1, source_target_pairs={{0,8},{8,16},{16,24},{24,32},{32,40},{40,48},{48,56},{56,64},{64,7... | collective-permute-start | bytes 393224 | tf_op jit(solution)/shard_map/ppermute | solution.py:12
  4.6 5.7 %collective-permute-start.1 = (f32[16,2,1024]{2,1,0:T(2,128)S(1)}, f32[16,2,1024]{2,1,0:T(2,128)S(1)}, u32[]{:S(2)}, u32[]{:S(2)}) collective-permute-start(f32[16,2,1024]{2,1,0:T(2,128)S(1)} %get-tuple-element.13), channel_id=1, source_target_pairs={{8,0},{16,8},{24,16},{32,24},{40,32},{48,40},{56,48},{64,56},{72,6... | collective-permute-start | bytes 393224 | tf_op jit(solution)/shard_map/ppermute | solution.py:15
  11.2 7.7 %collective-permute-start.2 = (f32[2,12,1024]{2,1,0:T(8,128)S(1)}, f32[2,12,1024]{2,1,0:T(8,128)S(1)}, u32[]{:S(2)}, u32[]{:S(2)}) collective-permute-start(f32[2,12,1024]{2,1,0:T(8,128)S(1)} %get-tuple-element.10), channel_id=1, source_target_pairs={{0,1},{1,2},{2,3},{3,4},{4,5},{5,6},{6,7},{8,9},{9,10},{10,11},{11... | collective-permute-start | bytes 294920 | tf_op jit(solution)/shard_map/ppermute | solution.py:12
  16.3 6.3 %collective-permute-start.3 = (f32[2,12,1024]{2,1,0:T(8,128)S(1)}, f32[2,12,1024]{2,1,0:T(8,128)S(1)}, u32[]{:S(2)}, u32[]{:S(2)}) collective-permute-start(f32[2,12,1024]{2,1,0:T(8,128)S(1)} %get-tuple-element.11), channel_id=1, source_target_pairs={{1,0},{2,1},{3,2},{4,3},{5,4},{6,5},{7,6},{9,8},{10,9},{11,10},{12... | collective-permute-start | bytes 294920 | tf_op jit(solution)/shard_map/ppermute | solution.py:15
where the time goes:
time: 90.7 us; the launch traced here: 90.2 us
  blocking collectives  30.7 us (34%)
  other arithmetic  27 us (30%)
  local copies, waits for them, and re-layouts  14.3 us (16%)
  starting transfers between devices  11.5 us (13%)
  waiting for transfers between devices  5.76 us (6%)
    all_to_all x1, blocking collectives, local(): lax.all_to_all(partial_value[:, :, None, :], 'depth', split_axis=3, conca...  30.7 us
    reduce_sum x1, other arithmetic, render_slab(): jnp.sum(weights * jax.nn.sigmoid(color_map[channel, 0] * smoothed + color...  8.34 us
    ppermute x2, starting transfers between devices, extended_2(): lax.ppermute(lax.slice_in_dim(block, block.shape[dim] - width, None, axis...  8.32 us
    unnamed x8, local copies, waits for them, and re-layouts  6.35 us
    another operation x1, other arithmetic, local(): through = jnp.cumprod(layers[3], axis=1)  6.33 us
    ppermute x2, waiting for transfers between devices, extended_2(): lax.ppermute(lax.slice_in_dim(block, 0, width, axis=dim), axis, backward)  5.76 us
    ppermute x2, starting transfers between devices, extended_2(): lax.ppermute(lax.slice_in_dim(block, 0, width, axis=dim), axis, backward)  3.21 us
    another operation x1, other arithmetic, render_slab(): prior_depth = jnp.cumsum(optical, axis=1) - optical  2.28 us
  transfers between devices with their start and end apart: 4, of which 2 were waited for; matrix products, arithmetic and copies ran while one was open for 3% of the time, Pallas kernels for 0%

commit v1 on v0

v1 whole, which is shorter than its diff:
```python
import functools

import jax
import jax.numpy as jnp
from jax import lax
from jax.experimental import pallas as pl
from jax.experimental.pallas import tpu as pltpu
from jax.sharding import PartitionSpec as P

ROWS, SLABS, SUB, LANE = 16, 8, 8, 128
VM = pl.BlockSpec(memory_space=pltpu.VMEM)
SM = pl.BlockSpec(memory_space=pltpu.SMEM)


def cells(x_ref, row, slab):
    return x_ref[pl.ds(row * 64 + slab, SUB, stride=SLABS), :]


def pack_depth(x_ref, low_ref, high_ref):
    for row in range(ROWS):
        for k in range(2):
            low_ref[k, row] = cells(x_ref, row, k)
            high_ref[k, row] = cells(x_ref, row, SLABS - 2 + k)


def pack_strip(x_ref, before_ref, after_ref, low_ref, high_ref):
    for k in range(2):
        low_ref[k] = before_ref[k, 0:2]
        high_ref[k] = before_ref[k, ROWS - 2 : ROWS]
        low_ref[SLABS + 2 + k] = after_ref[k, 0:2]
        high_ref[SLABS + 2 + k] = after_ref[k, ROWS - 2 : ROWS]
        for slab in range(SLABS):
            low_ref[2 + slab, k] = cells(x_ref, k, slab)
            high_ref[2 + slab, k] = cells(x_ref, ROWS - 2 + k, slab)


def column_neighbours(v):
    lane = lax.broadcasted_iota(jnp.int32, (SUB, LANE), 1)
    sub = lax.broadcasted_iota(jnp.int32, (SUB, LANE), 0)
    a = pltpu.roll(v, 1, 1)
    b = pltpu.roll(a, 1, 0)
    prev = jnp.where(lane == 0, jnp.where(sub == 0, 0.0, b), a)
    a = pltpu.roll(v, LANE - 1, 1)
    b = pltpu.roll(a, SUB - 1, 0)
    following = jnp.where(lane == LANE - 1, jnp.where(sub == SUB - 1, 0.0, b), a)
    return prev, following


def log1p_unit(e):
    t = e / (2.0 + e)
    q = t * t
    s = 1.0 / 13.0
    for d in (11.0, 9.0, 7.0, 5.0, 3.0):
        s = s * q + 1.0 / d
    return 2.0 * t + 2.0 * t * (q * s)


def render(ext_ref, cmap_ref, light_ref, edge_ref, x_ref, before_ref, after_ref,
           up_ref, down_ref, out_ref, z_ref, s_ref, ap_ref, am_ref, y_ref, part_ref):
    def slab_sums(v):
        e = [v[k] + v[k + 1] for k in range(SLABS + 3)]
        return [e[k] + e[k + 1] for k in range(SLABS + 2)]

    for k, ref in ((0, up_ref), (18, down_ref)):
        for j in range(2):
            z = slab_sums([ref[slab, j] for slab in range(SLABS + 4)])
            for slab in range(SLABS + 2):
                z_ref[k + j, slab] = z[slab]

    def first(row, _):
        v = [before_ref[k, row] for k in range(2)]
        v += [cells(x_ref, row, slab) for slab in range(SLABS)]
        v += [after_ref[k, row] for k in range(2)]
        z = slab_sums(v)
        for slab in range(SLABS + 2):
            z_ref[row + 2, slab] = z[slab]
        return 0

    lax.fori_loop(0, ROWS, first, 0)

    edge_up, edge_down, edge_before, edge_after = (edge_ref[i] for i in range(4))
    half_l0 = light_ref[0] * 0.5
    quarter_l1 = light_ref[1] * 0.5 * 0.25 * 0.25
    quarter_l2 = light_ref[2] * 0.5 * 0.25 * 0.25
    scale_p = half_l0 * 0.25 * 0.25

    def second(row, _):
        inside = jnp.where(row == 0, edge_up, jnp.where(row == ROWS + 1, edge_down, 1.0))
        scale = inside * (1.0 / 64.0)
        u, w = [], []
        for slab in range(SLABS + 2):
            mid = z_ref[row + 1, slab]
            m = (z_ref[row, slab] + mid) + (mid + z_ref[row + 2, slab])
            prev, following = column_neighbours(m)
            factor = scale
            if slab == 0:
                factor = scale * edge_before
            if slab == SLABS + 1:
                factor = scale * edge_after
            s = ((prev + following) + (m + m)) * factor
            if 1 <= slab <= SLABS:
                s_ref[row, slab - 1] = s
            prev, following = column_neighbours(s)
            u.append((prev + following) + (s + s))
            w.append(following - prev)
        for slab in range(SLABS):
            p = (u[slab] + u[slab + 1]) + (u[slab + 1] + u[slab + 2])
            q = u[slab + 2] - u[slab]
            t = (w[slab] + w[slab + 1]) + (w[slab + 1] + w[slab + 2])
            y = quarter_l1 * q + quarter_l2 * t
            p = scale_p * p
            ap_ref[row, slab] = y + p
            am_ref[row, slab] = y - p
            y_ref[row, slab] = y + y
        return 0

    lax.fori_loop(0, ROWS + 2, second, 0)

    ext = ext_ref[0]
    slopes = [cmap_ref[c, 0] * 0.5 for c in range(3)]
    offsets = [cmap_ref[c, 1] * 0.5 for c in range(3)]

    def third(row, _):
        through = None
        colors = [None] * 3
        for slab in range(SLABS):
            s = s_ref[row + 1, slab]
            facing = (ap_ref[row + 2, slab] + am_ref[row, slab]) + y_ref[row + 1, slab]
            shading = 1.0 - 0.7 / (1.0 + facing * facing)
            z = s + s
            soft = jnp.maximum(z, 0.0) + log1p_unit(jnp.exp(-jnp.abs(z)))
            clear = jnp.exp(-ext * soft)
            weight = (1.0 - clear) * shading
            if through is None:
                through = clear
            else:
                weight = weight * through
                through = through * clear
            for c in range(3):
                value = weight * (0.5 * jnp.tanh(slopes[c] * s + offsets[c]) + 0.5)
                colors[c] = value if colors[c] is None else colors[c] + value
        for c in range(3):
            part_ref[c, row] = colors[c]
        part_ref[3, row] = through
        return 0

    lax.fori_loop(0, ROWS, third, 0)

    chunk = lax.broadcasted_iota(jnp.int32, (SUB, LANE), 1) // 16
    for g in range(8):
        v = [part_ref[g // 2, (g % 2) * 8 + i] for i in range(8)]
        for bit in (4, 2, 1):
            upper = (chunk & bit) != 0
            for i in range(8):
                if i & bit == 0:
                    lo, hi = v[i], v[i + bit]
                    v[i] = jnp.where(upper, pltpu.roll(hi, 16 * bit, 1), lo)
                    v[i + bit] = jnp.where(upper, hi, pltpu.roll(lo, LANE - 16 * bit, 1))
        for m in range(8):
            out_ref[pl.ds(m * 8 + g, SUB, stride=64), :] = v[m]


def composite(parts_ref, out_ref, tmp_ref):
    sub = lax.broadcasted_iota(jnp.int32, (SUB, LANE), 0)
    is_clear = sub >= 6
    through = jnp.ones((SUB, LANE), jnp.float32)
    total = jnp.zeros((SUB, LANE), jnp.float32)
    for d in range(parts_ref.shape[0] // SUB):
        x = parts_ref[d * SUB : (d + 1) * SUB, :]
        total = total + through * x
        m = jnp.where(is_clear, x, 1.0)
        m = m * pltpu.roll(m, 2, 0)
        m = m * pltpu.roll(m, 4, 0)
        through = through * m
    result = jnp.where(is_clear, 1.0 - through, total)
    for i in range(8):
        moved = result if i == 0 else pltpu.roll(result, LANE - 16 * i, 1)
        tmp_ref[pl.ds(i, SUB, stride=SUB), :] = moved
    out_ref[...] = tmp_ref[:, 0:16]


def f32(*shape):
    return jax.ShapeDtypeStruct(shape, jnp.float32)


def local(volume, extinction, color_map, light_direction):
    strips, groups = lax.axis_size("strip"), lax.axis_size("depth")
    x = volume.reshape(ROWS, SLABS, SUB, LANE).transpose(0, 2, 1, 3).reshape(ROWS * 64, LANE)

    def pairs(count):
        forward = [(i, i + 1) for i in range(count - 1)]
        return forward, [(b, a) for a, b in forward]

    low, high = pl.pallas_call(
        pack_depth, in_specs=[VM], out_specs=[VM, VM], name="pack_depth",
        out_shape=[f32(2, ROWS, SUB, LANE)] * 2,
    )(x)
    forward, backward = pairs(groups)
    before = lax.ppermute(high, "depth", forward)
    after = lax.ppermute(low, "depth", backward)
    low, high = pl.pallas_call(
        pack_strip, in_specs=[VM] * 3, out_specs=[VM, VM], name="pack_strip",
        out_shape=[f32(SLABS + 4, 2, SUB, LANE)] * 2,
    )(x, before, after)
    forward, backward = pairs(strips)
    up = lax.ppermute(high, "strip", forward)
    down = lax.ppermute(low, "strip", backward)

    strip, group = lax.axis_index("strip"), lax.axis_index("depth")
    edges = jnp.stack([strip > 0, strip < strips - 1, group > 0, group < groups - 1])
    blocks = pl.pallas_call(
        render, in_specs=[SM] * 4 + [VM] * 5, out_specs=VM, name="render",
        out_shape=f32(groups * SUB, LANE),
        scratch_shapes=[
            pltpu.VMEM((ROWS + 4, SLABS + 2, SUB, LANE), jnp.float32),
            *[pltpu.VMEM((ROWS + 2, SLABS, SUB, LANE), jnp.float32)] * 4,
            pltpu.VMEM((4, ROWS, SUB, LANE), jnp.float32),
        ],
    )(extinction, color_map, light_direction, edges.astype(jnp.float32), x, before, after, up, down)
    layers = lax.all_to_all(
        blocks.reshape(groups, SUB, LANE), "depth", split_axis=0, concat_axis=0, tiled=True
    )
    image = pl.pallas_call(
        composite, in_specs=[VM], out_specs=VM, name="composite",
        out_shape=f32(64, 16), scratch_shapes=[pltpu.VMEM((64, LANE), jnp.float32)],
    )(layers.reshape(groups * SUB, LANE))
    return image.reshape(4, 16, 16)


def solution(mesh):
    in_specs = (P("strip", "depth", None), P(), P(), P())
    out_specs = P(None, "strip", "depth")
    return jax.shard_map(local, mesh=mesh, in_specs=in_specs, out_specs=out_specs, check_vma=False)
```

time: 90.7 us -> 65.4 us (0.72)
  other arithmetic: 27 us -> 0.66 us
  local copies, waits for them, and re-layouts: 14.3 us -> 1.97 us
  Pallas kernels: 0 us -> 12.3 us
  waiting for transfers between devices: 5.76 us -> 6.82 us
    pallas_call x0 -> x4, Pallas kernels: none -> 12.3 us  [the longest x1 6.98 us: local(): pl.pallas_call(render, in_specs=[SM] * 4 + [VM] * 5, out_specs=VM, name='...]
    reduce_sum x3 -> x0, other arithmetic: 11.2 us -> none  [the longest x1 8.34 us: render_slab(): jnp.sum(weights * jax.nn.sigmoid(color_map[channel, 0] * smoothed + color...]
    another operation x2 -> x0, other arithmetic: 8.61 us -> none  [the longest x1 6.33 us: local(): through = jnp.cumprod(layers[3], axis=1)]
    slice x6 -> x0, local copies, waits for them, and re-layouts: 6.38 us -> none  [the longest x1 2.21 us: local(): colors = jnp.sum(prior_pass[None] * layers[:3], axis=2)]
    unnamed x8 -> x11, local copies, waits for them, and re-layouts: 6.35 us -> 1.97 us
    mul x4 -> x0, other arithmetic: 2.48 us -> none  [the longest x3 1.76 us: slope_valid(): return 0.5 * (upper_cells - lower_cells)]
    concatenate x3 -> x0, other arithmetic: 1.4 us -> none  [the longest x1 0.76 us: extended_2(): block = jnp.concatenate([low, block, high], axis=dim)]
    all_to_all x1 -> x0, other arithmetic: 1.26 us -> none  [local(): lax.all_to_all(partial_value[:, :, None, :], 'depth', split_axis=3, conca...]
  transfers between devices with their start and end apart: 4 -> 4, of which waited for: 2 -> 2; matrix products, arithmetic and copies ran while one was open for 3% -> 2% of each run, Pallas kernels for 0% -> 0%
where the time goes in v1:
time: 65.4 us; the launch traced here: 65 us
  blocking collectives  31 us (47%)
  Pallas kernels  12.3 us (19%)
  starting transfers between devices  11.5 us (18%)
  waiting for transfers between devices  6.82 us (10%)
  local copies, waits for them, and re-layouts  1.97 us (3%)
  between operations  0.72 us (1%)
  other arithmetic  0.66 us (1%)
    all_to_all x1, blocking collectives, local(): lax.all_to_all(blocks.reshape(groups, SUB, LANE), 'depth', split_axis=0,...  31 us
    pallas_call x1, Pallas kernels, local(): pl.pallas_call(render, in_specs=[SM] * 4 + [VM] * 5, out_specs=VM, name='...  6.98 us
    ppermute x1, starting transfers between devices, local(): up = lax.ppermute(high, 'strip', forward)  5.1 us
    ppermute x1, waiting for transfers between devices, local(): down = lax.ppermute(low, 'strip', backward)  3.55 us
    ppermute x1, waiting for transfers between devices, local(): after = lax.ppermute(low, 'depth', backward)  3.26 us
    ppermute x1, starting transfers between devices, local(): before = lax.ppermute(high, 'depth', forward)  3.2 us
    unnamed x11, local copies, waits for them, and re-layouts  1.97 us
    ppermute x1, starting transfers between devices, local(): down = lax.ppermute(low, 'strip', backward)  1.92 us
  transfers between devices with their start and end apart: 4, of which 2 were waited for; matrix products, arithmetic and copies ran while one was open for 2% of the time, Pallas kernels for 0%

profile of v1, /device:TPU:3, one launch (start us, length us, event | category | flops | bytes accessed | tf_op | source)
XLA Modules:
  0.0 65.0 jit_solution(6102243819867041873)
XLA Ops:
  0.0 1.8 %pack_depth.1 = (f32[2,16,8,128]{3,2,1,0:T(8,128)}, f32[2,16,8,128]{3,2,1,0:T(8,128)}) custom-call(f32[1024,128]{1,0:T(8,128)} %bitcast.12), custom_call_target="tpu_custom_call" | custom-call | tf_op jit(solution)/shard_map/pack_depth/pallas_call | solution.py:194
  1.8 3.2 %collective-permute-start = (f32[2,16,8,128]{3,2,1,0:T(8,128)}, f32[2,16,8,128]{3,2,1,0:T(8,128)S(1)}, u32[]{:S(2)}, u32[]{:S(2)}) collective-permute-start(f32[2,16,8,128]{3,2,1,0:T(8,128)} %get-tuple-element.9), channel_id=1, source_target_pairs={{0,8},{8,16},{16,24},{24,32},{32,40},{40,48},{48,56},{56,64},{64,7... | collective-permute-start | bytes 393224 | tf_op jit(solution)/shard_map/ppermute | solution.py:199
  5.0 1.3 %collective-permute-start.1 = (f32[2,16,8,128]{3,2,1,0:T(8,128)}, f32[2,16,8,128]{3,2,1,0:T(8,128)S(1)}, u32[]{:S(2)}, u32[]{:S(2)}) collective-permute-start(f32[2,16,8,128]{3,2,1,0:T(8,128)} %get-tuple-element.10), channel_id=1, source_target_pairs={{8,0},{16,8},{24,16},{32,24},{40,32},{48,40},{56,48},{64,56},{72,6... | collective-permute-start | bytes 393224 | tf_op jit(solution)/shard_map/ppermute | solution.py:200
  6.3 0.0 copy-start.4
  7.0 0.0 copy-done.4
  7.0 0.7 %copy.5.cmap_ref = f32[3,2]{1,0:T(4,128)} copy(f32[3,2]{0,1:T(2,128)S(1)} %copy-done.4) | data formatting | bytes 48 | tf_op args[2]
  7.7 0.0 collective-permute-done.before_ref
  7.7 0.0 copy-start
  7.7 3.3 %collective-permute-done.1.after_ref = f32[2,16,8,128]{3,2,1,0:T(8,128)S(1)} collective-permute-done((f32[2,16,8,128]{3,2,1,0:T(8,128)}, f32[2,16,8,128]{3,2,1,0:T(8,128)S(1)}, u32[]{:S(2)}, u32[]{:S(2)}) %collective-permute-start.1) | collective-permute-done | bytes 131104 | tf_op jit(solution)/shard_map/ppermute | solution.py:200
  10.9 0.0 copy-done
  10.9 0.0 copy-start.1
  10.9 0.6 copy-done.1
  11.6 1.8 %pack_strip.1 = (f32[12,2,8,128]{3,2,1,0:T(8,128)}, f32[12,2,8,128]{3,2,1,0:T(8,128)}) custom-call(f32[1024,128]{1,0:T(8,128)} %bitcast.13, f32[2,16,8,128]{3,2,1,0:T(8,128)} %copy-done, f32[2,16,8,128]{3,2,1,0:T(8,128)} %copy-done.1), custom_call_target="tpu_custom_call" | custom-call | tf_op jit(solution)/shard_map/pack_strip/pallas_call | solution.py:201
  13.4 5.1 %collective-permute-start.2 = (f32[12,2,8,128]{3,2,1,0:T(8,128)}, f32[12,2,8,128]{3,2,1,0:T(8,128)S(1)}, u32[]{:S(2)}, u32[]{:S(2)}) collective-permute-start(f32[12,2,8,128]{3,2,1,0:T(8,128)} %get-tuple-element.11), channel_id=1, source_target_pairs={{0,1},{1,2},{2,3},{3,4},{4,5},{5,6},{6,7},{8,9},{9,10},{10,11},{11... | collective-permute-start | bytes 294920 | tf_op jit(solution)/shard_map/ppermute | solution.py:206
  18.5 1.9 %collective-permute-start.3 = (f32[12,2,8,128]{3,2,1,0:T(8,128)}, f32[12,2,8,128]{3,2,1,0:T(8,128)S(1)}, u32[]{:S(2)}, u32[]{:S(2)}) collective-permute-start(f32[12,2,8,128]{3,2,1,0:T(8,128)} %get-tuple-element.12), channel_id=1, source_target_pairs={{1,0},{2,1},{3,2},{4,3},{5,4},{6,5},{7,6},{9,8},{10,9},{11,10},{12... | collective-permute-start | bytes 294920 | tf_op jit(solution)/shard_map/ppermute | solution.py:207
  20.4 0.7 %add_convert_fusion.edge_ref = f32[4]{0:T(128)} fusion(pred[1]{0:T(512)(128)(4,1)} %bitcast.3, pred[1]{0:T(512)(128)(4,1)} %bitcast.2, pred[1]{0:T(512)(128)(4,1)} %bitcast.1, pred[1]{0:T(512)(128)(4,1)} %bitcast), kind=kLoop, calls=%fused_computation | loop fusion | flops 16 | bytes 20 | tf_op jit(solution)/shard_map/convert_element_type | solution.py:219
  21.1 0.0 collective-permute-done.2.up_ref
  21.1 0.0 copy-start.2
  21.1 3.6 %collective-permute-done.3.down_ref = f32[12,2,8,128]{3,2,1,0:T(8,128)S(1)} collective-permute-done((f32[12,2,8,128]{3,2,1,0:T(8,128)}, f32[12,2,8,128]{3,2,1,0:T(8,128)S(1)}, u32[]{:S(2)}, u32[]{:S(2)}) %collective-permute-start.3) | collective-permute-done | bytes 98336 | tf_op jit(solution)/shard_map/ppermute | solution.py:207
  24.7 0.0 copy-done.2
  24.7 0.6 copy-done.3
  25.3 7.0 %render.1 = f32[512,128]{1,0:T(8,128)} custom-call(f32[1]{0:T(128)S(6)} %copy.6.ext_ref, f32[3,2]{1,0:T(4,128)} %copy.5.cmap_ref, f32[3]{0:T(128)} %light_ref.1, f32[4]{0:T(128)} %add_convert_fusion.edge_ref, f32[1024,128]{1,0:T(8,128)} %bitcast.14, f32[2,16,8,128]{3,2,1,0:T(8,128)} %copy-done, f32[2,16,8,128]{3,2,1,0:T(8,128)} %copy-done.1, ...), custom_call_target="tpu_custom_call" | custom-call | tf_op jit(solution)/shard_map/render/pallas_call | solution.py:211
  32.3 31.0 %all_to_all.5 = f32[64,8,128]{2,1,0:T(8,128)} all-to-all(f32[64,8,128]{2,1,0:T(8,128)} %bitcast.16), channel_id=1, replica_groups=mesh['depth'=64,'strip'=8] {'depth'}, dimensions={0} | all-to-all | bytes 524288 | tf_op jit(solution)/shard_map/all_to_all | solution.py:220
  63.3 1.7 %composite.1 = f32[64,16]{1,0:T(8,128)} custom-call(f32[512,128]{1,0:T(8,128)} %bitcast.15), custom_call_target="tpu_custom_call" | custom-call | tf_op jit(solution)/shard_map/composite/pallas_call | solution.py:223
  (1 shorter events, 0.0 us)
Async XLA Ops:
  1.8 5.9 %collective-permute-start = (f32[2,16,8,128]{3,2,1,0:T(8,128)}, f32[2,16,8,128]{3,2,1,0:T(8,128)S(1)}, u32[]{:S(2)}, u32[]{:S(2)}) collective-permute-start(f32[2,16,8,128]{3,2,1,0:T(8,128)} %get-tuple-element.9), channel_id=1, source_target_pairs={{0,8},{8,16},{16,24},{24,32},{32,40},{40,48},{48,56},{56,64},{64,7... | collective-permute-start | bytes 393224 | tf_op jit(solution)/shard_map/ppermute | solution.py:199
  5.0 5.9 %collective-permute-start.1 = (f32[2,16,8,128]{3,2,1,0:T(8,128)}, f32[2,16,8,128]{3,2,1,0:T(8,128)S(1)}, u32[]{:S(2)}, u32[]{:S(2)}) collective-permute-start(f32[2,16,8,128]{3,2,1,0:T(8,128)} %get-tuple-element.10), channel_id=1, source_target_pairs={{8,0},{16,8},{24,16},{32,24},{40,32},{48,40},{56,48},{64,56},{72,6... | collective-permute-start | bytes 393224 | tf_op jit(solution)/shard_map/ppermute | solution.py:200
  6.3 0.7 %copy-start.4 = (f32[3,2]{0,1:T(2,128)S(1)}, f32[3,2]{0,1:T(2,128)}, u32[]{:S(2)}) copy-start(f32[3,2]{0,1:T(2,128)} %param.6) | copy-start | bytes 76
  7.7 3.3 %copy-start = (f32[2,16,8,128]{3,2,1,0:T(8,128)}, f32[2,16,8,128]{3,2,1,0:T(8,128)S(1)}, u32[]{:S(2)}) copy-start(f32[2,16,8,128]{3,2,1,0:T(8,128)S(1)} %collective-permute-done.before_ref) | copy-start | bytes 393220
  10.9 0.6 copy-start.1
  13.4 7.7 %collective-permute-start.2 = (f32[12,2,8,128]{3,2,1,0:T(8,128)}, f32[12,2,8,128]{3,2,1,0:T(8,128)S(1)}, u32[]{:S(2)}, u32[]{:S(2)}) collective-permute-start(f32[12,2,8,128]{3,2,1,0:T(8,128)} %get-tuple-element.11), channel_id=1, source_target_pairs={{0,1},{1,2},{2,3},{3,4},{4,5},{5,6},{6,7},{8,9},{9,10},{10,11},{11... | collective-permute-start | bytes 294920 | tf_op jit(solution)/shard_map/ppermute | solution.py:206
  18.5 6.1 %collective-permute-start.3 = (f32[12,2,8,128]{3,2,1,0:T(8,128)}, f32[12,2,8,128]{3,2,1,0:T(8,128)S(1)}, u32[]{:S(2)}, u32[]{:S(2)}) collective-permute-start(f32[12,2,8,128]{3,2,1,0:T(8,128)} %get-tuple-element.12), channel_id=1, source_target_pairs={{1,0},{2,1},{3,2},{4,3},{5,4},{6,5},{7,6},{9,8},{10,9},{11,10},{12... | collective-permute-start | bytes 294920 | tf_op jit(solution)/shard_map/ppermute | solution.py:207
  21.1 3.6 %copy-start.2 = (f32[12,2,8,128]{3,2,1,0:T(8,128)}, f32[12,2,8,128]{3,2,1,0:T(8,128)S(1)}, u32[]{:S(2)}) copy-start(f32[12,2,8,128]{3,2,1,0:T(8,128)S(1)} %collective-permute-done.2.up_ref) | copy-start | bytes 294916
  24.7 0.6 copy-start.3

commit v2 on v1

--- a/solution.py
+++ b/solution.py
@@ -1,5 +1,3 @@
-import functools
-
 import jax
 import jax.numpy as jnp
 from jax import lax
@@ -16,22 +14,38 @@
     return x_ref[pl.ds(row * 64 + slab, SUB, stride=SLABS), :]
 
 
-def pack_depth(x_ref, low_ref, high_ref):
+def parity(axis):
+    return lax.axis_index(axis) % 2
+
+
+def pack_depth(x_ref, first_ref, second_ref):
+    odd = parity("depth")
+    start = (SLABS - 2) * (1 - odd)
     for row in range(ROWS):
         for k in range(2):
-            low_ref[k, row] = cells(x_ref, row, k)
-            high_ref[k, row] = cells(x_ref, row, SLABS - 2 + k)
-
-
-def pack_strip(x_ref, before_ref, after_ref, low_ref, high_ref):
-    for k in range(2):
-        low_ref[k] = before_ref[k, 0:2]
-        high_ref[k] = before_ref[k, ROWS - 2 : ROWS]
-        low_ref[SLABS + 2 + k] = after_ref[k, 0:2]
-        high_ref[SLABS + 2 + k] = after_ref[k, ROWS - 2 : ROWS]
-        for slab in range(SLABS):
-            low_ref[2 + slab, k] = cells(x_ref, k, slab)
-            high_ref[2 + slab, k] = cells(x_ref, ROWS - 2 + k, slab)
+            first_ref[k, row] = cells(x_ref, row, start + k)
+            second_ref[k, row] = cells(x_ref, row, (SLABS - 2) - start + k)
+
+
+def by_parity(odd, first, second):
+    is_odd = odd == 1
+    return jnp.where(is_odd, first, second), jnp.where(is_odd, second, first)
+
+
+def pack_strip(x_ref, from_first_ref, from_second_ref, first_ref, second_ref):
+    odd = parity("strip")
+    group_odd = parity("depth")
+    start = (ROWS - 2) * (1 - odd)
+    for ref, row in ((first_ref, start), (second_ref, (ROWS - 2) - start)):
+        for k in range(2):
+            for j in range(2):
+                before, after = by_parity(
+                    group_odd, from_first_ref[j, row + k], from_second_ref[j, row + k]
+                )
+                ref[j, k] = before
+                ref[SLABS + 2 + j, k] = after
+            for slab in range(SLABS):
+                ref[2 + slab, k] = cells(x_ref, row + k, slab)
 
 
 def column_neighbours(v):
@@ -55,22 +69,29 @@
     return 2.0 * t + 2.0 * t * (q * s)
 
 
-def render(ext_ref, cmap_ref, light_ref, edge_ref, x_ref, before_ref, after_ref,
-           up_ref, down_ref, out_ref, z_ref, s_ref, ap_ref, am_ref, y_ref, part_ref):
+def render(ext_ref, cmap_ref, light_ref, x_ref, depth_first_ref, depth_second_ref,
+           strip_first_ref, strip_second_ref, out_ref, z_ref, s_ref, ap_ref, am_ref, y_ref,
+           part_ref):
+    odd_strip, odd_group = parity("strip"), parity("depth")
+
     def slab_sums(v):
         e = [v[k] + v[k + 1] for k in range(SLABS + 3)]
         return [e[k] + e[k + 1] for k in range(SLABS + 2)]
 
-    for k, ref in ((0, up_ref), (18, down_ref)):
+    def halo(row, ref):
         for j in range(2):
             z = slab_sums([ref[slab, j] for slab in range(SLABS + 4)])
             for slab in range(SLABS + 2):
-                z_ref[k + j, slab] = z[slab]
+                z_ref[row + j, slab] = z[slab]
+
+    halo((ROWS + 2) * (1 - odd_strip), strip_first_ref)
+    halo((ROWS + 2) * odd_strip, strip_second_ref)
 
     def first(row, _):
-        v = [before_ref[k, row] for k in range(2)]
+        ends = [by_parity(odd_group, depth_first_ref[k, row], depth_second_ref[k, row]) for k in range(2)]
+        v = [before for before, _ in ends]
         v += [cells(x_ref, row, slab) for slab in range(SLABS)]
-        v += [after_ref[k, row] for k in range(2)]
+        v += [after for _, after in ends]
         z = slab_sums(v)
         for slab in range(SLABS + 2):
             z_ref[row + 2, slab] = z[slab]
@@ -78,7 +99,12 @@
 
     lax.fori_loop(0, ROWS, first, 0)
 
-    edge_up, edge_down, edge_before, edge_after = (edge_ref[i] for i in range(4))
+    strip, strips = lax.axis_index("strip"), lax.axis_size("strip")
+    group, groups = lax.axis_index("depth"), lax.axis_size("depth")
+    edge_up = jnp.where(strip == 0, 0.0, 1.0)
+    edge_down = jnp.where(strip == strips - 1, 0.0, 1.0)
+    edge_before = jnp.where(group == 0, 0.0, 1.0)
+    edge_after = jnp.where(group == groups - 1, 0.0, 1.0)
     half_l0 = light_ref[0] * 0.5
     quarter_l1 = light_ref[1] * 0.5 * 0.25 * 0.25
     quarter_l2 = light_ref[2] * 0.5 * 0.25 * 0.25
@@ -180,50 +206,57 @@
 
 
 def f32(*shape):
-    return jax.ShapeDtypeStruct(shape, jnp.float32)
+    return pltpu.VMEM(shape, jnp.float32)
+
+
+def near(*arrays):
+    return [pltpu.with_memory_space_constraint(a, pltpu.VMEM) for a in arrays]
 
 
 def local(volume, extinction, color_map, light_direction):
-    strips, groups = lax.axis_size("strip"), lax.axis_size("depth")
-    x = volume.reshape(ROWS, SLABS, SUB, LANE).transpose(0, 2, 1, 3).reshape(ROWS * 64, LANE)
-
-    def pairs(count):
-        forward = [(i, i + 1) for i in range(count - 1)]
-        return forward, [(b, a) for a, b in forward]
-
-    low, high = pl.pallas_call(
-        pack_depth, in_specs=[VM], out_specs=[VM, VM], name="pack_depth",
-        out_shape=[f32(2, ROWS, SUB, LANE)] * 2,
-    )(x)
-    forward, backward = pairs(groups)
-    before = lax.ppermute(high, "depth", forward)
-    after = lax.ppermute(low, "depth", backward)
-    low, high = pl.pallas_call(
-        pack_strip, in_specs=[VM] * 3, out_specs=[VM, VM], name="pack_strip",
-        out_shape=[f32(SLABS + 4, 2, SUB, LANE)] * 2,
-    )(x, before, after)
-    forward, backward = pairs(strips)
-    up = lax.ppermute(high, "strip", forward)
-    down = lax.ppermute(low, "strip", backward)
-
-    strip, group = lax.axis_index("strip"), lax.axis_index("depth")
-    edges = jnp.stack([strip > 0, strip < strips - 1, group > 0, group < groups - 1])
+    groups = lax.axis_size("depth")
+    (x,) = near(volume.reshape(ROWS, SLABS, SUB, LANE).transpose(0, 2, 1, 3).reshape(ROWS * 64, LANE))
+
+    def swaps(count):
+        out = []
+        for start in range(2):
+            half = [(i, i + 1) for i in range(start, count - 1, 2)]
+            out.append(half + [(b, a) for a, b in half])
+        return out
+
+    def exchange(buffers, axis):
+        return near(*[lax.ppermute(v, axis, p) for v, p in zip(buffers, swaps(lax.axis_size(axis)))])
+
+    near_depth = exchange(
+        pl.pallas_call(
+            pack_depth, in_specs=[VM], out_specs=[VM, VM], name="pack_depth",
+            out_shape=[f32(2, ROWS, SUB, LANE)] * 2,
+        )(x),
+        "depth",
+    )
+    near_strip = exchange(
+        pl.pallas_call(
+            pack_strip, in_specs=[VM] * 3, out_specs=[VM, VM], name="pack_strip",
+            out_shape=[f32(SLABS + 4, 2, SUB, LANE)] * 2,
+        )(x, *near_depth),
+        "strip",
+    )
     blocks = pl.pallas_call(
-        render, in_specs=[SM] * 4 + [VM] * 5, out_specs=VM, name="render",
+        render, in_specs=[SM] * 3 + [VM] * 5, out_specs=VM, name="render",
         out_shape=f32(groups * SUB, LANE),
         scratch_shapes=[
             pltpu.VMEM((ROWS + 4, SLABS + 2, SUB, LANE), jnp.float32),
             *[pltpu.VMEM((ROWS + 2, SLABS, SUB, LANE), jnp.float32)] * 4,
             pltpu.VMEM((4, ROWS, SUB, LANE), jnp.float32),
         ],
-    )(extinction, color_map, light_direction, edges.astype(jnp.float32), x, before, after, up, down)
+    )(extinction, color_map, light_direction, x, *near_depth, *near_strip)
     layers = lax.all_to_all(
         blocks.reshape(groups, SUB, LANE), "depth", split_axis=0, concat_axis=0, tiled=True
     )
     image = pl.pallas_call(
         composite, in_specs=[VM], out_specs=VM, name="composite",
-        out_shape=f32(64, 16), scratch_shapes=[pltpu.VMEM((64, LANE), jnp.float32)],
-    )(layers.reshape(groups * SUB, LANE))
+        out_shape=jax.ShapeDtypeStruct((64, 16), jnp.float32), scratch_shapes=[pltpu.VMEM((64, LANE), jnp.float32)],
+    )(*near(layers.reshape(groups * SUB, LANE)))
     return image.reshape(4, 16, 16)
 
 

time: 65.4 us -> 58.4 us (0.89)
  the two profiles are of different devices: /device:TPU:3 before, /device:TPU:4 now
where the time goes in v2:
time: 58.4 us; the launch traced here: 58.1 us
  blocking collectives  35.4 us (61%)
  starting transfers between devices  8.62 us (15%)
  Pallas kernels  6.64 us (11%)
  waiting for transfers between devices  5.02 us (9%)
  local copies, waits for them, and re-layouts  1.71 us (3%)
  between operations  0.71 us (1%)
    all_to_all x1, blocking collectives, local(): lax.all_to_all(blocks.reshape(groups, SUB, LANE), 'depth', split_axis=0,...  35.4 us
    ppermute x4, starting transfers between devices, exchange(): lax.ppermute(v, axis, p)  8.62 us
    pallas_call x1, Pallas kernels, local(): pl.pallas_call(render, in_specs=[SM] * 3 + [VM] * 5, out_specs=VM, name='...  5.78 us
    ppermute x4, waiting for transfers between devices, exchange(): lax.ppermute(v, axis, p)  5.02 us
    unnamed x5, local copies, waits for them, and re-layouts  1.71 us
  transfers between devices with their start and end apart: 4, of which 2 were waited for; matrix products, arithmetic and copies ran while one was open for 1% of the time, Pallas kernels for 0%

profile of v2, /device:TPU:4, one launch (start us, length us, event | category | flops | bytes accessed | tf_op | source)
XLA Modules:
  0.0 58.1 jit_solution(11691147530980634104)
XLA Ops:
  0.0 0.0 copy-start
  0.0 1.0 %copy-done = f32[16,8,1024]{2,1,0:T(8,128)S(1)} copy-done((f32[16,8,1024]{2,1,0:T(8,128)S(1)}, f32[16,8,1024]{2,1,0:T(8,128)}, u32[]{:S(2)}) %copy-start) | copy-done | bytes 524312
  1.0 0.1 pack_depth.1
  1.1 3.5 %collective-permute-start = (f32[2,16,8,128]{3,2,1,0:T(8,128)S(1)}, f32[2,16,8,128]{3,2,1,0:T(8,128)S(1)}, u32[]{:S(2)}, u32[]{:S(2)}) collective-permute-start(f32[2,16,8,128]{3,2,1,0:T(8,128)S(1)} %get-tuple-element.9), channel_id=1, source_target_pairs={{0,8},{16,24},{32,40},{48,56},{64,72},{80,88},{96,104},{112,120},{... | collective-permute-start | bytes 393224 | tf_op jit(solution)/shard_map/ppermute | solution.py:228
  4.6 0.7 %collective-permute-start.1 = (f32[2,16,8,128]{3,2,1,0:T(8,128)S(1)}, f32[2,16,8,128]{3,2,1,0:T(8,128)S(1)}, u32[]{:S(2)}, u32[]{:S(2)}) collective-permute-start(f32[2,16,8,128]{3,2,1,0:T(8,128)S(1)} %get-tuple-element.10), channel_id=1, source_target_pairs={{8,16},{24,32},{40,48},{56,64},{72,80},{88,96},{104,112},{120,128}... | collective-permute-start | bytes 393224 | tf_op jit(solution)/shard_map/ppermute | solution.py:228
  5.3 3.0 %collective-permute-done.from_first_ref.depth_first_ref = f32[2,16,8,128]{3,2,1,0:T(8,128)S(1)} collective-permute-done((f32[2,16,8,128]{3,2,1,0:T(8,128)S(1)}, f32[2,16,8,128]{3,2,1,0:T(8,128)S(1)}, u32[]{:S(2)}, u32[]{:S(2)}) %collective-permute-start) | collective-permute-done | bytes 131104 | tf_op jit(solution)/shard_map/ppermute | solution.py:228
  8.2 0.0 collective-permute-done.1.from_second_ref.depth_second_ref
  8.3 1.9 %collective-permute-start.2 = (f32[12,2,8,128]{3,2,1,0:T(8,128)S(1)}, f32[12,2,8,128]{3,2,1,0:T(8,128)S(1)}, u32[]{:S(2)}, u32[]{:S(2)}) collective-permute-start(f32[12,2,8,128]{3,2,1,0:T(8,128)S(1)} %get-tuple-element.11), channel_id=1, source_target_pairs={{0,1},{2,3},{4,5},{6,7},{1,0},{3,2},{5,4},{7,6},{8,9},{10,11},{12,... | collective-permute-start | bytes 294920 | tf_op jit(solution)/shard_map/ppermute | solution.py:228
  10.2 0.0 copy-start.1
  10.2 2.5 %collective-permute-start.3 = (f32[12,2,8,128]{3,2,1,0:T(8,128)S(1)}, f32[12,2,8,128]{3,2,1,0:T(8,128)S(1)}, u32[]{:S(2)}, u32[]{:S(2)}) collective-permute-start(f32[12,2,8,128]{3,2,1,0:T(8,128)S(1)} %get-tuple-element.12), channel_id=1, source_target_pairs={{1,2},{3,4},{5,6},{2,1},{4,3},{6,5},{9,10},{11,12},{13,14},{10,9},... | collective-permute-start | bytes 294920 | tf_op jit(solution)/shard_map/ppermute | solution.py:228
  13.4 0.0 copy-done.1
  13.4 0.7 %copy.5.cmap_ref = f32[3,2]{1,0:T(4,128)} copy(f32[3,2]{0,1:T(2,128)S(1)} %copy-done.1) | data formatting | bytes 48 | tf_op args[2]
  14.1 0.0 collective-permute-done.2.strip_first_ref
  14.1 2.1 %collective-permute-done.3.strip_second_ref = f32[12,2,8,128]{3,2,1,0:T(8,128)S(1)} collective-permute-done((f32[12,2,8,128]{3,2,1,0:T(8,128)S(1)}, f32[12,2,8,128]{3,2,1,0:T(8,128)S(1)}, u32[]{:S(2)}, u32[]{:S(2)}) %collective-permute-start.3) | collective-permute-done | bytes 98336 | tf_op jit(solution)/shard_map/ppermute | solution.py:228
  16.1 5.8 %render.1 = f32[512,128]{1,0:T(8,128)S(1)} custom-call(f32[1]{0:T(128)S(6)} %copy.6.ext_ref, f32[3,2]{1,0:T(4,128)} %copy.5.cmap_ref, f32[3]{0:T(128)} %light_ref.1, f32[1024,128]{1,0:T(8,128)S(1)} %bitcast.10, f32[2,16,8,128]{3,2,1,0:T(8,128)S(1)} %collective-permute-done.from_first_ref.depth_first_ref, ...), custom_call_target="tpu_custom_call" | custom-call | tf_op jit(solution)/shard_map/render/pallas_call | solution.py:244
  21.9 35.4 %all_to_all.5 = f32[64,8,128]{2,1,0:T(8,128)S(1)} all-to-all(f32[64,8,128]{2,1,0:T(8,128)S(1)} %bitcast.12), channel_id=1, replica_groups=mesh['depth'=64,'strip'=8] {'depth'}, dimensions={0} | all-to-all | bytes 524288 | tf_op jit(solution)/shard_map/all_to_all | solution.py:253
  57.4 0.8 %composite.1 = f32[64,16]{1,0:T(8,128)} custom-call(f32[512,128]{1,0:T(8,128)S(1)} %bitcast.11), custom_call_target="tpu_custom_call" | custom-call | tf_op jit(solution)/shard_map/composite/pallas_call | solution.py:256
  (1 shorter events, 0.0 us)
Async XLA Ops:
  0.0 1.0 %copy-start = (f32[16,8,1024]{2,1,0:T(8,128)S(1)}, f32[16,8,1024]{2,1,0:T(8,128)}, u32[]{:S(2)}) copy-start(f32[16,8,1024]{2,1,0:T(8,128)} %param.4) | copy-start | bytes 1572868
  1.1 7.1 %collective-permute-start = (f32[2,16,8,128]{3,2,1,0:T(8,128)S(1)}, f32[2,16,8,128]{3,2,1,0:T(8,128)S(1)}, u32[]{:S(2)}, u32[]{:S(2)}) collective-permute-start(f32[2,16,8,128]{3,2,1,0:T(8,128)S(1)} %get-tuple-element.9), channel_id=1, source_target_pairs={{0,8},{16,24},{32,40},{48,56},{64,72},{80,88},{96,104},{112,120},{... | collective-permute-start | bytes 393224 | tf_op jit(solution)/shard_map/ppermute | solution.py:228
  4.6 3.6 %collective-permute-start.1 = (f32[2,16,8,128]{3,2,1,0:T(8,128)S(1)}, f32[2,16,8,128]{3,2,1,0:T(8,128)S(1)}, u32[]{:S(2)}, u32[]{:S(2)}) collective-permute-start(f32[2,16,8,128]{3,2,1,0:T(8,128)S(1)} %get-tuple-element.10), channel_id=1, source_target_pairs={{8,16},{24,32},{40,48},{56,64},{72,80},{88,96},{104,112},{120,128}... | collective-permute-start | bytes 393224 | tf_op jit(solution)/shard_map/ppermute | solution.py:228
  8.3 5.8 %collective-permute-start.2 = (f32[12,2,8,128]{3,2,1,0:T(8,128)S(1)}, f32[12,2,8,128]{3,2,1,0:T(8,128)S(1)}, u32[]{:S(2)}, u32[]{:S(2)}) collective-permute-start(f32[12,2,8,128]{3,2,1,0:T(8,128)S(1)} %get-tuple-element.11), channel_id=1, source_target_pairs={{0,1},{2,3},{4,5},{6,7},{1,0},{3,2},{5,4},{7,6},{8,9},{10,11},{12,... | collective-permute-start | bytes 294920 | tf_op jit(solution)/shard_map/ppermute | solution.py:228
  10.2 3.2 %copy-start.1 = (f32[3,2]{0,1:T(2,128)S(1)}, f32[3,2]{0,1:T(2,128)}, u32[]{:S(2)}) copy-start(f32[3,2]{0,1:T(2,128)} %param.6) | copy-start | bytes 76
  10.2 5.9 %collective-permute-start.3 = (f32[12,2,8,128]{3,2,1,0:T(8,128)S(1)}, f32[12,2,8,128]{3,2,1,0:T(8,128)S(1)}, u32[]{:S(2)}, u32[]{:S(2)}) collective-permute-start(f32[12,2,8,128]{3,2,1,0:T(8,128)S(1)} %get-tuple-element.12), channel_id=1, source_target_pairs={{1,2},{3,4},{5,6},{2,1},{4,3},{6,5},{9,10},{11,12},{13,14},{10,9},... | collective-permute-start | bytes 294920 | tf_op jit(solution)/shard_map/ppermute | solution.py:228

commit v3 on v2

v3 whole, which is shorter than its diff:
```python
import jax
import jax.numpy as jnp
from jax import lax
from jax.experimental import pallas as pl
from jax.experimental.pallas import tpu as pltpu
from jax.sharding import PartitionSpec as P

ROWS, SLABS, SUB, LANE = 16, 8, 8, 128
VM = pl.BlockSpec(memory_space=pltpu.VMEM)
SM = pl.BlockSpec(memory_space=pltpu.SMEM)


SMALL = pltpu.CompilerParams(vmem_limit_bytes=4 << 20)


def cells(x_ref, row, slab):
    return x_ref[pl.ds(row * 64 + slab, SUB, stride=SLABS), :]


def parity(axis):
    return lax.axis_index(axis) % 2


def pack_depth(x_ref, first_ref, second_ref):
    odd = parity("depth")
    start = (SLABS - 2) * (1 - odd)
    for row in range(ROWS):
        for k in range(2):
            first_ref[k, row] = cells(x_ref, row, start + k)
            second_ref[k, row] = cells(x_ref, row, (SLABS - 2) - start + k)


def by_parity(odd, first, second):
    is_odd = odd == 1
    return jnp.where(is_odd, first, second), jnp.where(is_odd, second, first)


def pack_strip(x_ref, from_first_ref, from_second_ref, _, first_ref, second_ref):
    odd = parity("strip")
    group_odd = parity("depth")
    start = (ROWS - 2) * (1 - odd)
    for ref, row in ((first_ref, start), (second_ref, (ROWS - 2) - start)):
        for k in range(2):
            for j in range(2):
                before, after = by_parity(
                    group_odd, from_first_ref[j, row + k], from_second_ref[j, row + k]
                )
                ref[j, k] = before
                ref[SLABS + 2 + j, k] = after
            for slab in range(SLABS):
                ref[2 + slab, k] = cells(x_ref, row + k, slab)


def column_neighbours(v):
    lane = lax.broadcasted_iota(jnp.int32, (SUB, LANE), 1)
    sub = lax.broadcasted_iota(jnp.int32, (SUB, LANE), 0)
    a = pltpu.roll(v, 1, 1)
    b = pltpu.roll(a, 1, 0)
    prev = jnp.where(lane == 0, jnp.where(sub == 0, 0.0, b), a)
    a = pltpu.roll(v, LANE - 1, 1)
    b = pltpu.roll(a, SUB - 1, 0)
    following = jnp.where(lane == LANE - 1, jnp.where(sub == SUB - 1, 0.0, b), a)
    return prev, following


def log1p_unit(e):
    t = e / (2.0 + e)
    q = t * t
    s = 1.0 / 13.0
    for d in (11.0, 9.0, 7.0, 5.0, 3.0):
        s = s * q + 1.0 / d
    return 2.0 * t + 2.0 * t * (q * s)


def smoothed(lower, middle, upper, factor):
    m = (lower + middle) + (middle + upper)
    prev, following = column_neighbours(m)
    return ((prev + following) + (m + m)) * factor


def column_parts(s):
    prev, following = column_neighbours(s)
    return (prev + following) + (s + s), following - prev


def gradient_parts(u, w, light):
    p = (u[0] + u[1]) + (u[1] + u[2])
    q = u[2] - u[0]
    t = (w[0] + w[1]) + (w[1] + w[2])
    scale = 0.5 * 0.25 * 0.25
    y = (light[1] * scale) * q + (light[2] * scale) * t
    p = (light[0] * scale) * p
    return y + p, y - p, y + y


def shade(s, facing, ext, slopes, offsets):
    shading = 1.0 - 0.7 / (1.0 + facing * facing)
    z = s + s
    soft = jnp.maximum(z, 0.0) + log1p_unit(jnp.exp(-jnp.abs(z)))
    clear = jnp.exp(-ext * soft)
    weight = (1.0 - clear) * shading
    return [weight * (0.5 * jnp.tanh(a * s + b) + 0.5) for a, b in zip(slopes, offsets)] + [clear]


def over(front, back):
    if front is None:
        return back
    through = front[3]
    return [f + through * c for f, c in zip(front[:3], back[:3])] + [through * back[3]]


def coefficients(ext_ref, cmap_ref, light_ref):
    light = [light_ref[i] for i in range(3)]
    slopes = [cmap_ref[c, 0] * 0.5 for c in range(3)]
    offsets = [cmap_ref[c, 1] * 0.5 for c in range(3)]
    return light, (ext_ref[0], slopes, offsets)


def ends_inside(axis):
    index, count = lax.axis_index(axis), lax.axis_size(axis)
    return jnp.where(index == 0, 0.0, 1.0), jnp.where(index == count - 1, 0.0, 1.0)


def binomial(v):
    e = [a + b for a, b in zip(v, v[1:])]
    return [a + b for a, b in zip(e, e[1:])]


def render_inner(ext_ref, cmap_ref, light_ref, x_ref, _, z_ref, u_ref, w_ref, ap_ref, am_ref, y_ref,
                 s_ref, mid_ref):
    light, color = coefficients(ext_ref, cmap_ref, light_ref)

    def first(row, _):
        z = binomial([cells(x_ref, row, slab) for slab in range(SLABS)])
        for i, v in enumerate(z):
            z_ref[row, i] = v
        return 0

    lax.fori_loop(0, ROWS, first, 0)

    def second(row, _):
        s = [
            smoothed(z_ref[row - 1, i], z_ref[row, i], z_ref[row + 1, i], 1.0 / 64.0)
            for i in range(6)
        ]
        u, w = zip(*[column_parts(v) for v in s])
        for i, k in enumerate((0, 1, 4, 5)):
            u_ref[row, i] = u[k]
            w_ref[row, i] = w[k]
        for i in range(4):
            ap, am, y = gradient_parts(u[i : i + 3], w[i : i + 3], light)
            ap_ref[row, i] = ap
            am_ref[row, i] = am
            y_ref[row, i] = y
        for i in range(6):
            s_ref[row, i] = s[i]
        return 0

    lax.fori_loop(1, ROWS - 1, second, 0)

    def third(row, _):
        total = None
        for i in range(4):
            facing = (ap_ref[row + 1, i] + am_ref[row - 1, i]) + y_ref[row, i]
            total = over(total, shade(s_ref[row, i + 1], facing, *color))
        for c in range(4):
            mid_ref[c, row] = total[c]
        return 0

    lax.fori_loop(2, ROWS - 2, third, 0)


def render_outer(ext_ref, cmap_ref, light_ref, x_ref, depth_first_ref, depth_second_ref, ui_ref,
                 wi_ref, si_ref, mid_ref, z_ref, ap_ref, am_ref, y_ref, s_ref, part_ref):
    light, color = coefficients(ext_ref, cmap_ref, light_ref)
    odd_group = parity("depth")
    edge_before, edge_after = ends_inside("depth")

    def first(row, _):
        ends = [
            by_parity(odd_group, depth_first_ref[k, row], depth_second_ref[k, row])
            for k in range(2)
        ]
        z = binomial([ends[0][0], ends[1][0], cells(x_ref, row, 0), cells(x_ref, row, 1)])
        z += binomial([cells(x_ref, row, 6), cells(x_ref, row, 7), ends[0][1], ends[1][1]])
        for i, v in enumerate(z):
            z_ref[row, i] = v
        return 0

    lax.fori_loop(0, ROWS, first, 0)

    def second(row, _):
        edges = (edge_before, None, None, edge_after)
        s = []
        for i, edge in enumerate(edges):
            factor = 1.0 / 64.0 if edge is None else edge * (1.0 / 64.0)
            s.append(smoothed(z_ref[row - 1, i], z_ref[row, i], z_ref[row + 1, i], factor))
        u, w = zip(*[column_parts(v) for v in s])
        ui = [ui_ref[row, i] for i in range(4)]
        wi = [wi_ref[row, i] for i in range(4)]
        u = [u[0], u[1], ui[0], ui[1]], [ui[2], ui[3], u[2], u[3]]
        w = [w[0], w[1], wi[0], wi[1]], [wi[2], wi[3], w[2], w[3]]
        for side in range(2):
            for j in range(2):
                i = 2 * side + j
                ap, am, y = gradient_parts(u[side][j : j + 3], w[side][j : j + 3], light)
                ap_ref[row, i] = ap
                am_ref[row, i] = am
                y_ref[row, i] = y
        s_ref[row, 0] = s[1]
        s_ref[row, 1] = s[2]
        return 0

    lax.fori_loop(1, ROWS - 1, second, 0)

    def third(row, _):
        smooth = [s_ref[row, 0], si_ref[row, 0], si_ref[row, 5], s_ref[row, 1]]
        total = None
        for i in range(4):
            if i == 2:
                total = over(total, [mid_ref[c, row] for c in range(4)])
            facing = (ap_ref[row + 1, i] + am_ref[row - 1, i]) + y_ref[row, i]
            total = over(total, shade(smooth[i], facing, *color))
        for c in range(4):
            part_ref[c, row] = total[c]
        return 0

    lax.fori_loop(2, ROWS - 2, third, 0)


def render_rows(ext_ref, cmap_ref, light_ref, strip_first_ref, strip_second_ref, zi_ref, api_ref,
                ami_ref, yi_ref, si_ref, zo_ref, apo_ref, amo_ref, yo_ref, so_ref, part_ref,
                out_ref, halo_ref, here_ref, s_ref, all_ref):
    light, color = coefficients(ext_ref, cmap_ref, light_ref)
    odd_strip = parity("strip")
    edge_before, edge_after = ends_inside("depth")
    edge_up, edge_down = ends_inside("strip")

    for base, ref in ((2 * (1 - odd_strip), strip_first_ref), (2 * odd_strip, strip_second_ref)):
        for j in range(2):
            for i, v in enumerate(binomial([ref[slab, j] for slab in range(SLABS + 4)])):
                halo_ref[base + j, i] = v

    def sums(row, slab):
        if row < 0:
            return halo_ref[row + 2, slab + 1]
        if row >= ROWS:
            return halo_ref[row - ROWS + 2, slab + 1]
        if 1 <= slab <= 6:
            return zi_ref[row, slab - 1]
        return zo_ref[row, slab + 1 if slab < 1 else slab - 5]

    def kept(inner_ref, outer_ref, row, slab):
        if 2 <= slab <= 5:
            return inner_ref[row, slab - 2]
        return outer_ref[row, slab if slab < 2 else slab - 4]

    def kept_smooth(row, slab):
        return si_ref[row, slab - 1] if 1 <= slab <= 6 else so_ref[row, slab // 7]

    for n, row in enumerate((-1, 0, ROWS - 1, ROWS)):
        outside = {-1: edge_up, ROWS: edge_down}.get(row)
        u, w = [], []
        for slab in range(-1, SLABS + 1):
            factor = 1.0 / 64.0
            for edge in (outside, {-1: edge_before, SLABS: edge_after}.get(slab)):
                factor = factor if edge is None else factor * edge
            v = smoothed(sums(row - 1, slab), sums(row, slab), sums(row + 1, slab), factor)
            if 0 <= slab < SLABS and 0 <= row < ROWS:
                s_ref[n - 1, slab] = v
            a, b = column_parts(v)
            u.append(a)
            w.append(b)
        for slab in range(SLABS):
            for i, v in enumerate(gradient_parts(u[slab : slab + 3], w[slab : slab + 3], light)):
                here_ref[n, i, slab] = v

    for row in (0, 1, ROWS - 2, ROWS - 1):
        total = None
        for slab in range(SLABS):
            if row == 0:
                facing = kept(api_ref, apo_ref, 1, slab) + here_ref[0, 1, slab] + here_ref[1, 2, slab]
            elif row == 1:
                facing = kept(api_ref, apo_ref, 2, slab) + here_ref[1, 1, slab] + kept(yi_ref, yo_ref, 1, slab)
            elif row == ROWS - 2:
                facing = here_ref[2, 0, slab] + kept(ami_ref, amo_ref, row - 1, slab) + kept(yi_ref, yo_ref, row, slab)
            else:
                facing = here_ref[3, 0, slab] + kept(ami_ref, amo_ref, row - 1, slab) + here_ref[2, 2, slab]
            s = s_ref[row // 8, slab] if row in (0, ROWS - 1) else kept_smooth(row, slab)
            total = over(total, shade(s, facing, *color))
        for c in range(4):
            all_ref[(c * ROWS + row) * SUB : (c * ROWS + row + 1) * SUB, :] = total[c]
    for c in range(4):
        for row in range(2, ROWS - 2):
            all_ref[(c * ROWS + row) * SUB : (c * ROWS + row + 1) * SUB, :] = part_ref[c, row]

    chunk = lax.broadcasted_iota(jnp.int32, (SUB, LANE), 1) // 16
    for tile in range(SUB):
        v = [all_ref[pl.ds(g * 64 + tile, SUB, stride=SUB), :] for g in range(8)]
        for bit in (4, 2, 1):
            upper = (chunk & bit) != 0
            for i in range(8):
                if i & bit == 0:
                    lo, hi = v[i], v[i + bit]
                    v[i] = jnp.where(upper, pltpu.roll(hi, 16 * bit, 1), lo)
                    v[i + bit] = jnp.where(upper, hi, pltpu.roll(lo, LANE - 16 * bit, 1))
        for m in range(8):
            row = (tile * 8 + m) * SUB
            out_ref[row : row + SUB, :] = v[m]


def composite(parts_ref, out_ref):
    is_clear = lax.broadcasted_iota(jnp.int32, (SUB, LANE), 1) >= 96
    through = jnp.ones((SUB, LANE), jnp.float32)
    total = jnp.zeros((SUB, LANE), jnp.float32)
    for d in range(parts_ref.shape[0] // SUB):
        x = parts_ref[d * SUB : (d + 1) * SUB, :]
        total = total + through * x
        m = jnp.where(is_clear, x, 1.0)
        m = m * pltpu.roll(m, 32, 1)
        m = m * pltpu.roll(m, 64, 1)
        through = through * m
    result = jnp.where(is_clear, 1.0 - through, total)
    for i in range(8):
        moved = result if i == 0 else pltpu.roll(result, LANE - 16 * i, 1)
        out_ref[i * SUB : (i + 1) * SUB, :] = moved[:, 0:16]


def f32(*shape):
    return pltpu.VMEM(shape, jnp.float32)


def near(*arrays):
    return [pltpu.with_memory_space_constraint(a, pltpu.VMEM) for a in arrays]


def local(volume, extinction, color_map, light_direction):
    groups = lax.axis_size("depth")
    x = volume.reshape(ROWS, SLABS, SUB, LANE).transpose(0, 2, 1, 3).reshape(ROWS * 64, LANE)

    def swaps(count):
        out = []
        for start in range(2):
            half = [(i, i + 1) for i in range(start, count - 1, 2)]
            out.append(half + [(b, a) for a, b in half])
        return out

    def exchange(buffers, axis):
        return [lax.ppermute(v, axis, p) for v, p in zip(buffers, swaps(lax.axis_size(axis)))]

    packed = pl.pallas_call(
        pack_depth, in_specs=[VM], compiler_params=SMALL, out_specs=[VM, VM], name="pack_depth",
        out_shape=[f32(2, ROWS, SUB, LANE)] * 2,
    )(*near(x))
    near_depth = exchange(packed, "depth")

    params = (extinction, color_map, light_direction)

    def kernel(body, operands, shapes, scratch=()):
        return pl.pallas_call(
            body, in_specs=[SM] * 3 + [VM] * len(operands), out_specs=[VM] * len(shapes),
            name=body.__name__, compiler_params=SMALL, out_shape=[f32(*shape) for shape in shapes],
            scratch_shapes=[f32(*shape) for shape in scratch],
        )(*params, *near(*operands))

    four = (ROWS, 4, SUB, LANE)
    zi, ui, wi, api, ami, yi, si, mid = kernel(
        render_inner, (x, packed[0]),
        [(ROWS, 6, SUB, LANE)] + [four] * 5 + [(ROWS, 6, SUB, LANE), (4, ROWS, SUB, LANE)],
    )
    near_strip = exchange(
        pl.pallas_call(
            pack_strip, in_specs=[VM] * 4, compiler_params=SMALL, out_specs=[VM, VM], name="pack_strip",
            out_shape=[f32(SLABS + 4, 2, SUB, LANE)] * 2,
        )(*near(x, *near_depth, mid)),
        "strip",
    )
    zo, apo, amo, yo, so, part = kernel(
        render_outer, (x, *near_depth, ui, wi, si, mid),
        [four] * 4 + [(ROWS, 2, SUB, LANE), (4, ROWS, SUB, LANE)],
    )
    (blocks,) = kernel(
        render_rows, (*near_strip, zi, api, ami, yi, si, zo, apo, amo, yo, so, part),
        [(groups * SUB, LANE)],
        [(4, SLABS + 2, SUB, LANE), (4, 3, SLABS, SUB, LANE), (2, SLABS, SUB, LANE),
         (4 * ROWS * SUB, LANE)],
    )
    layers = lax.all_to_all(
        blocks.reshape(groups, SUB, LANE), "depth", split_axis=0, concat_axis=0, tiled=True
    )
    image = pl.pallas_call(
        composite, in_specs=[VM], compiler_params=SMALL, out_specs=VM, name="composite",
        out_shape=jax.ShapeDtypeStruct((64, 16), jnp.float32),
    )(*near(layers.reshape(groups * SUB, LANE)))
    return image.reshape(4, 16, 16)


def solution(mesh):
    in_specs = (P("strip", "depth", None), P(), P(), P())
    out_specs = P(None, "strip", "depth")
    return jax.shard_map(local, mesh=mesh, in_specs=in_specs, out_specs=out_specs, check_vma=False)
```

time: 58.4 us -> 56.1 us (0.961)
  waiting for transfers between devices: 5.02 us -> 0.01 us
  Pallas kernels: 6.64 us -> 11.1 us
  blocking collectives: 35.4 us -> 34 us
    ppermute x4, waiting for transfers between devices: 5.02 us -> 0.01 us  [exchange(): lax.ppermute(v, axis, p)]
    pallas_call x4 -> x6, Pallas kernels: 6.64 us -> 11.1 us  [the longest x3 10.1 us: kernel(): pl.pallas_call(body, in_specs=[SM] * 3 + [VM] * len(operands), out_specs=...]
    all_to_all x1, blocking collectives: 35.4 us -> 34 us  [local(): lax.all_to_all(blocks.reshape(groups, SUB, LANE), 'depth', split_axis=0,...]
    unnamed x5 -> x9, local copies, waits for them, and re-layouts: 1.71 us -> 1.15 us
  transfers between devices with their start and end apart: 4 -> 4, of which waited for: 2 -> 0; matrix products, arithmetic and copies ran while one was open for 1% -> 0% of each run, Pallas kernels for 0% -> 14%
where the time goes in v3:
time: 56.1 us; the launch traced here: 55.8 us
  blocking collectives  34 us (61%)
  Pallas kernels  11.1 us (20%)
  starting transfers between devices  8.75 us (16%)
  local copies, waits for them, and re-layouts  1.15 us (2%)
  between operations  0.79 us (1%)
    all_to_all x1, blocking collectives, local(): lax.all_to_all(blocks.reshape(groups, SUB, LANE), 'depth', split_axis=0,...  34 us
    pallas_call x3, Pallas kernels, kernel(): pl.pallas_call(body, in_specs=[SM] * 3 + [VM] * len(operands), out_specs=...  10.1 us
    ppermute x4, starting transfers between devices, exchange(): lax.ppermute(v, axis, p)  8.75 us
    unnamed x9, local copies, waits for them, and re-layouts  1.15 us
  transfers between devices with their start and end apart: 4, of which 0 were waited for; matrix products, arithmetic and copies ran while one was open for 0% of the time, Pallas kernels for 14%

profile of v3, /device:TPU:4, one launch (start us, length us, event | category | flops | bytes accessed | tf_op | source)
XLA Modules:
  0.0 55.8 jit_solution(6703147978604897031)
XLA Ops:
  0.0 0.0 copy-start
  0.0 1.0 %copy-done = f32[16,8,1024]{2,1,0:T(8,128)S(1)} copy-done((f32[16,8,1024]{2,1,0:T(8,128)S(1)}, f32[16,8,1024]{2,1,0:T(8,128)}, u32[]{:S(2)}) %copy-start) | copy-done | bytes 524312
  1.0 0.0 copy-start.1
  1.0 0.1 pack_depth.1
  1.1 0.0 copy-start.3
  1.1 3.6 %collective-permute-start = (f32[2,16,8,128]{3,2,1,0:T(8,128)S(1)}, f32[2,16,8,128]{3,2,1,0:T(8,128)S(1)}, u32[]{:S(2)}, u32[]{:S(2)}) collective-permute-start(f32[2,16,8,128]{3,2,1,0:T(8,128)S(1)} %get-tuple-element.23._), channel_id=1, source_target_pairs={{0,8},{16,24},{32,40},{48,56},{64,72},{80,88},{96,104},{112,120},{... | collective-permute-start | bytes 393224 | tf_op jit(solution)/shard_map/ppermute | solution.py:349
  4.7 0.7 %collective-permute-start.1 = (f32[2,16,8,128]{3,2,1,0:T(8,128)S(1)}, f32[2,16,8,128]{3,2,1,0:T(8,128)S(1)}, u32[]{:S(2)}, u32[]{:S(2)}) collective-permute-start(f32[2,16,8,128]{3,2,1,0:T(8,128)S(1)} %get-tuple-element.24), channel_id=1, source_target_pairs={{8,16},{24,32},{40,48},{56,64},{72,80},{88,96},{104,112},{120,128}... | collective-permute-start | bytes 393224 | tf_op jit(solution)/shard_map/ppermute | solution.py:349
  5.4 0.0 copy-done.3
  5.4 0.1 copy.7.cmap_ref
  5.5 0.0 copy-start.2
  6.2 0.0 copy-done.1
  6.2 0.0 copy-done.2
  6.2 3.8 %render_inner.1 = (f32[16,6,8,128]{3,2,1,0:T(8,128)S(1)}, f32[16,4,8,128]{3,2,1,0:T(8,128)S(1)}, f32[16,4,8,128]{3,2,1,0:T(8,128)S(1)}, f32[16,4,8,128]{3,2,1,0:...) custom-call(f32[1]{0:T(128)S(6)} %copy.8.ext_ref, ...), custom_call_target="tpu_custom_call" | custom-call | tf_op jit(solution)/shard_map/render_inner/pallas_call | solution.py:360
  10.0 0.0 collective-permute-done.from_first_ref.depth_first_ref
  10.0 0.0 collective-permute-done.1.from_second_ref.depth_second_ref
  10.1 1.9 %collective-permute-start.2 = (f32[12,2,8,128]{3,2,1,0:T(8,128)S(1)}, f32[12,2,8,128]{3,2,1,0:T(8,128)S(1)}, u32[]{:S(2)}, u32[]{:S(2)}) collective-permute-start(f32[12,2,8,128]{3,2,1,0:T(8,128)S(1)} %get-tuple-element.26), channel_id=1, source_target_pairs={{0,1},{2,3},{4,5},{6,7},{1,0},{3,2},{5,4},{7,6},{8,9},{10,11},{12,... | collective-permute-start | bytes 294920 | tf_op jit(solution)/shard_map/ppermute | solution.py:349
  12.0 2.5 %collective-permute-start.3 = (f32[12,2,8,128]{3,2,1,0:T(8,128)S(1)}, f32[12,2,8,128]{3,2,1,0:T(8,128)S(1)}, u32[]{:S(2)}, u32[]{:S(2)}) collective-permute-start(f32[12,2,8,128]{3,2,1,0:T(8,128)S(1)} %get-tuple-element.27), channel_id=1, source_target_pairs={{1,2},{3,4},{5,6},{2,1},{4,3},{6,5},{9,10},{11,12},{13,14},{10,9},... | collective-permute-start | bytes 294920 | tf_op jit(solution)/shard_map/ppermute | solution.py:349
  14.5 3.8 %render_outer.1 = (f32[16,4,8,128]{3,2,1,0:T(8,128)S(1)}, f32[16,4,8,128]{3,2,1,0:T(8,128)S(1)}, f32[16,4,8,128]{3,2,1,0:T(8,128)S(1)}, f32[16,4,8,128]{3,2,1,0:...) custom-call(f32[1]{0:T(128)S(6)} %copy.8.ext_ref, f32[3,2]{1,0:T(4,128)S(1)} %copy.7.cmap_ref, ...), custom_call_target="tpu_custom_call" | custom-call | tf_op jit(solution)/shard_map/render_outer/pallas_call | solution.py:360
  18.3 0.0 collective-permute-done.2.strip_first_ref
  18.3 0.0 collective-permute-done.3.strip_second_ref
  18.3 2.5 %render_rows.1 = f32[512,128]{1,0:T(8,128)S(1)} custom-call(f32[1]{0:T(128)S(6)} %copy.8.ext_ref, f32[3,2]{1,0:T(4,128)S(1)} %copy.7.cmap_ref, f32[3]{0:T(128)S(1)} %copy-done.2, f32[12,2,8,128]{3,2,1,0:T(8,128)S(1)} %collective-permute-done.2.strip_first_ref, f32[12,2,8,128]{3,2,1,0:T(8,128)S(1)} %collective-permute-done.3.strip_second_ref, ...), custom_call_target="tpu_custom_call" | custom-call | tf_op jit(solution)/shard_map/render_rows/pallas_call | solution.py:360
  20.9 34.0 %all_to_all.5 = f32[64,8,128]{2,1,0:T(8,128)S(1)} all-to-all(f32[64,8,128]{2,1,0:T(8,128)S(1)} %bitcast.13), channel_id=1, replica_groups=mesh['depth'=64,'strip'=8] {'depth'}, dimensions={0} | all-to-all | bytes 524288 | tf_op jit(solution)/shard_map/all_to_all | solution.py:388
  54.9 0.9 %composite.1 = f32[64,16]{1,0:T(8,128)} custom-call(f32[512,128]{1,0:T(8,128)S(1)} %bitcast.12), custom_call_target="tpu_custom_call" | custom-call | tf_op jit(solution)/shard_map/composite/pallas_call | solution.py:391
  (1 shorter events, 0.0 us)
Async XLA Ops:
  0.0 1.0 %copy-start = (f32[16,8,1024]{2,1,0:T(8,128)S(1)}, f32[16,8,1024]{2,1,0:T(8,128)}, u32[]{:S(2)}) copy-start(f32[16,8,1024]{2,1,0:T(8,128)} %param.4) | copy-start | bytes 1572868
  1.0 5.1 %copy-start.1 = (f32[16,8,1024]{2,1,0:T(8,128)S(1)}, f32[16,8,1024]{2,1,0:T(8,128)}, u32[]{:S(2)}) copy-start(f32[16,8,1024]{2,1,0:T(8,128)} %param.4) | copy-start | bytes 1572868
  1.1 4.3 %copy-start.3 = (f32[3,2]{0,1:T(2,128)S(1)}, f32[3,2]{0,1:T(2,128)}, u32[]{:S(2)}) copy-start(f32[3,2]{0,1:T(2,128)} %param.6) | copy-start | bytes 76
  1.1 8.9 %collective-permute-start = (f32[2,16,8,128]{3,2,1,0:T(8,128)S(1)}, f32[2,16,8,128]{3,2,1,0:T(8,128)S(1)}, u32[]{:S(2)}, u32[]{:S(2)}) collective-permute-start(f32[2,16,8,128]{3,2,1,0:T(8,128)S(1)} %get-tuple-element.23._), channel_id=1, source_target_pairs={{0,8},{16,24},{32,40},{48,56},{64,72},{80,88},{96,104},{112,120},{... | collective-permute-start | bytes 393224 | tf_op jit(solution)/shard_map/ppermute | solution.py:349
  4.7 5.3 %collective-permute-start.1 = (f32[2,16,8,128]{3,2,1,0:T(8,128)S(1)}, f32[2,16,8,128]{3,2,1,0:T(8,128)S(1)}, u32[]{:S(2)}, u32[]{:S(2)}) collective-permute-start(f32[2,16,8,128]{3,2,1,0:T(8,128)S(1)} %get-tuple-element.24), channel_id=1, source_target_pairs={{8,16},{24,32},{40,48},{56,64},{72,80},{88,96},{104,112},{120,128}... | collective-permute-start | bytes 393224 | tf_op jit(solution)/shard_map/ppermute | solution.py:349
  5.5 0.7 %copy-start.2 = (f32[3]{0:T(128)S(1)}, f32[3]{0:T(128)}, u32[]{:S(2)}) copy-start(f32[3]{0:T(128)} %light_ref.5) | copy-start | bytes 40
  10.1 8.3 %collective-permute-start.2 = (f32[12,2,8,128]{3,2,1,0:T(8,128)S(1)}, f32[12,2,8,128]{3,2,1,0:T(8,128)S(1)}, u32[]{:S(2)}, u32[]{:S(2)}) collective-permute-start(f32[12,2,8,128]{3,2,1,0:T(8,128)S(1)} %get-tuple-element.26), channel_id=1, source_target_pairs={{0,1},{2,3},{4,5},{6,7},{1,0},{3,2},{5,4},{7,6},{8,9},{10,11},{12,... | collective-permute-start | bytes 294920 | tf_op jit(solution)/shard_map/ppermute | solution.py:349
  12.0 6.3 %collective-permute-start.3 = (f32[12,2,8,128]{3,2,1,0:T(8,128)S(1)}, f32[12,2,8,128]{3,2,1,0:T(8,128)S(1)}, u32[]{:S(2)}, u32[]{:S(2)}) collective-permute-start(f32[12,2,8,128]{3,2,1,0:T(8,128)S(1)} %get-tuple-element.27), channel_id=1, source_target_pairs={{1,2},{3,4},{5,6},{2,1},{4,3},{6,5},{9,10},{11,12},{13,14},{10,9},... | collective-permute-start | bytes 294920 | tf_op jit(solution)/shard_map/ppermute | solution.py:349

commit v4 on v3

v4 whole, which is shorter than its diff:
```python
import jax
import jax.numpy as jnp
from jax import lax
from jax.experimental import pallas as pl
from jax.experimental.pallas import tpu as pltpu
from jax.sharding import PartitionSpec as P

ROWS, SLABS, SUB, LANE = 16, 8, 8, 128
PAIR = 2
VM = pl.BlockSpec(memory_space=pltpu.VMEM)
SM = pl.BlockSpec(memory_space=pltpu.SMEM)


SMALL = pltpu.CompilerParams(vmem_limit_bytes=4 << 20)


def cells(x_ref, row, slab):
    return x_ref[pl.ds(row * 64 + slab, SUB, stride=SLABS), :]


def parity(axis):
    return lax.axis_index(axis) % 2


def pack_depth(x_ref, first_ref, second_ref):
    odd = parity("depth")
    start = (SLABS - 2) * (1 - odd)
    for row in range(ROWS):
        for k in range(2):
            first_ref[k, row] = cells(x_ref, row, start + k)
            second_ref[k, row] = cells(x_ref, row, (SLABS - 2) - start + k)


def by_parity(odd, first, second):
    is_odd = odd == 1
    return jnp.where(is_odd, first, second), jnp.where(is_odd, second, first)


def pack_strip(x_ref, from_first_ref, from_second_ref, _, first_ref, second_ref):
    odd = parity("strip")
    group_odd = parity("depth")
    start = (ROWS - 2) * (1 - odd)
    for ref, row in ((first_ref, start), (second_ref, (ROWS - 2) - start)):
        for k in range(2):
            for j in range(2):
                before, after = by_parity(
                    group_odd, from_first_ref[j, row + k], from_second_ref[j, row + k]
                )
                ref[j, k] = before
                ref[SLABS + 2 + j, k] = after
            for slab in range(SLABS):
                ref[2 + slab, k] = cells(x_ref, row + k, slab)


def rolled(v, shift, axis):
    return pltpu.roll(v.reshape(-1, SUB, LANE), shift, axis + 1).reshape(v.shape)


def column_neighbours(v):
    lane = lax.broadcasted_iota(jnp.int32, v.shape, v.ndim - 1)
    sub = lax.broadcasted_iota(jnp.int32, v.shape, v.ndim - 2)
    a = rolled(v, 1, 1)
    prev = jnp.where(lane == 0, jnp.where(sub == 0, 0.0, rolled(a, 1, 0)), a)
    a = rolled(v, LANE - 1, 1)
    following = jnp.where(lane == LANE - 1, jnp.where(sub == SUB - 1, 0.0, rolled(a, SUB - 1, 0)), a)
    return prev, following


def log1p_unit(e):
    t = e / (2.0 + e)
    q = t * t
    s = 1.0 / 13.0
    for d in (11.0, 9.0, 7.0, 5.0, 3.0):
        s = s * q + 1.0 / d
    return 2.0 * t + 2.0 * t * (q * s)


def row_sums(z):
    e = z[:-1] + z[1:]
    return e[:-1] + e[1:]


def slab_sums(v):
    e = v[:, :-1] + v[:, 1:]
    return e[:, :-1] + e[:, 1:]


def smoothed(m, factor):
    prev, following = column_neighbours(m)
    return ((prev + following) + (m + m)) * factor


def column_parts(s):
    prev, following = column_neighbours(s)
    return (prev + following) + (s + s), following - prev


def gradient_parts(u, w, light):
    scale = 0.5 * 0.25 * 0.25
    y = (light[1] * scale) * (u[:, 2:] - u[:, :-2]) + (light[2] * scale) * slab_sums(w)
    p = (light[0] * scale) * slab_sums(u)
    return y + p, y - p, y + y


def shade(s, facing, front, ext, slopes, offsets):
    half = 0.5 - 0.35 / (1.0 + facing * facing)
    z = s + s
    soft = jnp.maximum(z, 0.0) + log1p_unit(jnp.exp(-jnp.abs(z)))
    clear = jnp.exp(-ext * soft)
    weight = (1.0 - clear) * half
    tones = [jnp.tanh(a * s + b) + 1.0 for a, b in zip(slopes, offsets)]
    total = front
    for k in range(s.shape[1]):
        if total is None:
            total = [weight[:, k] * t[:, k] for t in tones] + [clear[:, k]]
        else:
            here = weight[:, k] * total[3]
            total = [c + here * t[:, k] for c, t in zip(total, tones)] + [total[3] * clear[:, k]]
    return total


def over(front, back):
    through = front[3]
    return [f + through * c for f, c in zip(front[:3], back[:3])] + [through * back[3]]


def coefficients(ext_ref, cmap_ref, light_ref):
    light = [light_ref[i] for i in range(3)]
    slopes = [cmap_ref[c, 0] * 0.5 for c in range(3)]
    offsets = [cmap_ref[c, 1] * 0.5 for c in range(3)]
    return light, (ext_ref[0], slopes, offsets)


def ends_inside(axis):
    index, count = lax.axis_index(axis), lax.axis_size(axis)
    return jnp.where(index == 0, 0.0, 1.0), jnp.where(index == count - 1, 0.0, 1.0)


def binomial(v):
    e = [a + b for a, b in zip(v, v[1:])]
    return [a + b for a, b in zip(e, e[1:])]


def render_inner(ext_ref, cmap_ref, light_ref, x_ref, _, z_ref, u_ref, w_ref, ap_ref, am_ref, y_ref,
                 s_ref, mid_ref):
    light, color = coefficients(ext_ref, cmap_ref, light_ref)

    def first(i, _):
        for row in (2 * i, 2 * i + 1):
            z = binomial([cells(x_ref, row, slab) for slab in range(SLABS)])
            for i, v in enumerate(z):
                z_ref[row, i] = v
        return 0

    lax.fori_loop(0, ROWS // 2, first, 0)

    def second(i, _):
        row = PAIR * i + 1
        s = smoothed(row_sums(z_ref[pl.ds(row - 1, PAIR + 2)]), 1.0 / 64.0)
        u, w = column_parts(s)
        here = pl.ds(row, PAIR)
        for i, k in enumerate((0, 1, 4, 5)):
            u_ref[here, i] = u[:, k]
            w_ref[here, i] = w[:, k]
        ap_ref[here], am_ref[here], y_ref[here] = gradient_parts(u, w, light)
        s_ref[here] = s
        return 0

    lax.fori_loop(0, (ROWS - 2) // PAIR, second, 0)

    def third(i, _):
        row = 2 * i + 2
        here = pl.ds(row, 2)
        facing = (ap_ref[pl.ds(row + 1, 2)] + am_ref[pl.ds(row - 1, 2)]) + y_ref[here]
        total = shade(s_ref[here, 1:5], facing, None, *color)
        for c in range(4):
            mid_ref[c, here] = total[c]
        return 0

    lax.fori_loop(0, (ROWS - 4) // 2, third, 0)


def render_outer(ext_ref, cmap_ref, light_ref, x_ref, depth_first_ref, depth_second_ref, zi_ref,
                 ui_ref, wi_ref, api_ref, ami_ref, yi_ref, si_ref, mid_ref, part_ref, zk_ref,
                 facing_ref, sk_ref, z_ref, ap_ref, am_ref, y_ref, s_ref):
    light, color = coefficients(ext_ref, cmap_ref, light_ref)
    odd_group = parity("depth")
    edge_before, edge_after = ends_inside("depth")

    def first(i, _):
        for row in (2 * i, 2 * i + 1):
            ends = [
                by_parity(odd_group, depth_first_ref[k, row], depth_second_ref[k, row])
                for k in range(2)
            ]
            z = binomial([ends[0][0], ends[1][0], cells(x_ref, row, 0), cells(x_ref, row, 1)])
            z += binomial([cells(x_ref, row, 6), cells(x_ref, row, 7), ends[0][1], ends[1][1]])
            z_ref[row, 0] = z[0] * edge_before
            z_ref[row, 1] = z[1]
            z_ref[row, 2] = z[2]
            z_ref[row, 3] = z[3] * edge_after
        return 0

    lax.fori_loop(0, ROWS // 2, first, 0)

    def second(i, _):
        row = PAIR * i + 1
        here = pl.ds(row, PAIR)
        s = smoothed(row_sums(z_ref[pl.ds(row - 1, PAIR + 2)]), 1.0 / 64.0)
        u, w = column_parts(s)
        for side in range(2):
            at = pl.ds(2 * side, 2)
            if side == 0:
                us = jnp.concatenate([u[:, 0:2], ui_ref[here, 0:2]], 1)
                ws = jnp.concatenate([w[:, 0:2], wi_ref[here, 0:2]], 1)
            else:
                us = jnp.concatenate([ui_ref[here, 2:4], u[:, 2:4]], 1)
                ws = jnp.concatenate([wi_ref[here, 2:4], w[:, 2:4]], 1)
            ap_ref[here, at], am_ref[here, at], y_ref[here, at] = gradient_parts(us, ws, light)
        s_ref[here, 0] = s[:, 1]
        s_ref[here, 1] = si_ref[here, 0]
        s_ref[here, 2] = si_ref[here, 5]
        s_ref[here, 3] = s[:, 2]
        return 0

    lax.fori_loop(0, (ROWS - 2) // PAIR, second, 0)

    def third(i, _):
        row = 2 * i + 2
        here = pl.ds(row, 2)
        facing = (ap_ref[pl.ds(row + 1, 2)] + am_ref[pl.ds(row - 1, 2)]) + y_ref[here]
        s = s_ref[here]
        front = shade(s[:, 0:2], facing[:, 0:2], None, *color)
        total = over(front, [mid_ref[c, here] for c in range(4)])
        total = shade(s[:, 2:4], facing[:, 2:4], total, *color)
        for c in range(4):
            part_ref[c, here] = total[c]
        return 0

    lax.fori_loop(0, (ROWS - 4) // 2, third, 0)

    def whole(inner, outer):
        return jnp.concatenate([outer[0:2], inner, outer[2:4]], 0)

    for i, row in enumerate((0, 1, ROWS - 2, ROWS - 1)):
        zk_ref[i] = whole(zi_ref[row], z_ref[row])
    facing_ref[0] = whole(api_ref[1], ap_ref[1])
    facing_ref[1] = whole(api_ref[2] + yi_ref[1], ap_ref[2] + y_ref[1])
    facing_ref[2] = whole(ami_ref[ROWS - 3] + yi_ref[ROWS - 2], am_ref[ROWS - 3] + y_ref[ROWS - 2])
    facing_ref[3] = whole(ami_ref[ROWS - 2], am_ref[ROWS - 2])
    for i, row in enumerate((1, ROWS - 2)):
        sk_ref[i, 0] = s_ref[row, 0]
        sk_ref[i, 1:7] = si_ref[row]
        sk_ref[i, 7] = s_ref[row, 3]


def render_rows(ext_ref, cmap_ref, light_ref, strip_first_ref, strip_second_ref, part_ref, zk_ref,
                facing_ref, sk_ref, out_ref, halo_ref, all_ref):
    light, color = coefficients(ext_ref, cmap_ref, light_ref)
    odd_strip = parity("strip")
    edge_before, edge_after = ends_inside("depth")
    edge_up, edge_down = ends_inside("strip")

    for base, ref in ((2 * (1 - odd_strip), strip_first_ref), (2 * odd_strip, strip_second_ref)):
        for j in range(2):
            z = binomial([ref[slab, j] for slab in range(SLABS + 4)])
            z[0] = z[0] * edge_before
            z[-1] = z[-1] * edge_after
            for i, v in enumerate(z):
                halo_ref[base + j, i] = v

    def row_parts(lower, middle, upper, factor):
        s = smoothed((lower + middle) + (middle + upper), factor)[None]
        u, w = column_parts(s)
        return s[:, 1:-1], *gradient_parts(u, w, light)

    def finish(row, s, facing):
        total = shade(s, facing, None, *color)
        for c in range(4):
            all_ref[(c * ROWS + row) * SUB : (c * ROWS + row + 1) * SUB, :] = total[c][0]

    _, _, above, _ = row_parts(halo_ref[0], halo_ref[1], zk_ref[0], edge_up * (1.0 / 64.0))
    s, _, am, y = row_parts(halo_ref[1], zk_ref[0], zk_ref[1], 1.0 / 64.0)
    finish(0, s, facing_ref[0:1] + above + y)
    finish(1, sk_ref[0:1], facing_ref[1:2] + am)
    _, below, _, _ = row_parts(zk_ref[3], halo_ref[2], halo_ref[3], edge_down * (1.0 / 64.0))
    s, ap, _, y = row_parts(zk_ref[2], zk_ref[3], halo_ref[2], 1.0 / 64.0)
    finish(ROWS - 1, s, facing_ref[3:4] + below + y)
    finish(ROWS - 2, sk_ref[1:2], facing_ref[2:3] + ap)
    for c in range(4):
        for row in range(2, ROWS - 2):
            all_ref[(c * ROWS + row) * SUB : (c * ROWS + row + 1) * SUB, :] = part_ref[c, row]

    chunk = lax.broadcasted_iota(jnp.int32, (SUB, LANE), 1) // 16
    for tile in range(SUB):
        v = [all_ref[pl.ds(g * 64 + tile, SUB, stride=SUB), :] for g in range(8)]
        for bit in (4, 2, 1):
            upper = (chunk & bit) != 0
            for i in range(8):
                if i & bit == 0:
                    lo, hi = v[i], v[i + bit]
                    v[i] = jnp.where(upper, pltpu.roll(hi, 16 * bit, 1), lo)
                    v[i + bit] = jnp.where(upper, hi, pltpu.roll(lo, LANE - 16 * bit, 1))
        for m in range(8):
            row = (tile * 8 + m) * SUB
            out_ref[row : row + SUB, :] = v[m]


def composite(parts_ref, out_ref):
    is_clear = lax.broadcasted_iota(jnp.int32, (SUB, LANE), 1) >= 96
    through = jnp.ones((SUB, LANE), jnp.float32)
    total = jnp.zeros((SUB, LANE), jnp.float32)
    for d in range(parts_ref.shape[0] // SUB):
        x = parts_ref[d * SUB : (d + 1) * SUB, :]
        total = total + through * x
        m = jnp.where(is_clear, x, 1.0)
        m = m * pltpu.roll(m, 32, 1)
        m = m * pltpu.roll(m, 64, 1)
        through = through * m
    result = jnp.where(is_clear, 1.0 - through, total)
    for i in range(8):
        moved = result if i == 0 else pltpu.roll(result, LANE - 16 * i, 1)
        out_ref[i * SUB : (i + 1) * SUB, :] = moved[:, 0:16]


def f32(*shape):
    return pltpu.VMEM(shape, jnp.float32)


def near(*arrays):
    return [pltpu.with_memory_space_constraint(a, pltpu.VMEM) for a in arrays]


def local(volume, extinction, color_map, light_direction):
    groups = lax.axis_size("depth")
    x = volume.reshape(ROWS, SLABS, SUB, LANE).transpose(0, 2, 1, 3).reshape(ROWS * 64, LANE)

    def swaps(count):
        out = []
        for start in range(2):
            half = [(i, i + 1) for i in range(start, count - 1, 2)]
            out.append(half + [(b, a) for a, b in half])
        return out

    def exchange(buffers, axis):
        return [lax.ppermute(v, axis, p) for v, p in zip(buffers, swaps(lax.axis_size(axis)))]

    packed = pl.pallas_call(
        pack_depth, in_specs=[VM], compiler_params=SMALL, out_specs=[VM, VM], name="pack_depth",
        out_shape=[f32(2, ROWS, SUB, LANE)] * 2,
    )(*near(x))
    near_depth = exchange(packed, "depth")

    params = (extinction, color_map, light_direction)

    def kernel(body, operands, shapes, scratch=()):
        return pl.pallas_call(
            body, in_specs=[SM] * 3 + [VM] * len(operands), out_specs=[VM] * len(shapes),
            name=body.__name__, compiler_params=SMALL, out_shape=[f32(*shape) for shape in shapes],
            scratch_shapes=[f32(*shape) for shape in scratch],
        )(*params, *near(*operands))

    four = (ROWS, 4, SUB, LANE)
    zi, ui, wi, api, ami, yi, si, mid = kernel(
        render_inner, (x, packed[0]),
        [(ROWS, 6, SUB, LANE)] + [four] * 5 + [(ROWS, 6, SUB, LANE), (4, ROWS, SUB, LANE)],
    )
    near_strip = exchange(
        pl.pallas_call(
            pack_strip, in_specs=[VM] * 4, compiler_params=SMALL, out_specs=[VM, VM], name="pack_strip",
            out_shape=[f32(SLABS + 4, 2, SUB, LANE)] * 2,
        )(*near(x, *near_depth, mid)),
        "strip",
    )
    kept = kernel(
        render_outer, (x, *near_depth, zi, ui, wi, api, ami, yi, si, mid),
        [(4, ROWS, SUB, LANE), (4, SLABS + 2, SUB, LANE), (4, SLABS, SUB, LANE), (2, SLABS, SUB, LANE)],
        [four] * 5,
    )
    (blocks,) = kernel(
        render_rows, (*near_strip, *kept),
        [(groups * SUB, LANE)], [(4, SLABS + 2, SUB, LANE), (4 * ROWS * SUB, LANE)],
    )
    layers = lax.all_to_all(
        blocks.reshape(groups, SUB, LANE), "depth", split_axis=0, concat_axis=0, tiled=True
    )
    image = pl.pallas_call(
        composite, in_specs=[VM], compiler_params=SMALL, out_specs=VM, name="composite",
        out_shape=jax.ShapeDtypeStruct((64, 16), jnp.float32),
    )(*near(layers.reshape(groups * SUB, LANE)))
    return image.reshape(4, 16, 16)


def solution(mesh):
    in_specs = (P("strip", "depth", None), P(), P(), P())
    out_specs = P(None, "strip", "depth")
    return jax.shard_map(local, mesh=mesh, in_specs=in_specs, out_specs=out_specs, check_vma=False)
```

time: 56.1 us -> 53.1 us (0.947)
  blocking collectives: 34 us -> 30.4 us
  Pallas kernels: 11.1 us -> 7.54 us
  starting transfers between devices: 8.75 us -> 11.6 us
  waiting for transfers between devices: 0.01 us -> 0.88 us
    all_to_all x1, blocking collectives: 34 us -> 30.4 us  [local(): lax.all_to_all(blocks.reshape(groups, SUB, LANE), 'depth', split_axis=0,...]
    pallas_call x3, Pallas kernels: 10.1 us -> 6.51 us  [kernel(): pl.pallas_call(body, in_specs=[SM] * 3 + [VM] * len(operands), out_specs=...]
    ppermute x4, starting transfers between devices: 8.75 us -> 11.6 us  [exchange(): lax.ppermute(v, axis, p)]
    ppermute x4, waiting for transfers between devices: 0.01 us -> 0.88 us  [exchange(): lax.ppermute(v, axis, p)]
  transfers between devices with their start and end apart: 4 -> 4, of which waited for: 0 -> 1; matrix products, arithmetic and copies ran while one was open for 0% -> 0% of each run, Pallas kernels for 14% -> 9%
where the time goes in v4:
time: 53.1 us; the launch traced here: 52.8 us
  blocking collectives  30.4 us (57%)
  starting transfers between devices  11.6 us (22%)
  Pallas kernels  7.54 us (14%)
  local copies, waits for them, and re-layouts  1.7 us (3%)
  waiting for transfers between devices  0.88 us (2%)
  between operations  0.76 us (1%)
    all_to_all x1, blocking collectives, local(): lax.all_to_all(blocks.reshape(groups, SUB, LANE), 'depth', split_axis=0,...  30.4 us
    ppermute x4, starting transfers between devices, exchange(): lax.ppermute(v, axis, p)  11.6 us
    pallas_call x3, Pallas kernels, kernel(): pl.pallas_call(body, in_specs=[SM] * 3 + [VM] * len(operands), out_specs=...  6.51 us
    unnamed x9, local copies, waits for them, and re-layouts  1.7 us
  transfers between devices with their start and end apart: 4, of which 1 were waited for; matrix products, arithmetic and copies ran while one was open for 0% of the time, Pallas kernels for 9%

profile of v4, /device:TPU:4, one launch (start us, length us, event | category | flops | bytes accessed | tf_op | source)
XLA Modules:
  0.0 52.8 jit_solution(11345275965091375899)
XLA Ops:
  0.0 0.0 copy-start
  0.0 1.0 %copy-done = f32[16,8,1024]{2,1,0:T(8,128)S(1)} copy-done((f32[16,8,1024]{2,1,0:T(8,128)S(1)}, f32[16,8,1024]{2,1,0:T(8,128)}, u32[]{:S(2)}) %copy-start) | copy-done | bytes 524312
  1.0 0.0 copy-start.1
  1.0 0.1 pack_depth.1
  1.1 0.8 %collective-permute-start.1 = (f32[2,16,8,128]{3,2,1,0:T(8,128)S(1)}, f32[2,16,8,128]{3,2,1,0:T(8,128)S(1)}, u32[]{:S(2)}, u32[]{:S(2)}) collective-permute-start(f32[2,16,8,128]{3,2,1,0:T(8,128)S(1)} %get-tuple-element.22), channel_id=1, source_target_pairs={{8,16},{24,32},{40,48},{56,64},{72,80},{88,96},{104,112},{120,128}... | collective-permute-start | bytes 393224 | tf_op jit(solution)/shard_map/ppermute | solution.py:346
  1.9 0.0 copy-start.3
  1.9 6.3 %collective-permute-start = (f32[2,16,8,128]{3,2,1,0:T(8,128)S(1)}, f32[2,16,8,128]{3,2,1,0:T(8,128)S(1)}, u32[]{:S(2)}, u32[]{:S(2)}) collective-permute-start(f32[2,16,8,128]{3,2,1,0:T(8,128)S(1)} %get-tuple-element.21._), channel_id=1, source_target_pairs={{0,8},{16,24},{32,40},{48,56},{64,72},{80,88},{96,104},{112,120},{... | collective-permute-start | bytes 393224 | tf_op jit(solution)/shard_map/ppermute | solution.py:346
  8.9 0.0 copy-done.3
  8.9 0.0 copy-start.2
  8.9 0.1 copy.7.cmap_ref
  9.0 0.0 copy-done.1
  9.0 0.6 %copy-done.2 = f32[3]{0:T(128)S(1)} copy-done((f32[3]{0:T(128)S(1)}, f32[3]{0:T(128)}, u32[]{:S(2)}) %copy-start.2) | copy-done | bytes 36
  9.5 2.5 %render_inner.1 = (f32[16,6,8,128]{3,2,1,0:T(8,128)S(1)}, f32[16,4,8,128]{3,2,1,0:T(8,128)S(1)}, f32[16,4,8,128]{3,2,1,0:T(8,128)S(1)}, f32[16,4,8,128]{3,2,1,0:...) custom-call(f32[1]{0:T(128)S(6)} %copy.8.ext_ref, ...), custom_call_target="tpu_custom_call" | custom-call | tf_op jit(solution)/shard_map/render_inner/pallas_call | solution.py:357
  12.1 0.0 collective-permute-done.1.from_second_ref.depth_second_ref
  12.1 0.0 collective-permute-done.from_first_ref.depth_first_ref
  12.1 1.9 %collective-permute-start.2 = (f32[12,2,8,128]{3,2,1,0:T(8,128)S(1)}, f32[12,2,8,128]{3,2,1,0:T(8,128)S(1)}, u32[]{:S(2)}, u32[]{:S(2)}) collective-permute-start(f32[12,2,8,128]{3,2,1,0:T(8,128)S(1)} %get-tuple-element.24), channel_id=1, source_target_pairs={{0,1},{2,3},{4,5},{6,7},{1,0},{3,2},{5,4},{7,6},{8,9},{10,11},{12,... | collective-permute-start | bytes 294920 | tf_op jit(solution)/shard_map/ppermute | solution.py:346
  14.1 2.5 %collective-permute-start.3 = (f32[12,2,8,128]{3,2,1,0:T(8,128)S(1)}, f32[12,2,8,128]{3,2,1,0:T(8,128)S(1)}, u32[]{:S(2)}, u32[]{:S(2)}) collective-permute-start(f32[12,2,8,128]{3,2,1,0:T(8,128)S(1)} %get-tuple-element.25), channel_id=1, source_target_pairs={{1,2},{3,4},{5,6},{2,1},{4,3},{6,5},{9,10},{11,12},{13,14},{10,9},... | collective-permute-start | bytes 294920 | tf_op jit(solution)/shard_map/ppermute | solution.py:346
  16.6 2.5 %render_outer.1 = (f32[4,16,8,128]{3,2,1,0:T(8,128)S(1)}, f32[4,10,8,128]{3,2,1,0:T(8,128)S(1)}, f32[4,8,8,128]{3,2,1,0:T(8,128)S(1)}, f32[2,8,8,128]{3,2,1,0:T(8,128)S(1)}) custom-call(f32[1]{0:T(128)S(6)} %copy.8.ext_ref, f32[3,2]{1,0:T(4,128)S(1)} %copy.7.cmap_ref, f32[3]{0:T(128)S(1)} %copy-done.2, f32[1024,128]{1,0:T(8,128)S(1)} %bitcast.11, ...), custom_call_target="tpu_custom_call" | custom-call | tf_op jit(solution)/shard_map/render_outer/pallas_call | solution.py:357
  19.1 0.0 collective-permute-done.2.strip_first_ref
  19.1 0.9 %collective-permute-done.3.strip_second_ref = f32[12,2,8,128]{3,2,1,0:T(8,128)S(1)} collective-permute-done((f32[12,2,8,128]{3,2,1,0:T(8,128)S(1)}, f32[12,2,8,128]{3,2,1,0:T(8,128)S(1)}, u32[]{:S(2)}, u32[]{:S(2)}) %collective-permute-start.3) | collective-permute-done | bytes 98336 | tf_op jit(solution)/shard_map/ppermute | solution.py:346
  20.0 1.5 %render_rows.1 = f32[512,128]{1,0:T(8,128)S(1)} custom-call(f32[1]{0:T(128)S(6)} %copy.8.ext_ref, f32[3,2]{1,0:T(4,128)S(1)} %copy.7.cmap_ref, f32[3]{0:T(128)S(1)} %copy-done.2, f32[12,2,8,128]{3,2,1,0:T(8,128)S(1)} %collective-permute-done.2.strip_first_ref, f32[12,2,8,128]{3,2,1,0:T(8,128)S(1)} %collective-permute-done.3.strip_second_ref, ...), custom_call_target="tpu_custom_call" | custom-call | tf_op jit(solution)/shard_map/render_rows/pallas_call | solution.py:357
  21.5 30.4 %all_to_all.5 = f32[64,8,128]{2,1,0:T(8,128)S(1)} all-to-all(f32[64,8,128]{2,1,0:T(8,128)S(1)} %bitcast.12), channel_id=1, replica_groups=mesh['depth'=64,'strip'=8] {'depth'}, dimensions={0} | all-to-all | bytes 524288 | tf_op jit(solution)/shard_map/all_to_all | solution.py:384
  51.9 0.9 %composite.1 = f32[64,16]{1,0:T(8,128)} custom-call(f32[512,128]{1,0:T(8,128)S(1)} %bitcast.13), custom_call_target="tpu_custom_call" | custom-call | tf_op jit(solution)/shard_map/composite/pallas_call | solution.py:387
  (1 shorter events, 0.0 us)
Async XLA Ops:
  0.0 1.0 %copy-start = (f32[16,8,1024]{2,1,0:T(8,128)S(1)}, f32[16,8,1024]{2,1,0:T(8,128)}, u32[]{:S(2)}) copy-start(f32[16,8,1024]{2,1,0:T(8,128)} %param.4) | copy-start | bytes 1572868
  1.0 8.0 %copy-start.1 = (f32[16,8,1024]{2,1,0:T(8,128)S(1)}, f32[16,8,1024]{2,1,0:T(8,128)}, u32[]{:S(2)}) copy-start(f32[16,8,1024]{2,1,0:T(8,128)} %param.4) | copy-start | bytes 1572868
  1.1 11.0 %collective-permute-start.1 = (f32[2,16,8,128]{3,2,1,0:T(8,128)S(1)}, f32[2,16,8,128]{3,2,1,0:T(8,128)S(1)}, u32[]{:S(2)}, u32[]{:S(2)}) collective-permute-start(f32[2,16,8,128]{3,2,1,0:T(8,128)S(1)} %get-tuple-element.22), channel_id=1, source_target_pairs={{8,16},{24,32},{40,48},{56,64},{72,80},{88,96},{104,112},{120,128}... | collective-permute-start | bytes 393224 | tf_op jit(solution)/shard_map/ppermute | solution.py:346
  1.9 7.0 %copy-start.3 = (f32[3,2]{0,1:T(2,128)S(1)}, f32[3,2]{0,1:T(2,128)}, u32[]{:S(2)}) copy-start(f32[3,2]{0,1:T(2,128)} %param.6) | copy-start | bytes 76
  1.9 10.2 %collective-permute-start = (f32[2,16,8,128]{3,2,1,0:T(8,128)S(1)}, f32[2,16,8,128]{3,2,1,0:T(8,128)S(1)}, u32[]{:S(2)}, u32[]{:S(2)}) collective-permute-start(f32[2,16,8,128]{3,2,1,0:T(8,128)S(1)} %get-tuple-element.21._), channel_id=1, source_target_pairs={{0,8},{16,24},{32,40},{48,56},{64,72},{80,88},{96,104},{112,120},{... | collective-permute-start | bytes 393224 | tf_op jit(solution)/shard_map/ppermute | solution.py:346
  8.9 0.7 %copy-start.2 = (f32[3]{0:T(128)S(1)}, f32[3]{0:T(128)}, u32[]{:S(2)}) copy-start(f32[3]{0:T(128)} %light_ref.5) | copy-start | bytes 40
  12.1 7.0 %collective-permute-start.2 = (f32[12,2,8,128]{3,2,1,0:T(8,128)S(1)}, f32[12,2,8,128]{3,2,1,0:T(8,128)S(1)}, u32[]{:S(2)}, u32[]{:S(2)}) collective-permute-start(f32[12,2,8,128]{3,2,1,0:T(8,128)S(1)} %get-tuple-element.24), channel_id=1, source_target_pairs={{0,1},{2,3},{4,5},{6,7},{1,0},{3,2},{5,4},{7,6},{8,9},{10,11},{12,... | collective-permute-start | bytes 294920 | tf_op jit(solution)/shard_map/ppermute | solution.py:346
  14.1 5.9 %collective-permute-start.3 = (f32[12,2,8,128]{3,2,1,0:T(8,128)S(1)}, f32[12,2,8,128]{3,2,1,0:T(8,128)S(1)}, u32[]{:S(2)}, u32[]{:S(2)}) collective-permute-start(f32[12,2,8,128]{3,2,1,0:T(8,128)S(1)} %get-tuple-element.25), channel_id=1, source_target_pairs={{1,2},{3,4},{5,6},{2,1},{4,3},{6,5},{9,10},{11,12},{13,14},{10,9},... | collective-permute-start | bytes 294920 | tf_op jit(solution)/shard_map/ppermute | solution.py:346

commit v5 on v4

--- a/solution.py
+++ b/solution.py
@@ -4,6 +4,7 @@
 from jax.experimental import pallas as pl
 from jax.experimental.pallas import tpu as pltpu
 from jax.sharding import PartitionSpec as P
+
 
 ROWS, SLABS, SUB, LANE = 16, 8, 8, 128
 PAIR = 2
@@ -67,12 +68,8 @@
 
 
 def log1p_unit(e):
-    t = e / (2.0 + e)
-    q = t * t
-    s = 1.0 / 13.0
-    for d in (11.0, 9.0, 7.0, 5.0, 3.0):
-        s = s * q + 1.0 / d
-    return 2.0 * t + 2.0 * t * (q * s)
+    w = 1.0 + e
+    return jnp.log(w) + (e - (w - 1.0))
 
 
 def row_sums(z):
@@ -152,7 +149,7 @@
                 z_ref[row, i] = v
         return 0
 
-    lax.fori_loop(0, ROWS // 2, first, 0)
+    lax.fori_loop(0, ROWS // 2, first, 0, unroll=True)
 
     def second(i, _):
         row = PAIR * i + 1
@@ -166,7 +163,7 @@
         s_ref[here] = s
         return 0
 
-    lax.fori_loop(0, (ROWS - 2) // PAIR, second, 0)
+    lax.fori_loop(0, (ROWS - 2) // PAIR, second, 0, unroll=True)
 
     def third(i, _):
         row = 2 * i + 2
@@ -177,7 +174,7 @@
             mid_ref[c, here] = total[c]
         return 0
 
-    lax.fori_loop(0, (ROWS - 4) // 2, third, 0)
+    lax.fori_loop(0, (ROWS - 4) // 2, third, 0, unroll=True)
 
 
 def render_outer(ext_ref, cmap_ref, light_ref, x_ref, depth_first_ref, depth_second_ref, zi_ref,
@@ -201,7 +198,7 @@
             z_ref[row, 3] = z[3] * edge_after
         return 0
 
-    lax.fori_loop(0, ROWS // 2, first, 0)
+    lax.fori_loop(0, ROWS // 2, first, 0, unroll=True)
 
     def second(i, _):
         row = PAIR * i + 1
@@ -223,7 +220,7 @@
         s_ref[here, 3] = s[:, 2]
         return 0
 
-    lax.fori_loop(0, (ROWS - 2) // PAIR, second, 0)
+    lax.fori_loop(0, (ROWS - 2) // PAIR, second, 0, unroll=True)
 
     def third(i, _):
         row = 2 * i + 2
@@ -237,17 +234,17 @@
             part_ref[c, here] = total[c]
         return 0
 
-    lax.fori_loop(0, (ROWS - 4) // 2, third, 0)
+    lax.fori_loop(0, (ROWS - 4) // 2, third, 0, unroll=True)
 
     def whole(inner, outer):
         return jnp.concatenate([outer[0:2], inner, outer[2:4]], 0)
 
-    for i, row in enumerate((0, 1, ROWS - 2, ROWS - 1)):
+    for i, row in enumerate((0, 1, ROWS - 1, ROWS - 2)):
         zk_ref[i] = whole(zi_ref[row], z_ref[row])
     facing_ref[0] = whole(api_ref[1], ap_ref[1])
     facing_ref[1] = whole(api_ref[2] + yi_ref[1], ap_ref[2] + y_ref[1])
-    facing_ref[2] = whole(ami_ref[ROWS - 3] + yi_ref[ROWS - 2], am_ref[ROWS - 3] + y_ref[ROWS - 2])
-    facing_ref[3] = whole(ami_ref[ROWS - 2], am_ref[ROWS - 2])
+    facing_ref[2] = whole(ami_ref[ROWS - 2], am_ref[ROWS - 2])
+    facing_ref[3] = whole(ami_ref[ROWS - 3] + yi_ref[ROWS - 2], am_ref[ROWS - 3] + y_ref[ROWS - 2])
     for i, row in enumerate((1, ROWS - 2)):
         sk_ref[i, 0] = s_ref[row, 0]
         sk_ref[i, 1:7] = si_ref[row]
@@ -261,63 +258,77 @@
     edge_before, edge_after = ends_inside("depth")
     edge_up, edge_down = ends_inside("strip")
 
-    for base, ref in ((2 * (1 - odd_strip), strip_first_ref), (2 * odd_strip, strip_second_ref)):
+    for half, ref in ((1 - odd_strip, strip_first_ref), (odd_strip, strip_second_ref)):
         for j in range(2):
             z = binomial([ref[slab, j] for slab in range(SLABS + 4)])
             z[0] = z[0] * edge_before
             z[-1] = z[-1] * edge_after
             for i, v in enumerate(z):
-                halo_ref[base + j, i] = v
-
-    def row_parts(lower, middle, upper, factor):
-        s = smoothed((lower + middle) + (middle + upper), factor)[None]
-        u, w = column_parts(s)
-        return s[:, 1:-1], *gradient_parts(u, w, light)
-
-    def finish(row, s, facing):
-        total = shade(s, facing, None, *color)
-        for c in range(4):
-            all_ref[(c * ROWS + row) * SUB : (c * ROWS + row + 1) * SUB, :] = total[c][0]
-
-    _, _, above, _ = row_parts(halo_ref[0], halo_ref[1], zk_ref[0], edge_up * (1.0 / 64.0))
-    s, _, am, y = row_parts(halo_ref[1], zk_ref[0], zk_ref[1], 1.0 / 64.0)
-    finish(0, s, facing_ref[0:1] + above + y)
-    finish(1, sk_ref[0:1], facing_ref[1:2] + am)
-    _, below, _, _ = row_parts(zk_ref[3], halo_ref[2], halo_ref[3], edge_down * (1.0 / 64.0))
-    s, ap, _, y = row_parts(zk_ref[2], zk_ref[3], halo_ref[2], 1.0 / 64.0)
-    finish(ROWS - 1, s, facing_ref[3:4] + below + y)
-    finish(ROWS - 2, sk_ref[1:2], facing_ref[2:3] + ap)
+                halo_ref[3 * half + (1 - 2 * half) * j, i] = v
+
+    def boundary(half, _):
+        sign = 1.0 - 2.0 * half.astype(jnp.float32)
+        inside = jnp.where(half == 0, edge_up, edge_down) * (1.0 / 64.0)
+        outer, inner = halo_ref[2 * half], halo_ref[2 * half + 1]
+        first, second = zk_ref[2 * half], zk_ref[2 * half + 1]
+        mirrored = [light[0] * sign, light[1], light[2]]
+
+        def row_parts(lower, middle, upper, factor):
+            s = smoothed((lower + middle) + (middle + upper), factor)[None]
+            return s[:, 1:-1], *gradient_parts(*column_parts(s), mirrored)
+
+        def finish(row, s, facing):
+            total = shade(s, facing, None, *color)
+            for c in range(4):
+                all_ref[pl.ds(pl.multiple_of((c * ROWS + row) * SUB, SUB), SUB), :] = total[c][0]
+
+        _, _, beyond, _ = row_parts(outer, inner, first, inside)
+        s, _, inward, own = row_parts(inner, first, second, 1.0 / 64.0)
+        finish((ROWS - 1) * half, s, facing_ref[pl.ds(2 * half, 1)] + beyond + own)
+        finish(1 + (ROWS - 3) * half, sk_ref[pl.ds(half, 1)], facing_ref[pl.ds(2 * half + 1, 1)] + inward)
+        return 0
+
+    lax.fori_loop(0, 2, boundary, 0)
     for c in range(4):
         for row in range(2, ROWS - 2):
             all_ref[(c * ROWS + row) * SUB : (c * ROWS + row + 1) * SUB, :] = part_ref[c, row]
 
-    chunk = lax.broadcasted_iota(jnp.int32, (SUB, LANE), 1) // 16
-    for tile in range(SUB):
-        v = [all_ref[pl.ds(g * 64 + tile, SUB, stride=SUB), :] for g in range(8)]
-        for bit in (4, 2, 1):
-            upper = (chunk & bit) != 0
-            for i in range(8):
-                if i & bit == 0:
-                    lo, hi = v[i], v[i + bit]
-                    v[i] = jnp.where(upper, pltpu.roll(hi, 16 * bit, 1), lo)
-                    v[i + bit] = jnp.where(upper, hi, pltpu.roll(lo, LANE - 16 * bit, 1))
+    group = 1
+    chunk = lax.broadcasted_iota(jnp.int32, (group, SUB, LANE), 2) // 16
+    for start in range(0, SUB, group):
+        v = []
+        for g in range(8):
+            tiles = [all_ref[pl.ds(g * 64 + start + t, SUB, stride=SUB), :] for t in range(group)]
+            v.append(rolled(jnp.stack(tiles), 16 * g, 1) if g else jnp.stack(tiles))
+        for bit in (1, 2, 4):
+            v = [jnp.where((chunk & bit) != 0, v[(k + bit) % 8], v[k]) for k in range(8)]
         for m in range(8):
-            row = (tile * 8 + m) * SUB
-            out_ref[row : row + SUB, :] = v[m]
+            block = rolled(v[-m % 8], LANE - 16 * m, 1) if m else v[0]
+            for t in range(group):
+                row = ((start + t) * 8 + m) * SUB
+                out_ref[row : row + SUB, :] = block[t]
 
 
 def composite(parts_ref, out_ref):
     is_clear = lax.broadcasted_iota(jnp.int32, (SUB, LANE), 1) >= 96
-    through = jnp.ones((SUB, LANE), jnp.float32)
-    total = jnp.zeros((SUB, LANE), jnp.float32)
-    for d in range(parts_ref.shape[0] // SUB):
-        x = parts_ref[d * SUB : (d + 1) * SUB, :]
-        total = total + through * x
-        m = jnp.where(is_clear, x, 1.0)
-        m = m * pltpu.roll(m, 32, 1)
-        m = m * pltpu.roll(m, 64, 1)
-        through = through * m
-    result = jnp.where(is_clear, 1.0 - through, total)
+    count = parts_ref.shape[0] // SUB
+    runs = 4
+    through = [jnp.ones((SUB, LANE), jnp.float32)] * runs
+    total = [jnp.zeros((SUB, LANE), jnp.float32)] * runs
+    for step in range(count // runs):
+        for run in range(runs):
+            d = run * (count // runs) + step
+            x = parts_ref[d * SUB : (d + 1) * SUB, :]
+            total[run] = total[run] + through[run] * x
+            m = jnp.where(is_clear, x, 1.0)
+            m = m * pltpu.roll(m, 32, 1)
+            m = m * pltpu.roll(m, 64, 1)
+            through[run] = through[run] * m
+    image, clear = total[0], through[0]
+    for run in range(1, runs):
+        image = image + clear * total[run]
+        clear = clear * through[run]
+    result = jnp.where(is_clear, 1.0 - clear, image)
     for i in range(8):
         moved = result if i == 0 else pltpu.roll(result, LANE - 16 * i, 1)
         out_ref[i * SUB : (i + 1) * SUB, :] = moved[:, 0:16]
@@ -343,7 +354,10 @@
         return out
 
     def exchange(buffers, axis):
-        return [lax.ppermute(v, axis, p) for v, p in zip(buffers, swaps(lax.axis_size(axis)))]
+        out = []
+        for v, p in zip(buffers, swaps(lax.axis_size(axis))):
+            out.append(lax.ppermute(v, axis, p))
+        return out
 
     packed = pl.pallas_call(
         pack_depth, in_specs=[VM], compiler_params=SMALL, out_specs=[VM, VM], name="pack_depth",
@@ -356,7 +370,7 @@
     def kernel(body, operands, shapes, scratch=()):
         return pl.pallas_call(
             body, in_specs=[SM] * 3 + [VM] * len(operands), out_specs=[VM] * len(shapes),
-            name=body.__name__, compiler_params=SMALL, out_shape=[f32(*shape) for shape in shapes],
+            compiler_params=SMALL, out_shape=[f32(*shape) for shape in shapes],
             scratch_shapes=[f32(*shape) for shape in scratch],
         )(*params, *near(*operands))
 

time: 53.1 us -> 53 us (level)
  Pallas kernels: 7.54 us -> 5.14 us
  waiting for transfers between devices: 0.88 us -> 2.49 us
  blocking collectives: 30.4 us -> 31.1 us
    pallas_call x3, Pallas kernels: 6.51 us -> 4.14 us  [kernel(): pl.pallas_call(body, in_specs=[SM] * 3 + [VM] * len(operands), out_specs=...]
    ppermute x4, waiting for transfers between devices: 0.88 us -> 2.49 us  [exchange(): out.append(lax.ppermute(v, axis, p))]
    all_to_all x1, blocking collectives: 30.4 us -> 31.1 us  [local(): lax.all_to_all(blocks.reshape(groups, SUB, LANE), 'depth', split_axis=0,...]
  transfers between devices with their start and end apart: 4 -> 4, of which waited for: 1 -> 2; matrix products, arithmetic and copies ran while one was open for 0% -> 0% of each run, Pallas kernels for 9% -> 5%
where the time goes in v5:
time: 53 us; the launch traced here: 52.7 us
  blocking collectives  31.1 us (59%)
  starting transfers between devices  11.6 us (22%)
  Pallas kernels  5.14 us (10%)
  waiting for transfers between devices  2.49 us (5%)
  local copies, waits for them, and re-layouts  1.7 us (3%)
  between operations  0.74 us (1%)
    all_to_all x1, blocking collectives, local(): lax.all_to_all(blocks.reshape(groups, SUB, LANE), 'depth', split_axis=0,...  31.1 us
    ppermute x4, starting transfers between devices, exchange(): out.append(lax.ppermute(v, axis, p))  11.6 us
    pallas_call x3, Pallas kernels, kernel(): pl.pallas_call(body, in_specs=[SM] * 3 + [VM] * len(operands), out_specs=...  4.14 us
    ppermute x4, waiting for transfers between devices, exchange(): out.append(lax.ppermute(v, axis, p))  2.49 us
    unnamed x9, local copies, waits for them, and re-layouts  1.7 us
  transfers between devices with their start and end apart: 4, of which 2 were waited for; matrix products, arithmetic and copies ran while one was open for 0% of the time, Pallas kernels for 5%

profile of v5, /device:TPU:4, one launch (start us, length us, event | category | flops | bytes accessed | tf_op | source)
XLA Modules:
  0.0 52.7 jit_solution(16954817572653557724)
XLA Ops:
  0.0 0.0 copy-start
  0.0 1.0 %copy-done = f32[16,8,1024]{2,1,0:T(8,128)S(1)} copy-done((f32[16,8,1024]{2,1,0:T(8,128)S(1)}, f32[16,8,1024]{2,1,0:T(8,128)}, u32[]{:S(2)}) %copy-start) | copy-done | bytes 524312
  1.0 0.0 copy-start.1
  1.0 0.1 pack_depth.1
  1.1 0.8 %collective-permute-start.1 = (f32[2,16,8,128]{3,2,1,0:T(8,128)S(1)}, f32[2,16,8,128]{3,2,1,0:T(8,128)S(1)}, u32[]{:S(2)}, u32[]{:S(2)}) collective-permute-start(f32[2,16,8,128]{3,2,1,0:T(8,128)S(1)} %get-tuple-element.22), channel_id=1, source_target_pairs={{8,16},{24,32},{40,48},{56,64},{72,80},{88,96},{104,112},{120,128}... | collective-permute-start | bytes 393224 | tf_op jit(solution)/shard_map/ppermute | solution.py:359
  1.9 0.0 copy-start.3
  1.9 6.3 %collective-permute-start = (f32[2,16,8,128]{3,2,1,0:T(8,128)S(1)}, f32[2,16,8,128]{3,2,1,0:T(8,128)S(1)}, u32[]{:S(2)}, u32[]{:S(2)}) collective-permute-start(f32[2,16,8,128]{3,2,1,0:T(8,128)S(1)} %get-tuple-element.21._), channel_id=1, source_target_pairs={{0,8},{16,24},{32,40},{48,56},{64,72},{80,88},{96,104},{112,120},{... | collective-permute-start | bytes 393224 | tf_op jit(solution)/shard_map/ppermute | solution.py:359
  8.9 0.0 copy-done.3
  8.9 0.0 copy-start.2
  8.9 0.1 copy.7.cmap_ref
  9.0 0.0 copy-done.1
  9.0 0.6 %copy-done.2 = f32[3]{0:T(128)S(1)} copy-done((f32[3]{0:T(128)S(1)}, f32[3]{0:T(128)}, u32[]{:S(2)}) %copy-start.2) | copy-done | bytes 36
  9.5 1.5 %shard_map.46 = (f32[16,6,8,128]{3,2,1,0:T(8,128)S(1)}, f32[16,4,8,128]{3,2,1,0:T(8,128)S(1)}, f32[16,4,8,128]{3,2,1,0:T(8,128)S(1)}, f32[16,4,8,128]{3,2,1,0:T(...) custom-call(f32[1]{0:T(128)S(6)} %copy.8.ext_ref, ...), custom_call_target="tpu_custom_call" | custom-call | tf_op jit(solution)/shard_map/pallas_call | solution.py:371
  11.0 0.0 collective-permute-done.1.from_second_ref.depth_second_ref
  11.0 0.4 collective-permute-done.from_first_ref.depth_first_ref
  11.5 1.9 %collective-permute-start.2 = (f32[12,2,8,128]{3,2,1,0:T(8,128)S(1)}, f32[12,2,8,128]{3,2,1,0:T(8,128)S(1)}, u32[]{:S(2)}, u32[]{:S(2)}) collective-permute-start(f32[12,2,8,128]{3,2,1,0:T(8,128)S(1)} %get-tuple-element.24), channel_id=1, source_target_pairs={{0,1},{2,3},{4,5},{6,7},{1,0},{3,2},{5,4},{7,6},{8,9},{10,11},{12,... | collective-permute-start | bytes 294920 | tf_op jit(solution)/shard_map/ppermute | solution.py:359
  13.4 2.5 %collective-permute-start.3 = (f32[12,2,8,128]{3,2,1,0:T(8,128)S(1)}, f32[12,2,8,128]{3,2,1,0:T(8,128)S(1)}, u32[]{:S(2)}, u32[]{:S(2)}) collective-permute-start(f32[12,2,8,128]{3,2,1,0:T(8,128)S(1)} %get-tuple-element.25), channel_id=1, source_target_pairs={{1,2},{3,4},{5,6},{2,1},{4,3},{6,5},{9,10},{11,12},{13,14},{10,9},... | collective-permute-start | bytes 294920 | tf_op jit(solution)/shard_map/ppermute | solution.py:359
  15.9 1.3 %shard_map.47 = (f32[4,16,8,128]{3,2,1,0:T(8,128)S(1)}, f32[4,10,8,128]{3,2,1,0:T(8,128)S(1)}, f32[4,8,8,128]{3,2,1,0:T(8,128)S(1)}, f32[2,8,8,128]{3,2,1,0:T(8,128)S(1)}) custom-call(f32[1]{0:T(128)S(6)} %copy.8.ext_ref, f32[3,2]{1,0:T(4,128)S(1)} %copy.7.cmap_ref, f32[3]{0:T(128)S(1)} %copy-done.2, f32[1024,128]{1,0:T(8,128)S(1)} %bitcast.11, ...), custom_call_target="tpu_custom_call" | custom-call | tf_op jit(solution)/shard_map/pallas_call | solution.py:371
  17.2 0.0 collective-permute-done.2.strip_first_ref
  17.3 2.1 %collective-permute-done.3.strip_second_ref = f32[12,2,8,128]{3,2,1,0:T(8,128)S(1)} collective-permute-done((f32[12,2,8,128]{3,2,1,0:T(8,128)S(1)}, f32[12,2,8,128]{3,2,1,0:T(8,128)S(1)}, u32[]{:S(2)}, u32[]{:S(2)}) %collective-permute-start.3) | collective-permute-done | bytes 98336 | tf_op jit(solution)/shard_map/ppermute | solution.py:359
  19.3 1.4 %shard_map.48 = f32[512,128]{1,0:T(8,128)S(1)} custom-call(f32[1]{0:T(128)S(6)} %copy.8.ext_ref, f32[3,2]{1,0:T(4,128)S(1)} %copy.7.cmap_ref, f32[3]{0:T(128)S(1)} %copy-done.2, f32[12,2,8,128]{3,2,1,0:T(8,128)S(1)} %collective-permute-done.2.strip_first_ref, f32[12,2,8,128]{3,2,1,0:T(8,128)S(1)} %collective-permute-done.3.strip_second_ref, ...), custom_call_target="tpu_custom_call" | custom-call | tf_op jit(solution)/shard_map/pallas_call | solution.py:371
  20.7 31.1 %all_to_all.5 = f32[64,8,128]{2,1,0:T(8,128)S(1)} all-to-all(f32[64,8,128]{2,1,0:T(8,128)S(1)} %bitcast.12), channel_id=1, replica_groups=mesh['depth'=64,'strip'=8] {'depth'}, dimensions={0} | all-to-all | bytes 524288 | tf_op jit(solution)/shard_map/all_to_all | solution.py:398
  51.8 0.9 %composite.1 = f32[64,16]{1,0:T(8,128)} custom-call(f32[512,128]{1,0:T(8,128)S(1)} %bitcast.13), custom_call_target="tpu_custom_call" | custom-call | tf_op jit(solution)/shard_map/composite/pallas_call | solution.py:401
  (1 shorter events, 0.0 us)
Async XLA Ops:
  0.0 1.0 %copy-start = (f32[16,8,1024]{2,1,0:T(8,128)S(1)}, f32[16,8,1024]{2,1,0:T(8,128)}, u32[]{:S(2)}) copy-start(f32[16,8,1024]{2,1,0:T(8,128)} %param.4) | copy-start | bytes 1572868
  1.0 8.0 %copy-start.1 = (f32[16,8,1024]{2,1,0:T(8,128)S(1)}, f32[16,8,1024]{2,1,0:T(8,128)}, u32[]{:S(2)}) copy-start(f32[16,8,1024]{2,1,0:T(8,128)} %param.4) | copy-start | bytes 1572868
  1.1 9.9 %collective-permute-start.1 = (f32[2,16,8,128]{3,2,1,0:T(8,128)S(1)}, f32[2,16,8,128]{3,2,1,0:T(8,128)S(1)}, u32[]{:S(2)}, u32[]{:S(2)}) collective-permute-start(f32[2,16,8,128]{3,2,1,0:T(8,128)S(1)} %get-tuple-element.22), channel_id=1, source_target_pairs={{8,16},{24,32},{40,48},{56,64},{72,80},{88,96},{104,112},{120,128}... | collective-permute-start | bytes 393224 | tf_op jit(solution)/shard_map/ppermute | solution.py:359
  1.9 7.0 %copy-start.3 = (f32[3,2]{0,1:T(2,128)S(1)}, f32[3,2]{0,1:T(2,128)}, u32[]{:S(2)}) copy-start(f32[3,2]{0,1:T(2,128)} %param.6) | copy-start | bytes 76
  1.9 9.5 %collective-permute-start = (f32[2,16,8,128]{3,2,1,0:T(8,128)S(1)}, f32[2,16,8,128]{3,2,1,0:T(8,128)S(1)}, u32[]{:S(2)}, u32[]{:S(2)}) collective-permute-start(f32[2,16,8,128]{3,2,1,0:T(8,128)S(1)} %get-tuple-element.21._), channel_id=1, source_target_pairs={{0,8},{16,24},{32,40},{48,56},{64,72},{80,88},{96,104},{112,120},{... | collective-permute-start | bytes 393224 | tf_op jit(solution)/shard_map/ppermute | solution.py:359
  8.9 0.7 %copy-start.2 = (f32[3]{0:T(128)S(1)}, f32[3]{0:T(128)}, u32[]{:S(2)}) copy-start(f32[3]{0:T(128)} %light_ref.5) | copy-start | bytes 40
  11.5 5.8 %collective-permute-start.2 = (f32[12,2,8,128]{3,2,1,0:T(8,128)S(1)}, f32[12,2,8,128]{3,2,1,0:T(8,128)S(1)}, u32[]{:S(2)}, u32[]{:S(2)}) collective-permute-start(f32[12,2,8,128]{3,2,1,0:T(8,128)S(1)} %get-tuple-element.24), channel_id=1, source_target_pairs={{0,1},{2,3},{4,5},{6,7},{1,0},{3,2},{5,4},{7,6},{8,9},{10,11},{12,... | collective-permute-start | bytes 294920 | tf_op jit(solution)/shard_map/ppermute | solution.py:359
  13.4 5.9 %collective-permute-start.3 = (f32[12,2,8,128]{3,2,1,0:T(8,128)S(1)}, f32[12,2,8,128]{3,2,1,0:T(8,128)S(1)}, u32[]{:S(2)}, u32[]{:S(2)}) collective-permute-start(f32[12,2,8,128]{3,2,1,0:T(8,128)S(1)} %get-tuple-element.25), channel_id=1, source_target_pairs={{1,2},{3,4},{5,6},{2,1},{4,3},{6,5},{9,10},{11,12},{13,14},{10,9},... | collective-permute-start | bytes 294920 | tf_op jit(solution)/shard_map/ppermute | solution.py:359

commit v6 on v5

--- a/solution.py
+++ b/solution.py
@@ -23,13 +23,16 @@
     return lax.axis_index(axis) % 2
 
 
-def pack_depth(x_ref, first_ref, second_ref):
-    odd = parity("depth")
-    start = (SLABS - 2) * (1 - odd)
-    for row in range(ROWS):
+def pack_depth(x_ref, first_ref, second_ref, sems):
+    start = (SLABS - 2) * (1 - parity("depth"))
+    copies = []
+    for i, (ref, slab) in enumerate(((second_ref, (SLABS - 2) - start), (first_ref, start))):
         for k in range(2):
-            first_ref[k, row] = cells(x_ref, row, start + k)
-            second_ref[k, row] = cells(x_ref, row, (SLABS - 2) - start + k)
+            copies.append(pltpu.make_async_copy(x_ref.at[:, slab + k], ref.at[k], sems.at[i, k]))
+    for copy in copies:
+        copy.start()
+    for copy in copies:
+        copy.wait()
 
 
 def by_parity(odd, first, second):
@@ -231,7 +234,8 @@
         total = over(front, [mid_ref[c, here] for c in range(4)])
         total = shade(s[:, 2:4], facing[:, 2:4], total, *color)
         for c in range(4):
-            part_ref[c, here] = total[c]
+            at = pl.multiple_of((c * ROWS + row) * SUB, SUB)
+            part_ref[pl.ds(at, 2 * SUB), :] = total[c].reshape(2 * SUB, LANE)
         return 0
 
     lax.fori_loop(0, (ROWS - 4) // 2, third, 0, unroll=True)
@@ -251,8 +255,8 @@
         sk_ref[i, 7] = s_ref[row, 3]
 
 
-def render_rows(ext_ref, cmap_ref, light_ref, strip_first_ref, strip_second_ref, part_ref, zk_ref,
-                facing_ref, sk_ref, out_ref, halo_ref, all_ref):
+def render_rows(ext_ref, cmap_ref, light_ref, strip_first_ref, strip_second_ref, _, zk_ref,
+                facing_ref, sk_ref, out_ref, all_ref, halo_ref):
     light, color = coefficients(ext_ref, cmap_ref, light_ref)
     odd_strip = parity("strip")
     edge_before, edge_after = ends_inside("depth")
@@ -288,11 +292,7 @@
         finish(1 + (ROWS - 3) * half, sk_ref[pl.ds(half, 1)], facing_ref[pl.ds(2 * half + 1, 1)] + inward)
         return 0
 
-    lax.fori_loop(0, 2, boundary, 0)
-    for c in range(4):
-        for row in range(2, ROWS - 2):
-            all_ref[(c * ROWS + row) * SUB : (c * ROWS + row + 1) * SUB, :] = part_ref[c, row]
-
+    lax.fori_loop(0, 2, boundary, 0, unroll=True)
     group = 1
     chunk = lax.broadcasted_iota(jnp.int32, (group, SUB, LANE), 2) // 16
     for start in range(0, SUB, group):
@@ -360,17 +360,20 @@
         return out
 
     packed = pl.pallas_call(
-        pack_depth, in_specs=[VM], compiler_params=SMALL, out_specs=[VM, VM], name="pack_depth",
-        out_shape=[f32(2, ROWS, SUB, LANE)] * 2,
-    )(*near(x))
+        pack_depth, in_specs=[pl.BlockSpec(memory_space=pltpu.HBM)], out_specs=[VM, VM],
+        compiler_params=SMALL, name="pack_depth",
+        out_shape=[f32(2, ROWS * SUB, 1, LANE)] * 2,
+        scratch_shapes=[pltpu.SemaphoreType.DMA((2, 2))],
+    )(pltpu.with_memory_space_constraint(x.reshape(ROWS * SUB, SLABS, 1, LANE), pltpu.HBM))
+    packed = [v.reshape(2, ROWS, SUB, LANE) for v in packed]
     near_depth = exchange(packed, "depth")
 
     params = (extinction, color_map, light_direction)
 
-    def kernel(body, operands, shapes, scratch=()):
+    def kernel(body, operands, shapes, scratch=(), aliases={}):
         return pl.pallas_call(
             body, in_specs=[SM] * 3 + [VM] * len(operands), out_specs=[VM] * len(shapes),
-            compiler_params=SMALL, out_shape=[f32(*shape) for shape in shapes],
+            compiler_params=SMALL, input_output_aliases=aliases, out_shape=[f32(*shape) for shape in shapes],
             scratch_shapes=[f32(*shape) for shape in scratch],
         )(*params, *near(*operands))
 
@@ -388,12 +391,12 @@
     )
     kept = kernel(
         render_outer, (x, *near_depth, zi, ui, wi, api, ami, yi, si, mid),
-        [(4, ROWS, SUB, LANE), (4, SLABS + 2, SUB, LANE), (4, SLABS, SUB, LANE), (2, SLABS, SUB, LANE)],
+        [(4 * ROWS * SUB, LANE), (4, SLABS + 2, SUB, LANE), (4, SLABS, SUB, LANE), (2, SLABS, SUB, LANE)],
         [four] * 5,
     )
-    (blocks,) = kernel(
-        render_rows, (*near_strip, *kept),
-        [(groups * SUB, LANE)], [(4, SLABS + 2, SUB, LANE), (4 * ROWS * SUB, LANE)],
+    blocks, _ = kernel(
+        render_rows, (*near_strip, *kept), [(groups * SUB, LANE), (4 * ROWS * SUB, LANE)],
+        [(4, SLABS + 2, SUB, LANE)], {5: 1},
     )
     layers = lax.all_to_all(
         blocks.reshape(groups, SUB, LANE), "depth", split_axis=0, concat_axis=0, tiled=True

time: 53 us -> 52.6 us (level)
  the two profiles are of different devices: /device:TPU:4 before, /device:TPU:2 now
where the time goes in v6:
time: 52.6 us; the launch traced here: 52.4 us
  blocking collectives  29.5 us (56%)
  starting transfers between devices  14.1 us (27%)
  Pallas kernels  5.96 us (11%)
  waiting for transfers between devices  1.3 us (2%)
  local copies, waits for them, and re-layouts  0.76 us (1%)
  between operations  0.75 us (1%)
    all_to_all x1, blocking collectives, local(): lax.all_to_all(blocks.reshape(groups, SUB, LANE), 'depth', split_axis=0,...  29.5 us
    ppermute x4, starting transfers between devices, exchange(): out.append(lax.ppermute(v, axis, p))  14.1 us
    pallas_call x3, Pallas kernels, kernel(): pl.pallas_call(body, in_specs=[SM] * 3 + [VM] * len(operands), out_specs=...  3.98 us
    ppermute x4, waiting for transfers between devices, exchange(): out.append(lax.ppermute(v, axis, p))  1.3 us
  transfers between devices with their start and end apart: 4, of which 2 were waited for; matrix products, arithmetic and copies ran while one was open for 0% of the time, Pallas kernels for 5%

profile of v6, /device:TPU:2, one launch (start us, length us, event | category | flops | bytes accessed | tf_op | source)
XLA Modules:
  0.0 52.4 jit_solution(4589595780078564829)
XLA Ops:
  0.0 0.0 copy-start
  0.0 1.0 %pack_depth.1 = (f32[2,128,1,128]{3,2,1,0:T(1,128)S(1)}, f32[2,128,1,128]{3,2,1,0:T(1,128)S(1)}) custom-call(f32[128,8,1,128]{3,2,1,0:T(1,128)} %bitcast.12), custom_call_target="tpu_custom_call" | custom-call | tf_op jit(solution)/shard_map/pack_depth/pallas_call | solution.py:362
  1.0 0.7 %collective-permute-start.1 = (f32[2,16,8,128]{3,2,1,0:T(8,128)S(1)}, f32[2,16,8,128]{3,2,1,0:T(8,128)S(1)}, u32[]{:S(2)}, u32[]{:S(2)}) collective-permute-start(f32[2,16,8,128]{3,2,1,0:T(8,128)S(1)} %bitcast.20), channel_id=1, source_target_pairs={{8,16},{24,32},{40,48},{56,64},{72,80},{88,96},{104,112},{120,128}... | collective-permute-start | bytes 393224 | tf_op jit(solution)/shard_map/ppermute | solution.py:359
  1.7 0.0 copy-start.2
  1.7 6.3 %collective-permute-start = (f32[2,16,8,128]{3,2,1,0:T(8,128)S(1)}, f32[2,16,8,128]{3,2,1,0:T(8,128)S(1)}, u32[]{:S(2)}, u32[]{:S(2)}) collective-permute-start(f32[2,16,8,128]{3,2,1,0:T(8,128)S(1)} %bitcast.18), channel_id=1, source_target_pairs={{0,8},{16,24},{32,40},{48,56},{64,72},{80,88},{96,104},{112,120},{... | collective-permute-start | bytes 393224 | tf_op jit(solution)/shard_map/ppermute | solution.py:359
  8.7 0.0 copy-done.2
  8.7 0.1 copy.8.cmap_ref
  8.8 0.0 copy-start.1
  8.8 0.0 copy-done
  8.8 0.7 %copy-done.1 = f32[3]{0:T(128)S(1)} copy-done((f32[3]{0:T(128)S(1)}, f32[3]{0:T(128)}, u32[]{:S(2)}) %copy-start.1) | copy-done | bytes 36
  9.4 1.5 %shard_map.46 = (f32[16,6,8,128]{3,2,1,0:T(8,128)S(1)}, f32[16,4,8,128]{3,2,1,0:T(8,128)S(1)}, f32[16,4,8,128]{3,2,1,0:T(8,128)S(1)}, f32[16,4,8,128]{3,2,1,0:T(...) custom-call(f32[1]{0:T(128)S(6)} %copy.10.ext_ref, ...), custom_call_target="tpu_custom_call" | custom-call | tf_op jit(solution)/shard_map/pallas_call | solution.py:374
  10.9 0.0 collective-permute-done.1.from_second_ref.depth_second_ref
  10.9 0.3 collective-permute-done.from_first_ref.depth_first_ref
  11.3 1.9 %collective-permute-start.2 = (f32[12,2,8,128]{3,2,1,0:T(8,128)S(1)}, f32[12,2,8,128]{3,2,1,0:T(8,128)S(1)}, u32[]{:S(2)}, u32[]{:S(2)}) collective-permute-start(f32[12,2,8,128]{3,2,1,0:T(8,128)S(1)} %get-tuple-element.25), channel_id=1, source_target_pairs={{0,1},{2,3},{4,5},{6,7},{1,0},{3,2},{5,4},{7,6},{8,9},{10,11},{12,... | collective-permute-start | bytes 294920 | tf_op jit(solution)/shard_map/ppermute | solution.py:359
  13.2 5.2 %collective-permute-start.3 = (f32[12,2,8,128]{3,2,1,0:T(8,128)S(1)}, f32[12,2,8,128]{3,2,1,0:T(8,128)S(1)}, u32[]{:S(2)}, u32[]{:S(2)}) collective-permute-start(f32[12,2,8,128]{3,2,1,0:T(8,128)S(1)} %get-tuple-element.26), channel_id=1, source_target_pairs={{1,2},{3,4},{5,6},{2,1},{4,3},{6,5},{9,10},{11,12},{13,14},{10,9},... | collective-permute-start | bytes 294920 | tf_op jit(solution)/shard_map/ppermute | solution.py:359
  18.5 1.3 %shard_map.47 = (f32[512,128]{1,0:T(8,128)S(1)}, f32[4,10,8,128]{3,2,1,0:T(8,128)S(1)}, f32[4,8,8,128]{3,2,1,0:T(8,128)S(1)}, f32[2,8,8,128]{3,2,1,0:T(8,128)S(1)}) custom-call(f32[1]{0:T(128)S(6)} %copy.10.ext_ref, f32[3,2]{1,0:T(4,128)S(1)} %copy.8.cmap_ref, f32[3]{0:T(128)S(1)} %copy-done.1, f32[1024,128]{1,0:T(8,128)S(1)} %bitcast.15, ...), custom_call_target="tpu_custom_call" | custom-call | tf_op jit(solution)/shard_map/pallas_call | solution.py:374
  19.8 0.0 collective-permute-done.2.strip_first_ref
  19.8 1.0 %collective-permute-done.3.strip_second_ref = f32[12,2,8,128]{3,2,1,0:T(8,128)S(1)} collective-permute-done((f32[12,2,8,128]{3,2,1,0:T(8,128)S(1)}, f32[12,2,8,128]{3,2,1,0:T(8,128)S(1)}, u32[]{:S(2)}, u32[]{:S(2)}) %collective-permute-start.3) | collective-permute-done | bytes 98336 | tf_op jit(solution)/shard_map/ppermute | solution.py:359
  20.7 1.2 %shard_map.48 = (f32[512,128]{1,0:T(8,128)S(1)}, f32[512,128]{1,0:T(8,128)S(1)}) custom-call(f32[1]{0:T(128)S(6)} %copy.10.ext_ref, f32[3,2]{1,0:T(4,128)S(1)} %copy.8.cmap_ref, f32[3]{0:T(128)S(1)} %copy-done.1, f32[12,2,8,128]{3,2,1,0:T(8,128)S(1)} %collective-permute-done.2.strip_first_ref, ...), custom_call_target="tpu_custom_call", output_to_operand_aliasing={{1}: (5, {})} | custom-call | tf_op jit(solution)/shard_map/pallas_call | solution.py:374
  22.0 29.5 %all_to_all.5 = f32[64,8,128]{2,1,0:T(8,128)S(1)} all-to-all(f32[64,8,128]{2,1,0:T(8,128)S(1)} %bitcast.17), channel_id=1, replica_groups=mesh['depth'=64,'strip'=8] {'depth'}, dimensions={0} | all-to-all | bytes 524288 | tf_op jit(solution)/shard_map/all_to_all | solution.py:401
  51.4 0.9 %composite.1 = f32[64,16]{1,0:T(8,128)} custom-call(f32[512,128]{1,0:T(8,128)S(1)} %bitcast.16), custom_call_target="tpu_custom_call" | custom-call | tf_op jit(solution)/shard_map/composite/pallas_call | solution.py:404
  (1 shorter events, 0.0 us)
Async XLA Ops:
  0.0 8.8 %copy-start = (f32[16,8,1024]{2,1,0:T(8,128)S(1)}, f32[16,8,1024]{2,1,0:T(8,128)}, u32[]{:S(2)}) copy-start(f32[16,8,1024]{2,1,0:T(8,128)} %param.4) | copy-start | bytes 1572868
  1.0 9.9 %collective-permute-start.1 = (f32[2,16,8,128]{3,2,1,0:T(8,128)S(1)}, f32[2,16,8,128]{3,2,1,0:T(8,128)S(1)}, u32[]{:S(2)}, u32[]{:S(2)}) collective-permute-start(f32[2,16,8,128]{3,2,1,0:T(8,128)S(1)} %bitcast.20), channel_id=1, source_target_pairs={{8,16},{24,32},{40,48},{56,64},{72,80},{88,96},{104,112},{120,128}... | collective-permute-start | bytes 393224 | tf_op jit(solution)/shard_map/ppermute | solution.py:359
  1.7 7.0 %copy-start.2 = (f32[3,2]{0,1:T(2,128)S(1)}, f32[3,2]{0,1:T(2,128)}, u32[]{:S(2)}) copy-start(f32[3,2]{0,1:T(2,128)} %param.6) | copy-start | bytes 76
  1.7 9.5 %collective-permute-start = (f32[2,16,8,128]{3,2,1,0:T(8,128)S(1)}, f32[2,16,8,128]{3,2,1,0:T(8,128)S(1)}, u32[]{:S(2)}, u32[]{:S(2)}) collective-permute-start(f32[2,16,8,128]{3,2,1,0:T(8,128)S(1)} %bitcast.18), channel_id=1, source_target_pairs={{0,8},{16,24},{32,40},{48,56},{64,72},{80,88},{96,104},{112,120},{... | collective-permute-start | bytes 393224 | tf_op jit(solution)/shard_map/ppermute | solution.py:359
  8.8 0.7 %copy-start.1 = (f32[3]{0:T(128)S(1)}, f32[3]{0:T(128)}, u32[]{:S(2)}) copy-start(f32[3]{0:T(128)} %light_ref.5) | copy-start | bytes 40
  11.3 8.5 %collective-permute-start.2 = (f32[12,2,8,128]{3,2,1,0:T(8,128)S(1)}, f32[12,2,8,128]{3,2,1,0:T(8,128)S(1)}, u32[]{:S(2)}, u32[]{:S(2)}) collective-permute-start(f32[12,2,8,128]{3,2,1,0:T(8,128)S(1)} %get-tuple-element.25), channel_id=1, source_target_pairs={{0,1},{2,3},{4,5},{6,7},{1,0},{3,2},{5,4},{7,6},{8,9},{10,11},{12,... | collective-permute-start | bytes 294920 | tf_op jit(solution)/shard_map/ppermute | solution.py:359
  13.2 7.5 %collective-permute-start.3 = (f32[12,2,8,128]{3,2,1,0:T(8,128)S(1)}, f32[12,2,8,128]{3,2,1,0:T(8,128)S(1)}, u32[]{:S(2)}, u32[]{:S(2)}) collective-permute-start(f32[12,2,8,128]{3,2,1,0:T(8,128)S(1)} %get-tuple-element.26), channel_id=1, source_target_pairs={{1,2},{3,4},{5,6},{2,1},{4,3},{6,5},{9,10},{11,12},{13,14},{10,9},... | collective-permute-start | bytes 294920 | tf_op jit(solution)/shard_map/ppermute | solution.py:359

commit v7 on v6

--- a/solution.py
+++ b/solution.py
@@ -102,15 +102,17 @@
     return y + p, y - p, y + y
 
 
-def shade(s, facing, front, ext, slopes, offsets):
-    half = 0.5 - 0.35 / (1.0 + facing * facing)
+def matter(s, ext, slopes, offsets):
     z = s + s
     soft = jnp.maximum(z, 0.0) + log1p_unit(jnp.exp(-jnp.abs(z)))
-    clear = jnp.exp(-ext * soft)
-    weight = (1.0 - clear) * half
-    tones = [jnp.tanh(a * s + b) + 1.0 for a, b in zip(slopes, offsets)]
+    return jnp.exp(-ext * soft), [jnp.tanh(a * s + b) + 1.0 for a, b in zip(slopes, offsets)]
+
+
+def shade(cells_matter, facing, front):
+    clear, tones = cells_matter
+    weight = (1.0 - clear) * (0.5 - 0.35 / (1.0 + facing * facing))
     total = front
-    for k in range(s.shape[1]):
+    for k in range(facing.shape[1]):
         if total is None:
             total = [weight[:, k] * t[:, k] for t in tones] + [clear[:, k]]
         else:
@@ -124,6 +126,11 @@
     return [f + through * c for f, c in zip(front[:3], back[:3])] + [through * back[3]]
 
 
+def turned(v, channel, half):
+    turn = 16 * (2 * channel + half)
+    return rolled(v, turn, 1) if turn else v
+
+
 def coefficients(ext_ref, cmap_ref, light_ref):
     light = [light_ref[i] for i in range(3)]
     slopes = [cmap_ref[c, 0] * 0.5 for c in range(3)]
@@ -142,7 +149,7 @@
 
 
 def render_inner(ext_ref, cmap_ref, light_ref, x_ref, _, z_ref, u_ref, w_ref, ap_ref, am_ref, y_ref,
-                 s_ref, mid_ref):
+                 s_ref, mid_ref, sides_ref, ends_ref):
     light, color = coefficients(ext_ref, cmap_ref, light_ref)
 
     def first(i, _):
@@ -172,17 +179,25 @@
         row = 2 * i + 2
         here = pl.ds(row, 2)
         facing = (ap_ref[pl.ds(row + 1, 2)] + am_ref[pl.ds(row - 1, 2)]) + y_ref[here]
-        total = shade(s_ref[here, 1:5], facing, None, *color)
+        clear, tones = matter(s_ref[here], *color)
+        total = shade((clear[:, 1:5], [t[:, 1:5] for t in tones]), facing, None)
         for c in range(4):
             mid_ref[c, here] = total[c]
+        for c, v in enumerate((*tones, clear)):
+            sides_ref[c, here, 0] = v[:, 0]
+            sides_ref[c, here, 1] = v[:, 5]
         return 0
 
     lax.fori_loop(0, (ROWS - 4) // 2, third, 0, unroll=True)
+    for i, row in enumerate((1, ROWS - 2)):
+        clear, tones = matter(s_ref[row : row + 1], *color)
+        for c, v in enumerate((*tones, clear)):
+            ends_ref[c, i] = v[0]
 
 
 def render_outer(ext_ref, cmap_ref, light_ref, x_ref, depth_first_ref, depth_second_ref, zi_ref,
-                 ui_ref, wi_ref, api_ref, ami_ref, yi_ref, si_ref, mid_ref, part_ref, zk_ref,
-                 facing_ref, sk_ref, z_ref, ap_ref, am_ref, y_ref, s_ref):
+                 ui_ref, wi_ref, api_ref, ami_ref, yi_ref, mid_ref, sides_ref, ends_ref,
+                 part_ref, zk_ref, facing_ref, known_ref, z_ref, ap_ref, am_ref, y_ref, s_ref):
     light, color = coefficients(ext_ref, cmap_ref, light_ref)
     odd_group = parity("depth")
     edge_before, edge_after = ends_inside("depth")
@@ -217,28 +232,29 @@
                 us = jnp.concatenate([ui_ref[here, 2:4], u[:, 2:4]], 1)
                 ws = jnp.concatenate([wi_ref[here, 2:4], w[:, 2:4]], 1)
             ap_ref[here, at], am_ref[here, at], y_ref[here, at] = gradient_parts(us, ws, light)
-        s_ref[here, 0] = s[:, 1]
-        s_ref[here, 1] = si_ref[here, 0]
-        s_ref[here, 2] = si_ref[here, 5]
-        s_ref[here, 3] = s[:, 2]
+        s_ref[here] = s[:, 1:3]
         return 0
 
     lax.fori_loop(0, (ROWS - 2) // PAIR, second, 0, unroll=True)
 
-    def third(i, _):
+    def third(i):
         row = 2 * i + 2
         here = pl.ds(row, 2)
         facing = (ap_ref[pl.ds(row + 1, 2)] + am_ref[pl.ds(row - 1, 2)]) + y_ref[here]
-        s = s_ref[here]
-        front = shade(s[:, 0:2], facing[:, 0:2], None, *color)
-        total = over(front, [mid_ref[c, here] for c in range(4)])
-        total = shade(s[:, 2:4], facing[:, 2:4], total, *color)
+        clear, tones = matter(s_ref[here], *color)
+        own, kept = (*tones, clear), [sides_ref[c, here] for c in range(4)]
+        front = [jnp.concatenate([a[:, :1], b[:, :1]], 1) for a, b in zip(own, kept)]
+        back = [jnp.concatenate([b[:, 1:], a[:, 1:]], 1) for a, b in zip(own, kept)]
+        total = shade((front[3], front[:3]), facing[:, 0:2], None)
+        total = over(total, [mid_ref[c, here] for c in range(4)])
+        total = shade((back[3], back[:3]), facing[:, 2:4], total)
         for c in range(4):
             at = pl.multiple_of((c * ROWS + row) * SUB, SUB)
-            part_ref[pl.ds(at, 2 * SUB), :] = total[c].reshape(2 * SUB, LANE)
-        return 0
-
-    lax.fori_loop(0, (ROWS - 4) // 2, third, 0, unroll=True)
+            part_ref[pl.ds(at, 2 * SUB), :] = turned(total[c], c, i // 3).reshape(2 * SUB, LANE)
+        return 0
+
+    for i in range((ROWS - 4) // 2):
+        third(i)
 
     def whole(inner, outer):
         return jnp.concatenate([outer[0:2], inner, outer[2:4]], 0)
@@ -250,13 +266,15 @@
     facing_ref[2] = whole(ami_ref[ROWS - 2], am_ref[ROWS - 2])
     facing_ref[3] = whole(ami_ref[ROWS - 3] + yi_ref[ROWS - 2], am_ref[ROWS - 3] + y_ref[ROWS - 2])
     for i, row in enumerate((1, ROWS - 2)):
-        sk_ref[i, 0] = s_ref[row, 0]
-        sk_ref[i, 1:7] = si_ref[row]
-        sk_ref[i, 7] = s_ref[row, 3]
+        clear, tones = matter(s_ref[row : row + 1], *color)
+        for c, v in enumerate((*tones, clear)):
+            known_ref[c, i, 0] = v[0, 0]
+            known_ref[c, i, 1:7] = ends_ref[c, i]
+            known_ref[c, i, 7] = v[0, 1]
 
 
 def render_rows(ext_ref, cmap_ref, light_ref, strip_first_ref, strip_second_ref, _, zk_ref,
-                facing_ref, sk_ref, out_ref, all_ref, halo_ref):
+                facing_ref, known_ref, out_ref, all_ref, halo_ref):
     light, color = coefficients(ext_ref, cmap_ref, light_ref)
     odd_strip = parity("strip")
     edge_before, edge_after = ends_inside("depth")
@@ -270,9 +288,9 @@
             for i, v in enumerate(z):
                 halo_ref[3 * half + (1 - 2 * half) * j, i] = v
 
-    def boundary(half, _):
-        sign = 1.0 - 2.0 * half.astype(jnp.float32)
-        inside = jnp.where(half == 0, edge_up, edge_down) * (1.0 / 64.0)
+    for half in range(2):
+        sign = 1.0 - 2.0 * half
+        inside = (edge_down if half else edge_up) * (1.0 / 64.0)
         outer, inner = halo_ref[2 * half], halo_ref[2 * half + 1]
         first, second = zk_ref[2 * half], zk_ref[2 * half + 1]
         mirrored = [light[0] * sign, light[1], light[2]]
@@ -281,32 +299,26 @@
             s = smoothed((lower + middle) + (middle + upper), factor)[None]
             return s[:, 1:-1], *gradient_parts(*column_parts(s), mirrored)
 
-        def finish(row, s, facing):
-            total = shade(s, facing, None, *color)
+        def finish(row, found, facing):
+            total = shade(found, facing, None)
             for c in range(4):
-                all_ref[pl.ds(pl.multiple_of((c * ROWS + row) * SUB, SUB), SUB), :] = total[c][0]
+                at = (c * ROWS + row) * SUB
+                all_ref[at : at + SUB, :] = turned(total[c], c, half)[0]
 
         _, _, beyond, _ = row_parts(outer, inner, first, inside)
         s, _, inward, own = row_parts(inner, first, second, 1.0 / 64.0)
-        finish((ROWS - 1) * half, s, facing_ref[pl.ds(2 * half, 1)] + beyond + own)
-        finish(1 + (ROWS - 3) * half, sk_ref[pl.ds(half, 1)], facing_ref[pl.ds(2 * half + 1, 1)] + inward)
-        return 0
-
-    lax.fori_loop(0, 2, boundary, 0, unroll=True)
-    group = 1
-    chunk = lax.broadcasted_iota(jnp.int32, (group, SUB, LANE), 2) // 16
-    for start in range(0, SUB, group):
-        v = []
-        for g in range(8):
-            tiles = [all_ref[pl.ds(g * 64 + start + t, SUB, stride=SUB), :] for t in range(group)]
-            v.append(rolled(jnp.stack(tiles), 16 * g, 1) if g else jnp.stack(tiles))
+        finish((ROWS - 1) * half, matter(s, *color), facing_ref[pl.ds(2 * half, 1)] + beyond + own)
+        known = [known_ref[c, half : half + 1] for c in range(4)]
+        finish(1 + (ROWS - 3) * half, (known[3], known[:3]), facing_ref[pl.ds(2 * half + 1, 1)] + inward)
+
+    chunk = lax.broadcasted_iota(jnp.int32, (SUB, LANE), 1) // 16
+    for tile in range(SUB):
+        v = [all_ref[pl.ds(g * 64 + tile, SUB, stride=SUB), :] for g in range(8)]
         for bit in (1, 2, 4):
             v = [jnp.where((chunk & bit) != 0, v[(k + bit) % 8], v[k]) for k in range(8)]
         for m in range(8):
-            block = rolled(v[-m % 8], LANE - 16 * m, 1) if m else v[0]
-            for t in range(group):
-                row = ((start + t) * 8 + m) * SUB
-                out_ref[row : row + SUB, :] = block[t]
+            row = (tile * 8 + m) * SUB
+            out_ref[row : row + SUB, :] = rolled(v[-m % 8], LANE - 16 * m, 1) if m else v[0]
 
 
 def composite(parts_ref, out_ref):
@@ -378,9 +390,10 @@
         )(*params, *near(*operands))
 
     four = (ROWS, 4, SUB, LANE)
-    zi, ui, wi, api, ami, yi, si, mid = kernel(
+    zi, ui, wi, api, ami, yi, _, mid, sides, ends = kernel(
         render_inner, (x, packed[0]),
-        [(ROWS, 6, SUB, LANE)] + [four] * 5 + [(ROWS, 6, SUB, LANE), (4, ROWS, SUB, LANE)],
+        [(ROWS, 6, SUB, LANE)] + [four] * 5
+        + [(ROWS, 6, SUB, LANE), (4, ROWS, SUB, LANE), (4, ROWS, 2, SUB, LANE), (4, 2, 6, SUB, LANE)],
     )
     near_strip = exchange(
         pl.pallas_call(
@@ -390,9 +403,9 @@
         "strip",
     )
     kept = kernel(
-        render_outer, (x, *near_depth, zi, ui, wi, api, ami, yi, si, mid),
-        [(4 * ROWS * SUB, LANE), (4, SLABS + 2, SUB, LANE), (4, SLABS, SUB, LANE), (2, SLABS, SUB, LANE)],
-        [four] * 5,
+        render_outer, (x, *near_depth, zi, ui, wi, api, ami, yi, mid, sides, ends),
+        [(4 * ROWS * SUB, LANE), (4, SLABS + 2, SUB, LANE), (4, SLABS, SUB, LANE), (4, 2, SLABS, SUB, LANE)],
+        [four] * 4 + [(ROWS, 2, SUB, LANE)],
     )
     blocks, _ = kernel(
         render_rows, (*near_strip, *kept), [(groups * SUB, LANE), (4 * ROWS * SUB, LANE)],

time: 52.6 us -> 52.6 us (level)
  Pallas kernels: 5.96 us -> 6.63 us
    pallas_call x3, Pallas kernels: 3.98 us -> 4.66 us  [kernel(): pl.pallas_call(body, in_specs=[SM] * 3 + [VM] * len(operands), out_specs=...]
  transfers between devices with their start and end apart: 4 -> 4, of which waited for: 2 -> 1; matrix products, arithmetic and copies ran while one was open for 0% -> 0% of each run, Pallas kernels for 5% -> 7%
where the time goes in v7:
time: 52.6 us; the launch traced here: 52.3 us
  blocking collectives  29.5 us (56%)
  starting transfers between devices  13.7 us (26%)
  Pallas kernels  6.63 us (13%)
  waiting for transfers between devices  1 us (2%)
  local copies, waits for them, and re-layouts  0.76 us (1%)
  between operations  0.72 us (1%)
    all_to_all x1, blocking collectives, local(): lax.all_to_all(blocks.reshape(groups, SUB, LANE), 'depth', split_axis=0,...  29.5 us
    ppermute x4, starting transfers between devices, exchange(): out.append(lax.ppermute(v, axis, p))  13.7 us
    pallas_call x3, Pallas kernels, kernel(): pl.pallas_call(body, in_specs=[SM] * 3 + [VM] * len(operands), out_specs=...  4.66 us
  transfers between devices with their start and end apart: 4, of which 1 were waited for; matrix products, arithmetic and copies ran while one was open for 0% of the time, Pallas kernels for 7%

profile of v7, /device:TPU:2, one launch (start us, length us, event | category | flops | bytes accessed | tf_op | source)
XLA Modules:
  0.0 52.3 jit_solution(14966511193235201265)
XLA Ops:
  0.0 0.0 copy-start
  0.0 1.0 %pack_depth.1 = (f32[2,128,1,128]{3,2,1,0:T(1,128)S(1)}, f32[2,128,1,128]{3,2,1,0:T(1,128)S(1)}) custom-call(f32[128,8,1,128]{3,2,1,0:T(1,128)} %bitcast.12), custom_call_target="tpu_custom_call" | custom-call | tf_op jit(solution)/shard_map/pack_depth/pallas_call | solution.py:374
  1.0 0.7 %collective-permute-start.1 = (f32[2,16,8,128]{3,2,1,0:T(8,128)S(1)}, f32[2,16,8,128]{3,2,1,0:T(8,128)S(1)}, u32[]{:S(2)}, u32[]{:S(2)}) collective-permute-start(f32[2,16,8,128]{3,2,1,0:T(8,128)S(1)} %bitcast.20), channel_id=1, source_target_pairs={{8,16},{24,32},{40,48},{56,64},{72,80},{88,96},{104,112},{120,128}... | collective-permute-start | bytes 393224 | tf_op jit(solution)/shard_map/ppermute | solution.py:371
  1.7 0.0 copy-start.2
  1.7 6.3 %collective-permute-start = (f32[2,16,8,128]{3,2,1,0:T(8,128)S(1)}, f32[2,16,8,128]{3,2,1,0:T(8,128)S(1)}, u32[]{:S(2)}, u32[]{:S(2)}) collective-permute-start(f32[2,16,8,128]{3,2,1,0:T(8,128)S(1)} %bitcast.18), channel_id=1, source_target_pairs={{0,8},{16,24},{32,40},{48,56},{64,72},{80,88},{96,104},{112,120},{... | collective-permute-start | bytes 393224 | tf_op jit(solution)/shard_map/ppermute | solution.py:371
  8.7 0.0 copy-done.2
  8.7 0.1 copy.8.cmap_ref
  8.8 0.0 copy-start.1
  8.8 0.0 copy-done
  8.8 0.7 %copy-done.1 = f32[3]{0:T(128)S(1)} copy-done((f32[3]{0:T(128)S(1)}, f32[3]{0:T(128)}, u32[]{:S(2)}) %copy-start.1) | copy-done | bytes 36
  9.4 2.2 %shard_map.46 = (f32[16,6,8,128]{3,2,1,0:T(8,128)S(1)}, f32[16,4,8,128]{3,2,1,0:T(8,128)S(1)}, f32[16,4,8,128]{3,2,1,0:T(8,128)S(1)}, f32[16,4,8,128]{3,2,1,0:T(...) custom-call(f32[1]{0:T(128)S(6)} %copy.10.ext_ref, ...), custom_call_target="tpu_custom_call" | custom-call | tf_op jit(solution)/shard_map/pallas_call | solution.py:386
  11.6 0.0 collective-permute-done.1.from_second_ref.depth_second_ref
  11.6 0.0 collective-permute-done.from_first_ref.depth_first_ref
  11.7 1.9 %collective-permute-start.2 = (f32[12,2,8,128]{3,2,1,0:T(8,128)S(1)}, f32[12,2,8,128]{3,2,1,0:T(8,128)S(1)}, u32[]{:S(2)}, u32[]{:S(2)}) collective-permute-start(f32[12,2,8,128]{3,2,1,0:T(8,128)S(1)} %get-tuple-element.26), channel_id=1, source_target_pairs={{0,1},{2,3},{4,5},{6,7},{1,0},{3,2},{5,4},{7,6},{8,9},{10,11},{12,... | collective-permute-start | bytes 294920 | tf_op jit(solution)/shard_map/ppermute | solution.py:371
  13.6 4.8 %collective-permute-start.3 = (f32[12,2,8,128]{3,2,1,0:T(8,128)S(1)}, f32[12,2,8,128]{3,2,1,0:T(8,128)S(1)}, u32[]{:S(2)}, u32[]{:S(2)}) collective-permute-start(f32[12,2,8,128]{3,2,1,0:T(8,128)S(1)} %get-tuple-element.27), channel_id=1, source_target_pairs={{1,2},{3,4},{5,6},{2,1},{4,3},{6,5},{9,10},{11,12},{13,14},{10,9},... | collective-permute-start | bytes 294920 | tf_op jit(solution)/shard_map/ppermute | solution.py:371
  18.5 1.3 %shard_map.47 = (f32[512,128]{1,0:T(8,128)S(1)}, f32[4,10,8,128]{3,2,1,0:T(8,128)S(1)}, f32[4,8,8,128]{3,2,1,0:T(8,128)S(1)}, f32[4,2,8,8,128]{4,3,2,1,0:T(8,128)S(1)}) custom-call(f32[1]{0:T(128)S(6)} %copy.10.ext_ref, f32[3,2]{1,0:T(4,128)S(1)} %copy.8.cmap_ref, f32[3]{0:T(128)S(1)} %copy-done.1, f32[1024,128]{1,0:T(8,128)S(1)} %bitcast.15, ...), custom_call_target="tpu_custom_call" | custom-call | tf_op jit(solution)/shard_map/pallas_call | solution.py:386
  19.7 0.0 collective-permute-done.2.strip_first_ref
  19.7 1.0 %collective-permute-done.3.strip_second_ref = f32[12,2,8,128]{3,2,1,0:T(8,128)S(1)} collective-permute-done((f32[12,2,8,128]{3,2,1,0:T(8,128)S(1)}, f32[12,2,8,128]{3,2,1,0:T(8,128)S(1)}, u32[]{:S(2)}, u32[]{:S(2)}) %collective-permute-start.3) | collective-permute-done | bytes 98336 | tf_op jit(solution)/shard_map/ppermute | solution.py:371
  20.7 1.2 %shard_map.48 = (f32[512,128]{1,0:T(8,128)S(1)}, f32[512,128]{1,0:T(8,128)S(1)}) custom-call(f32[1]{0:T(128)S(6)} %copy.10.ext_ref, f32[3,2]{1,0:T(4,128)S(1)} %copy.8.cmap_ref, f32[3]{0:T(128)S(1)} %copy-done.1, f32[12,2,8,128]{3,2,1,0:T(8,128)S(1)} %collective-permute-done.2.strip_first_ref, ...), custom_call_target="tpu_custom_call", output_to_operand_aliasing={{1}: (5, {})} | custom-call | tf_op jit(solution)/shard_map/pallas_call | solution.py:386
  21.9 29.5 %all_to_all.5 = f32[64,8,128]{2,1,0:T(8,128)S(1)} all-to-all(f32[64,8,128]{2,1,0:T(8,128)S(1)} %bitcast.17), channel_id=1, replica_groups=mesh['depth'=64,'strip'=8] {'depth'}, dimensions={0} | all-to-all | bytes 524288 | tf_op jit(solution)/shard_map/all_to_all | solution.py:414
  51.4 0.9 %composite.1 = f32[64,16]{1,0:T(8,128)} custom-call(f32[512,128]{1,0:T(8,128)S(1)} %bitcast.16), custom_call_target="tpu_custom_call" | custom-call | tf_op jit(solution)/shard_map/composite/pallas_call | solution.py:417
  (1 shorter events, 0.0 us)
Async XLA Ops:
  0.0 8.8 %copy-start = (f32[16,8,1024]{2,1,0:T(8,128)S(1)}, f32[16,8,1024]{2,1,0:T(8,128)}, u32[]{:S(2)}) copy-start(f32[16,8,1024]{2,1,0:T(8,128)} %param.4) | copy-start | bytes 1572868
  1.0 10.6 %collective-permute-start.1 = (f32[2,16,8,128]{3,2,1,0:T(8,128)S(1)}, f32[2,16,8,128]{3,2,1,0:T(8,128)S(1)}, u32[]{:S(2)}, u32[]{:S(2)}) collective-permute-start(f32[2,16,8,128]{3,2,1,0:T(8,128)S(1)} %bitcast.20), channel_id=1, source_target_pairs={{8,16},{24,32},{40,48},{56,64},{72,80},{88,96},{104,112},{120,128}... | collective-permute-start | bytes 393224 | tf_op jit(solution)/shard_map/ppermute | solution.py:371
  1.7 7.0 %copy-start.2 = (f32[3,2]{0,1:T(2,128)S(1)}, f32[3,2]{0,1:T(2,128)}, u32[]{:S(2)}) copy-start(f32[3,2]{0,1:T(2,128)} %param.6) | copy-start | bytes 76
  1.7 9.9 %collective-permute-start = (f32[2,16,8,128]{3,2,1,0:T(8,128)S(1)}, f32[2,16,8,128]{3,2,1,0:T(8,128)S(1)}, u32[]{:S(2)}, u32[]{:S(2)}) collective-permute-start(f32[2,16,8,128]{3,2,1,0:T(8,128)S(1)} %bitcast.18), channel_id=1, source_target_pairs={{0,8},{16,24},{32,40},{48,56},{64,72},{80,88},{96,104},{112,120},{... | collective-permute-start | bytes 393224 | tf_op jit(solution)/shard_map/ppermute | solution.py:371
  8.8 0.7 %copy-start.1 = (f32[3]{0:T(128)S(1)}, f32[3]{0:T(128)}, u32[]{:S(2)}) copy-start(f32[3]{0:T(128)} %light_ref.5) | copy-start | bytes 40
  11.7 8.1 %collective-permute-start.2 = (f32[12,2,8,128]{3,2,1,0:T(8,128)S(1)}, f32[12,2,8,128]{3,2,1,0:T(8,128)S(1)}, u32[]{:S(2)}, u32[]{:S(2)}) collective-permute-start(f32[12,2,8,128]{3,2,1,0:T(8,128)S(1)} %get-tuple-element.26), channel_id=1, source_target_pairs={{0,1},{2,3},{4,5},{6,7},{1,0},{3,2},{5,4},{7,6},{8,9},{10,11},{12,... | collective-permute-start | bytes 294920 | tf_op jit(solution)/shard_map/ppermute | solution.py:371
  13.6 7.1 %collective-permute-start.3 = (f32[12,2,8,128]{3,2,1,0:T(8,128)S(1)}, f32[12,2,8,128]{3,2,1,0:T(8,128)S(1)}, u32[]{:S(2)}, u32[]{:S(2)}) collective-permute-start(f32[12,2,8,128]{3,2,1,0:T(8,128)S(1)} %get-tuple-element.27), channel_id=1, source_target_pairs={{1,2},{3,4},{5,6},{2,1},{4,3},{6,5},{9,10},{11,12},{13,14},{10,9},... | collective-permute-start | bytes 294920 | tf_op jit(solution)/shard_map/ppermute | solution.py:371

commit v8 on v7

--- a/solution.py
+++ b/solution.py
@@ -131,11 +131,9 @@
     return rolled(v, turn, 1) if turn else v
 
 
-def coefficients(ext_ref, cmap_ref, light_ref):
-    light = [light_ref[i] for i in range(3)]
-    slopes = [cmap_ref[c, 0] * 0.5 for c in range(3)]
-    offsets = [cmap_ref[c, 1] * 0.5 for c in range(3)]
-    return light, (ext_ref[0], slopes, offsets)
+def coefficients(splat_ref):
+    light, slopes, offsets = ([splat_ref[3 * i + c] for c in range(3)] for i in range(3))
+    return light, (splat_ref[9], slopes, offsets)
 
 
 def ends_inside(axis):
@@ -148,9 +146,13 @@
     return [a + b for a, b in zip(e, e[1:])]
 
 
-def render_inner(ext_ref, cmap_ref, light_ref, x_ref, _, z_ref, u_ref, w_ref, ap_ref, am_ref, y_ref,
+def render_inner(ext_ref, cmap_ref, light_ref, x_ref, _, splat_ref, z_ref, u_ref, w_ref, ap_ref, am_ref, y_ref,
                  s_ref, mid_ref, sides_ref, ends_ref):
-    light, color = coefficients(ext_ref, cmap_ref, light_ref)
+    values = [light_ref[c] for c in range(3)]
+    values += [cmap_ref[i, c] * 0.5 for i in range(2) for c in range(3)]
+    for i, v in enumerate((*values, ext_ref[0])):
+        splat_ref[i] = jnp.full((SUB, LANE), v, jnp.float32)
+    light, color = values[:3], (ext_ref[0], values[3:6], values[6:9])
 
     def first(i, _):
         for row in (2 * i, 2 * i + 1):
@@ -195,10 +197,10 @@
             ends_ref[c, i] = v[0]
 
 
-def render_outer(ext_ref, cmap_ref, light_ref, x_ref, depth_first_ref, depth_second_ref, zi_ref,
+def render_outer(splat_ref, x_ref, depth_first_ref, depth_second_ref, zi_ref,
                  ui_ref, wi_ref, api_ref, ami_ref, yi_ref, mid_ref, sides_ref, ends_ref,
                  part_ref, zk_ref, facing_ref, known_ref, z_ref, ap_ref, am_ref, y_ref, s_ref):
-    light, color = coefficients(ext_ref, cmap_ref, light_ref)
+    light, color = coefficients(splat_ref)
     odd_group = parity("depth")
     edge_before, edge_after = ends_inside("depth")
 
@@ -273,9 +275,9 @@
             known_ref[c, i, 7] = v[0, 1]
 
 
-def render_rows(ext_ref, cmap_ref, light_ref, strip_first_ref, strip_second_ref, _, zk_ref,
+def render_rows(splat_ref, strip_first_ref, strip_second_ref, _, zk_ref,
                 facing_ref, known_ref, out_ref, all_ref, halo_ref):
-    light, color = coefficients(ext_ref, cmap_ref, light_ref)
+    light, color = coefficients(splat_ref)
     odd_strip = parity("strip")
     edge_before, edge_after = ends_inside("depth")
     edge_up, edge_down = ends_inside("strip")
@@ -380,20 +382,21 @@
     packed = [v.reshape(2, ROWS, SUB, LANE) for v in packed]
     near_depth = exchange(packed, "depth")
 
-    params = (extinction, color_map, light_direction)
-
-    def kernel(body, operands, shapes, scratch=(), aliases={}):
+    params = (extinction, color_map.T, light_direction)
+
+    def kernel(body, operands, shapes, scratch=(), aliases={}, params=()):
         return pl.pallas_call(
-            body, in_specs=[SM] * 3 + [VM] * len(operands), out_specs=[VM] * len(shapes),
+            body, in_specs=[SM] * len(params) + [VM] * len(operands), out_specs=[VM] * len(shapes),
             compiler_params=SMALL, input_output_aliases=aliases, out_shape=[f32(*shape) for shape in shapes],
             scratch_shapes=[f32(*shape) for shape in scratch],
         )(*params, *near(*operands))
 
     four = (ROWS, 4, SUB, LANE)
-    zi, ui, wi, api, ami, yi, _, mid, sides, ends = kernel(
+    splat, zi, ui, wi, api, ami, yi, _, mid, sides, ends = kernel(
         render_inner, (x, packed[0]),
-        [(ROWS, 6, SUB, LANE)] + [four] * 5
+        [(10, SUB, LANE), (ROWS, 6, SUB, LANE)] + [four] * 5
         + [(ROWS, 6, SUB, LANE), (4, ROWS, SUB, LANE), (4, ROWS, 2, SUB, LANE), (4, 2, 6, SUB, LANE)],
+        params=params,
     )
     near_strip = exchange(
         pl.pallas_call(
@@ -403,13 +406,13 @@
         "strip",
     )
     kept = kernel(
-        render_outer, (x, *near_depth, zi, ui, wi, api, ami, yi, mid, sides, ends),
+        render_outer, (splat, x, *near_depth, zi, ui, wi, api, ami, yi, mid, sides, ends),
         [(4 * ROWS * SUB, LANE), (4, SLABS + 2, SUB, LANE), (4, SLABS, SUB, LANE), (4, 2, SLABS, SUB, LANE)],
         [four] * 4 + [(ROWS, 2, SUB, LANE)],
     )
     blocks, _ = kernel(
-        render_rows, (*near_strip, *kept), [(groups * SUB, LANE), (4 * ROWS * SUB, LANE)],
-        [(4, SLABS + 2, SUB, LANE)], {5: 1},
+        render_rows, (splat, *near_strip, *kept), [(groups * SUB, LANE), (4 * ROWS * SUB, LANE)],
+        [(4, SLABS + 2, SUB, LANE)], {3: 1},
     )
     layers = lax.all_to_all(
         blocks.reshape(groups, SUB, LANE), "depth", split_axis=0, concat_axis=0, tiled=True

time: 52.6 us -> 52 us (0.989)
  Pallas kernels: 6.63 us -> 5.53 us
  waiting for transfers between devices: 1 us -> 1.53 us
    pallas_call x3, Pallas kernels: 4.66 us -> 3.55 us  [kernel(): pl.pallas_call(body, in_specs=[SM] * len(params) + [VM] * len(operands),...]
    ppermute x4, waiting for transfers between devices: 1 us -> 1.53 us  [exchange(): out.append(lax.ppermute(v, axis, p))]
  transfers between devices with their start and end apart: 4 -> 4, of which waited for: 1 -> 1; matrix products, arithmetic and copies ran while one was open for 0% -> 0% of each run, Pallas kernels for 7% -> 6%
where the time goes in v8:
time: 52 us; the launch traced here: 51.7 us
  blocking collectives  29.5 us (57%)
  starting transfers between devices  13.8 us (27%)
  Pallas kernels  5.53 us (11%)
  waiting for transfers between devices  1.53 us (3%)
  between operations  0.73 us (1%)
  local copies, waits for them, and re-layouts  0.66 us (1%)
    all_to_all x1, blocking collectives, local(): lax.all_to_all(blocks.reshape(groups, SUB, LANE), 'depth', split_axis=0,...  29.5 us
    ppermute x4, starting transfers between devices, exchange(): out.append(lax.ppermute(v, axis, p))  13.8 us
    pallas_call x3, Pallas kernels, kernel(): pl.pallas_call(body, in_specs=[SM] * len(params) + [VM] * len(operands),...  3.55 us
    ppermute x4, waiting for transfers between devices, exchange(): out.append(lax.ppermute(v, axis, p))  1.53 us
  transfers between devices with their start and end apart: 4, of which 1 were waited for; matrix products, arithmetic and copies ran while one was open for 0% of the time, Pallas kernels for 6%

profile of v8, /device:TPU:2, one launch (start us, length us, event | category | flops | bytes accessed | tf_op | source)
XLA Modules:
  0.0 51.7 jit_solution(9201299088501355283)
XLA Ops:
  0.0 0.0 copy-start
  0.0 1.0 %pack_depth.1 = (f32[2,128,1,128]{3,2,1,0:T(1,128)S(1)}, f32[2,128,1,128]{3,2,1,0:T(1,128)S(1)}) custom-call(f32[128,8,1,128]{3,2,1,0:T(1,128)} %bitcast.13), custom_call_target="tpu_custom_call" | custom-call | tf_op jit(solution)/shard_map/pack_depth/pallas_call | solution.py:376
  1.0 0.7 %collective-permute-start.1 = (f32[2,16,8,128]{3,2,1,0:T(8,128)S(1)}, f32[2,16,8,128]{3,2,1,0:T(8,128)S(1)}, u32[]{:S(2)}, u32[]{:S(2)}) collective-permute-start(f32[2,16,8,128]{3,2,1,0:T(8,128)S(1)} %bitcast.22), channel_id=1, source_target_pairs={{8,16},{24,32},{40,48},{56,64},{72,80},{88,96},{104,112},{120,128}... | collective-permute-start | bytes 393224 | tf_op jit(solution)/shard_map/ppermute | solution.py:373
  1.7 6.3 %collective-permute-start = (f32[2,16,8,128]{3,2,1,0:T(8,128)S(1)}, f32[2,16,8,128]{3,2,1,0:T(8,128)S(1)}, u32[]{:S(2)}, u32[]{:S(2)}) collective-permute-start(f32[2,16,8,128]{3,2,1,0:T(8,128)S(1)} %bitcast.19), channel_id=1, source_target_pairs={{0,8},{16,24},{32,40},{48,56},{64,72},{80,88},{96,104},{112,120},{... | collective-permute-start | bytes 393224 | tf_op jit(solution)/shard_map/ppermute | solution.py:373
  8.7 0.0 copy-start.1
  8.7 0.0 copy-start.2
  8.7 0.0 copy-done
  8.7 0.6 %copy-done.1 = f32[3,2]{0,1:T(2,128)S(1)} copy-done((f32[3,2]{0,1:T(2,128)S(1)}, f32[3,2]{0,1:T(2,128)}, u32[]{:S(2)}) %copy-start.1) | copy-done | bytes 48
  9.4 0.0 copy-done.2
  9.4 2.2 %shard_map.46 = (f32[10,8,128]{2,1,0:T(8,128)S(1)}, f32[16,6,8,128]{3,2,1,0:T(8,128)S(1)}, f32[16,4,8,128]{3,2,1,0:T(8,128)S(1)}, f32[16,4,8,128]{3,2,1,0:T(8,12...) custom-call(f32[1]{0:T(128)S(6)} %copy.7.ext_ref, ...), custom_call_target="tpu_custom_call" | custom-call | tf_op jit(solution)/shard_map/pallas_call | solution.py:388
  11.5 0.0 collective-permute-done.1.from_second_ref.depth_second_ref
  11.5 0.0 collective-permute-done.from_first_ref.depth_first_ref
  11.6 1.9 %collective-permute-start.2 = (f32[12,2,8,128]{3,2,1,0:T(8,128)S(1)}, f32[12,2,8,128]{3,2,1,0:T(8,128)S(1)}, u32[]{:S(2)}, u32[]{:S(2)}) collective-permute-start(f32[12,2,8,128]{3,2,1,0:T(8,128)S(1)} %get-tuple-element.28), channel_id=1, source_target_pairs={{0,1},{2,3},{4,5},{6,7},{1,0},{3,2},{5,4},{7,6},{8,9},{10,11},{12,... | collective-permute-start | bytes 294920 | tf_op jit(solution)/shard_map/ppermute | solution.py:373
  13.5 4.9 %collective-permute-start.3 = (f32[12,2,8,128]{3,2,1,0:T(8,128)S(1)}, f32[12,2,8,128]{3,2,1,0:T(8,128)S(1)}, u32[]{:S(2)}, u32[]{:S(2)}) collective-permute-start(f32[12,2,8,128]{3,2,1,0:T(8,128)S(1)} %get-tuple-element.29), channel_id=1, source_target_pairs={{1,2},{3,4},{5,6},{2,1},{4,3},{6,5},{9,10},{11,12},{13,14},{10,9},... | collective-permute-start | bytes 294920 | tf_op jit(solution)/shard_map/ppermute | solution.py:373
  18.4 0.8 %shard_map.47 = (f32[512,128]{1,0:T(8,128)S(1)}, f32[4,10,8,128]{3,2,1,0:T(8,128)S(1)}, f32[4,8,8,128]{3,2,1,0:T(8,128)S(1)}, f32[4,2,8,8,128]{4,3,2,1,0:T(8,128)S(1)}) custom-call(f32[10,8,128]{2,1,0:T(8,128)S(1)} %get-tuple-element.25.splat_ref, f32[1024,128]{1,0:T(8,128)S(1)} %bitcast.16, ...), custom_call_target="tpu_custom_call" | custom-call | tf_op jit(solution)/shard_map/pallas_call | solution.py:388
  19.2 0.0 collective-permute-done.2.strip_first_ref
  19.2 1.5 %collective-permute-done.3.strip_second_ref = f32[12,2,8,128]{3,2,1,0:T(8,128)S(1)} collective-permute-done((f32[12,2,8,128]{3,2,1,0:T(8,128)S(1)}, f32[12,2,8,128]{3,2,1,0:T(8,128)S(1)}, u32[]{:S(2)}, u32[]{:S(2)}) %collective-permute-start.3) | collective-permute-done | bytes 98336 | tf_op jit(solution)/shard_map/ppermute | solution.py:373
  20.7 0.6 %shard_map.48 = (f32[512,128]{1,0:T(8,128)S(1)}, f32[512,128]{1,0:T(8,128)S(1)}) custom-call(f32[10,8,128]{2,1,0:T(8,128)S(1)} %get-tuple-element.25.splat_ref, f32[12,2,8,128]{3,2,1,0:T(8,128)S(1)} %collective-permute-done.2.strip_first_ref, f32[12,2,8,128]{3,2,1,0:T(8,128)S(1)} %collective-permute-done.3.strip_second_ref, ...), custom_call_target="tpu_custom_call", output_to_operand_aliasing={{1}: (3, {})} | custom-call | tf_op jit(solution)/shard_map/pallas_call | solution.py:388
  21.4 29.5 %all_to_all.5 = f32[64,8,128]{2,1,0:T(8,128)S(1)} all-to-all(f32[64,8,128]{2,1,0:T(8,128)S(1)} %bitcast.18), channel_id=1, replica_groups=mesh['depth'=64,'strip'=8] {'depth'}, dimensions={0} | all-to-all | bytes 524288 | tf_op jit(solution)/shard_map/all_to_all | solution.py:417
  50.8 0.9 %composite.1 = f32[64,16]{1,0:T(8,128)} custom-call(f32[512,128]{1,0:T(8,128)S(1)} %bitcast.17), custom_call_target="tpu_custom_call" | custom-call | tf_op jit(solution)/shard_map/composite/pallas_call | solution.py:420
  (1 shorter events, 0.0 us)
Async XLA Ops:
  0.0 8.7 %copy-start = (f32[16,8,1024]{2,1,0:T(8,128)S(1)}, f32[16,8,1024]{2,1,0:T(8,128)}, u32[]{:S(2)}) copy-start(f32[16,8,1024]{2,1,0:T(8,128)} %param.4) | copy-start | bytes 1572868
  1.0 10.5 %collective-permute-start.1 = (f32[2,16,8,128]{3,2,1,0:T(8,128)S(1)}, f32[2,16,8,128]{3,2,1,0:T(8,128)S(1)}, u32[]{:S(2)}, u32[]{:S(2)}) collective-permute-start(f32[2,16,8,128]{3,2,1,0:T(8,128)S(1)} %bitcast.22), channel_id=1, source_target_pairs={{8,16},{24,32},{40,48},{56,64},{72,80},{88,96},{104,112},{120,128}... | collective-permute-start | bytes 393224 | tf_op jit(solution)/shard_map/ppermute | solution.py:373
  1.7 9.8 %collective-permute-start = (f32[2,16,8,128]{3,2,1,0:T(8,128)S(1)}, f32[2,16,8,128]{3,2,1,0:T(8,128)S(1)}, u32[]{:S(2)}, u32[]{:S(2)}) collective-permute-start(f32[2,16,8,128]{3,2,1,0:T(8,128)S(1)} %bitcast.19), channel_id=1, source_target_pairs={{0,8},{16,24},{32,40},{48,56},{64,72},{80,88},{96,104},{112,120},{... | collective-permute-start | bytes 393224 | tf_op jit(solution)/shard_map/ppermute | solution.py:373
  8.7 0.7 %copy-start.1 = (f32[3,2]{0,1:T(2,128)S(1)}, f32[3,2]{0,1:T(2,128)}, u32[]{:S(2)}) copy-start(f32[3,2]{0,1:T(2,128)} %param.6) | copy-start | bytes 76
  8.7 0.7 %copy-start.2 = (f32[3]{0:T(128)S(1)}, f32[3]{0:T(128)}, u32[]{:S(2)}) copy-start(f32[3]{0:T(128)} %light_ref.1) | copy-start | bytes 40
  11.6 7.6 %collective-permute-start.2 = (f32[12,2,8,128]{3,2,1,0:T(8,128)S(1)}, f32[12,2,8,128]{3,2,1,0:T(8,128)S(1)}, u32[]{:S(2)}, u32[]{:S(2)}) collective-permute-start(f32[12,2,8,128]{3,2,1,0:T(8,128)S(1)} %get-tuple-element.28), channel_id=1, source_target_pairs={{0,1},{2,3},{4,5},{6,7},{1,0},{3,2},{5,4},{7,6},{8,9},{10,11},{12,... | collective-permute-start | bytes 294920 | tf_op jit(solution)/shard_map/ppermute | solution.py:373
  13.5 7.2 %collective-permute-start.3 = (f32[12,2,8,128]{3,2,1,0:T(8,128)S(1)}, f32[12,2,8,128]{3,2,1,0:T(8,128)S(1)}, u32[]{:S(2)}, u32[]{:S(2)}) collective-permute-start(f32[12,2,8,128]{3,2,1,0:T(8,128)S(1)} %get-tuple-element.29), channel_id=1, source_target_pairs={{1,2},{3,4},{5,6},{2,1},{4,3},{6,5},{9,10},{11,12},{13,14},{10,9},... | collective-permute-start | bytes 294920 | tf_op jit(solution)/shard_map/ppermute | solution.py:373

commit v9 on v8

--- a/solution.py
+++ b/solution.py
@@ -9,7 +9,6 @@
 ROWS, SLABS, SUB, LANE = 16, 8, 8, 128
 PAIR = 2
 VM = pl.BlockSpec(memory_space=pltpu.VMEM)
-SM = pl.BlockSpec(memory_space=pltpu.SMEM)
 
 
 SMALL = pltpu.CompilerParams(vmem_limit_bytes=4 << 20)
@@ -146,13 +145,9 @@
     return [a + b for a, b in zip(e, e[1:])]
 
 
-def render_inner(ext_ref, cmap_ref, light_ref, x_ref, _, splat_ref, z_ref, u_ref, w_ref, ap_ref, am_ref, y_ref,
+def render_inner(splat_ref, x_ref, _, z_ref, u_ref, w_ref, ap_ref, am_ref, y_ref,
                  s_ref, mid_ref, sides_ref, ends_ref):
-    values = [light_ref[c] for c in range(3)]
-    values += [cmap_ref[i, c] * 0.5 for i in range(2) for c in range(3)]
-    for i, v in enumerate((*values, ext_ref[0])):
-        splat_ref[i] = jnp.full((SUB, LANE), v, jnp.float32)
-    light, color = values[:3], (ext_ref[0], values[3:6], values[6:9])
+    light, color = coefficients(splat_ref)
 
     def first(i, _):
         for row in (2 * i, 2 * i + 1):
@@ -382,21 +377,21 @@
     packed = [v.reshape(2, ROWS, SUB, LANE) for v in packed]
     near_depth = exchange(packed, "depth")
 
-    params = (extinction, color_map.T, light_direction)
-
-    def kernel(body, operands, shapes, scratch=(), aliases={}, params=()):
+    values = jnp.concatenate([light_direction, 0.5 * color_map.T.reshape(6), extinction])
+    splat = jnp.broadcast_to(values[:, None, None], (10, SUB, LANE))
+
+    def kernel(body, operands, shapes, scratch=(), aliases={}):
         return pl.pallas_call(
-            body, in_specs=[SM] * len(params) + [VM] * len(operands), out_specs=[VM] * len(shapes),
+            body, in_specs=[VM] * len(operands), out_specs=[VM] * len(shapes),
             compiler_params=SMALL, input_output_aliases=aliases, out_shape=[f32(*shape) for shape in shapes],
             scratch_shapes=[f32(*shape) for shape in scratch],
-        )(*params, *near(*operands))
+        )(*near(*operands))
 
     four = (ROWS, 4, SUB, LANE)
-    splat, zi, ui, wi, api, ami, yi, _, mid, sides, ends = kernel(
-        render_inner, (x, packed[0]),
-        [(10, SUB, LANE), (ROWS, 6, SUB, LANE)] + [four] * 5
+    zi, ui, wi, api, ami, yi, _, mid, sides, ends = kernel(
+        render_inner, (splat, x, packed[0]),
+        [(ROWS, 6, SUB, LANE)] + [four] * 5
         + [(ROWS, 6, SUB, LANE), (4, ROWS, SUB, LANE), (4, ROWS, 2, SUB, LANE), (4, 2, 6, SUB, LANE)],
-        params=params,
     )
     near_strip = exchange(
         pl.pallas_call(

time: 52 us -> 52 us (level)
  transfers between devices with their start and end apart: 4 -> 4, of which waited for: 1 -> 1; matrix products, arithmetic and copies ran while one was open for 0% -> 0% of each run, Pallas kernels for 6% -> 5%
where the time goes in v9:
time: 52 us; the launch traced here: 51.7 us
  blocking collectives  29.5 us (57%)
  starting transfers between devices  14.1 us (27%)
  Pallas kernels  5.02 us (10%)
  waiting for transfers between devices  1.57 us (3%)
  between operations  0.74 us (1%)
  local copies, waits for them, and re-layouts  0.73 us (1%)
    all_to_all x1, blocking collectives, local(): lax.all_to_all(blocks.reshape(groups, SUB, LANE), 'depth', split_axis=0,...  29.5 us
    ppermute x4, starting transfers between devices, exchange(): out.append(lax.ppermute(v, axis, p))  14.1 us
    pallas_call x3, Pallas kernels, kernel(): pl.pallas_call(body, in_specs=[VM] * len(operands), out_specs=[VM] * len(...  3.05 us
    ppermute x4, waiting for transfers between devices, exchange(): out.append(lax.ppermute(v, axis, p))  1.57 us
  transfers between devices with their start and end apart: 4, of which 1 were waited for; matrix products, arithmetic and copies ran while one was open for 0% of the time, Pallas kernels for 5%

profile of v9, /device:TPU:2, one launch (start us, length us, event | category | flops | bytes accessed | tf_op | source)
XLA Modules:
  0.0 51.7 jit_solution(16200135705941613093)
XLA Ops:
  0.0 0.0 copy-start
  0.0 1.0 %pack_depth.1 = (f32[2,128,1,128]{3,2,1,0:T(1,128)S(1)}, f32[2,128,1,128]{3,2,1,0:T(1,128)S(1)}) custom-call(f32[128,8,1,128]{3,2,1,0:T(1,128)} %bitcast.14), custom_call_target="tpu_custom_call" | custom-call | tf_op jit(solution)/shard_map/pack_depth/pallas_call | solution.py:371
  1.0 0.7 %collective-permute-start.1 = (f32[2,16,8,128]{3,2,1,0:T(8,128)S(1)}, f32[2,16,8,128]{3,2,1,0:T(8,128)S(1)}, u32[]{:S(2)}, u32[]{:S(2)}) collective-permute-start(f32[2,16,8,128]{3,2,1,0:T(8,128)S(1)} %bitcast.22), channel_id=1, source_target_pairs={{8,16},{24,32},{40,48},{56,64},{72,80},{88,96},{104,112},{120,128}... | collective-permute-start | bytes 393224 | tf_op jit(solution)/shard_map/ppermute | solution.py:368
  1.7 0.0 copy-start.1
  1.7 6.3 %collective-permute-start = (f32[2,16,8,128]{3,2,1,0:T(8,128)S(1)}, f32[2,16,8,128]{3,2,1,0:T(8,128)S(1)}, u32[]{:S(2)}, u32[]{:S(2)}) collective-permute-start(f32[2,16,8,128]{3,2,1,0:T(8,128)S(1)} %bitcast.20), channel_id=1, source_target_pairs={{0,8},{16,24},{32,40},{48,56},{64,72},{80,88},{96,104},{112,120},{... | collective-permute-start | bytes 393224 | tf_op jit(solution)/shard_map/ppermute | solution.py:368
  8.0 0.0 copy-done.1
  8.7 0.0 copy-start.2
  8.7 0.1 mul.11
  8.8 0.6 %copy-done.2 = f32[3]{0:T(128)S(1)} copy-done((f32[3]{0:T(128)S(1)}, f32[3]{0:T(128)}, u32[]{:S(2)}) %copy-start.2) | copy-done | bytes 36
  9.4 0.1 pad_maximum_fusion
  9.4 0.1 broadcast_in_dim.2.splat_ref
  9.5 0.0 copy-done
  9.5 1.7 %shard_map.46 = (f32[16,6,8,128]{3,2,1,0:T(8,128)S(1)}, f32[16,4,8,128]{3,2,1,0:T(8,128)S(1)}, f32[16,4,8,128]{3,2,1,0:T(8,128)S(1)}, f32[16,4,8,128]{3,2,1,0:T(...) custom-call(f32[10,8,128]{2,1,0:T(8,128)S(1)} %broadcast_in_dim.2.sp, ...), custom_call_target="tpu_custom_call" | custom-call | tf_op jit(solution)/shard_map/pallas_call | solution.py:384
  11.2 0.0 collective-permute-done.1.from_second_ref.depth_second_ref
  11.2 0.0 collective-permute-done.from_first_ref.depth_first_ref
  11.3 1.9 %collective-permute-start.2 = (f32[12,2,8,128]{3,2,1,0:T(8,128)S(1)}, f32[12,2,8,128]{3,2,1,0:T(8,128)S(1)}, u32[]{:S(2)}, u32[]{:S(2)}) collective-permute-start(f32[12,2,8,128]{3,2,1,0:T(8,128)S(1)} %get-tuple-element.26), channel_id=1, source_target_pairs={{0,1},{2,3},{4,5},{6,7},{1,0},{3,2},{5,4},{7,6},{8,9},{10,11},{12,... | collective-permute-start | bytes 294920 | tf_op jit(solution)/shard_map/ppermute | solution.py:368
  13.2 5.2 %collective-permute-start.3 = (f32[12,2,8,128]{3,2,1,0:T(8,128)S(1)}, f32[12,2,8,128]{3,2,1,0:T(8,128)S(1)}, u32[]{:S(2)}, u32[]{:S(2)}) collective-permute-start(f32[12,2,8,128]{3,2,1,0:T(8,128)S(1)} %get-tuple-element.27), channel_id=1, source_target_pairs={{1,2},{3,4},{5,6},{2,1},{4,3},{6,5},{9,10},{11,12},{13,14},{10,9},... | collective-permute-start | bytes 294920 | tf_op jit(solution)/shard_map/ppermute | solution.py:368
  18.5 0.8 %shard_map.47 = (f32[512,128]{1,0:T(8,128)S(1)}, f32[4,10,8,128]{3,2,1,0:T(8,128)S(1)}, f32[4,8,8,128]{3,2,1,0:T(8,128)S(1)}, f32[4,2,8,8,128]{4,3,2,1,0:T(8,128)S(1)}) custom-call(f32[10,8,128]{2,1,0:T(8,128)S(1)} %broadcast_in_dim.2.splat_ref, f32[1024,128]{1,0:T(8,128)S(1)} %bitcast.17, ...), custom_call_target="tpu_custom_call" | custom-call | tf_op jit(solution)/shard_map/pallas_call | solution.py:384
  19.2 0.0 collective-permute-done.2.strip_first_ref
  19.2 1.5 %collective-permute-done.3.strip_second_ref = f32[12,2,8,128]{3,2,1,0:T(8,128)S(1)} collective-permute-done((f32[12,2,8,128]{3,2,1,0:T(8,128)S(1)}, f32[12,2,8,128]{3,2,1,0:T(8,128)S(1)}, u32[]{:S(2)}, u32[]{:S(2)}) %collective-permute-start.3) | collective-permute-done | bytes 98336 | tf_op jit(solution)/shard_map/ppermute | solution.py:368
  20.7 0.6 %shard_map.48 = (f32[512,128]{1,0:T(8,128)S(1)}, f32[512,128]{1,0:T(8,128)S(1)}) custom-call(f32[10,8,128]{2,1,0:T(8,128)S(1)} %broadcast_in_dim.2.splat_ref, f32[12,2,8,128]{3,2,1,0:T(8,128)S(1)} %collective-permute-done.2.strip_first_ref, f32[12,2,8,128]{3,2,1,0:T(8,128)S(1)} %collective-permute-done.3.strip_second_ref, ...), custom_call_target="tpu_custom_call", output_to_operand_aliasing={{1}: (3, {})} | custom-call | tf_op jit(solution)/shard_map/pallas_call | solution.py:384
  21.4 29.5 %all_to_all.5 = f32[64,8,128]{2,1,0:T(8,128)S(1)} all-to-all(f32[64,8,128]{2,1,0:T(8,128)S(1)} %bitcast.19), channel_id=1, replica_groups=mesh['depth'=64,'strip'=8] {'depth'}, dimensions={0} | all-to-all | bytes 524288 | tf_op jit(solution)/shard_map/all_to_all | solution.py:412
  50.8 0.9 %composite.1 = f32[64,16]{1,0:T(8,128)} custom-call(f32[512,128]{1,0:T(8,128)S(1)} %bitcast.18), custom_call_target="tpu_custom_call" | custom-call | tf_op jit(solution)/shard_map/composite/pallas_call | solution.py:415
  (2 shorter events, 0.0 us)
Async XLA Ops:
  0.0 9.5 %copy-start = (f32[16,8,1024]{2,1,0:T(8,128)S(1)}, f32[16,8,1024]{2,1,0:T(8,128)}, u32[]{:S(2)}) copy-start(f32[16,8,1024]{2,1,0:T(8,128)} %param.4) | copy-start | bytes 1572868
  1.0 10.2 %collective-permute-start.1 = (f32[2,16,8,128]{3,2,1,0:T(8,128)S(1)}, f32[2,16,8,128]{3,2,1,0:T(8,128)S(1)}, u32[]{:S(2)}, u32[]{:S(2)}) collective-permute-start(f32[2,16,8,128]{3,2,1,0:T(8,128)S(1)} %bitcast.22), channel_id=1, source_target_pairs={{8,16},{24,32},{40,48},{56,64},{72,80},{88,96},{104,112},{120,128}... | collective-permute-start | bytes 393224 | tf_op jit(solution)/shard_map/ppermute | solution.py:368
  1.7 6.3 %copy-start.1 = (f32[3,2]{0,1:T(2,128)S(1)}, f32[3,2]{0,1:T(2,128)}, u32[]{:S(2)}) copy-start(f32[3,2]{0,1:T(2,128)} %param.6) | copy-start | bytes 76
  1.7 9.5 %collective-permute-start = (f32[2,16,8,128]{3,2,1,0:T(8,128)S(1)}, f32[2,16,8,128]{3,2,1,0:T(8,128)S(1)}, u32[]{:S(2)}, u32[]{:S(2)}) collective-permute-start(f32[2,16,8,128]{3,2,1,0:T(8,128)S(1)} %bitcast.20), channel_id=1, source_target_pairs={{0,8},{16,24},{32,40},{48,56},{64,72},{80,88},{96,104},{112,120},{... | collective-permute-start | bytes 393224 | tf_op jit(solution)/shard_map/ppermute | solution.py:368
  8.7 0.7 %copy-start.2 = (f32[3]{0:T(128)S(1)}, f32[3]{0:T(128)}, u32[]{:S(2)}) copy-start(f32[3]{0:T(128)} %param.7) | copy-start | bytes 40
  11.3 7.9 %collective-permute-start.2 = (f32[12,2,8,128]{3,2,1,0:T(8,128)S(1)}, f32[12,2,8,128]{3,2,1,0:T(8,128)S(1)}, u32[]{:S(2)}, u32[]{:S(2)}) collective-permute-start(f32[12,2,8,128]{3,2,1,0:T(8,128)S(1)} %get-tuple-element.26), channel_id=1, source_target_pairs={{0,1},{2,3},{4,5},{6,7},{1,0},{3,2},{5,4},{7,6},{8,9},{10,11},{12,... | collective-permute-start | bytes 294920 | tf_op jit(solution)/shard_map/ppermute | solution.py:368
  13.2 7.5 %collective-permute-start.3 = (f32[12,2,8,128]{3,2,1,0:T(8,128)S(1)}, f32[12,2,8,128]{3,2,1,0:T(8,128)S(1)}, u32[]{:S(2)}, u32[]{:S(2)}) collective-permute-start(f32[12,2,8,128]{3,2,1,0:T(8,128)S(1)} %get-tuple-element.27), channel_id=1, source_target_pairs={{1,2},{3,4},{5,6},{2,1},{4,3},{6,5},{9,10},{11,12},{13,14},{10,9},... | collective-permute-start | bytes 294920 | tf_op jit(solution)/shard_map/ppermute | solution.py:368

commit v10 on v9

--- a/solution.py
+++ b/solution.py
@@ -18,6 +18,10 @@
     return x_ref[pl.ds(row * 64 + slab, SUB, stride=SLABS), :]
 
 
+def halo_cells(halo_ref, row, k):
+    return halo_ref[pl.ds(row * 16 + k, SUB, stride=2), :]
+
+
 def parity(axis):
     return lax.axis_index(axis) % 2
 
@@ -26,8 +30,7 @@
     start = (SLABS - 2) * (1 - parity("depth"))
     copies = []
     for i, (ref, slab) in enumerate(((second_ref, (SLABS - 2) - start), (first_ref, start))):
-        for k in range(2):
-            copies.append(pltpu.make_async_copy(x_ref.at[:, slab + k], ref.at[k], sems.at[i, k]))
+        copies.append(pltpu.make_async_copy(x_ref.at[:, pl.ds(slab, 2)], ref, sems.at[i]))
     for copy in copies:
         copy.start()
     for copy in copies:
@@ -47,7 +50,7 @@
         for k in range(2):
             for j in range(2):
                 before, after = by_parity(
-                    group_odd, from_first_ref[j, row + k], from_second_ref[j, row + k]
+                    group_odd, halo_cells(from_first_ref, row + k, j), halo_cells(from_second_ref, row + k, j)
                 )
                 ref[j, k] = before
                 ref[SLABS + 2 + j, k] = after
@@ -202,7 +205,7 @@
     def first(i, _):
         for row in (2 * i, 2 * i + 1):
             ends = [
-                by_parity(odd_group, depth_first_ref[k, row], depth_second_ref[k, row])
+                by_parity(odd_group, halo_cells(depth_first_ref, row, k), halo_cells(depth_second_ref, row, k))
                 for k in range(2)
             ]
             z = binomial([ends[0][0], ends[1][0], cells(x_ref, row, 0), cells(x_ref, row, 1)])
@@ -371,10 +374,10 @@
     packed = pl.pallas_call(
         pack_depth, in_specs=[pl.BlockSpec(memory_space=pltpu.HBM)], out_specs=[VM, VM],
         compiler_params=SMALL, name="pack_depth",
-        out_shape=[f32(2, ROWS * SUB, 1, LANE)] * 2,
-        scratch_shapes=[pltpu.SemaphoreType.DMA((2, 2))],
+        out_shape=[f32(ROWS * SUB, 2, 1, LANE)] * 2,
+        scratch_shapes=[pltpu.SemaphoreType.DMA((2,))],
     )(pltpu.with_memory_space_constraint(x.reshape(ROWS * SUB, SLABS, 1, LANE), pltpu.HBM))
-    packed = [v.reshape(2, ROWS, SUB, LANE) for v in packed]
+    packed = [v.reshape(2 * ROWS * SUB, LANE) for v in packed]
     near_depth = exchange(packed, "depth")
 
     values = jnp.concatenate([light_direction, 0.5 * color_map.T.reshape(6), extinction])

time: 52 us -> 52 us (level)
  no operation moved by 1% of the time
where the time goes in v10:
time: 52 us; the launch traced here: 51.8 us
  blocking collectives  29.5 us (57%)
  starting transfers between devices  14.1 us (27%)
  Pallas kernels  5.03 us (10%)
  waiting for transfers between devices  1.58 us (3%)
  between operations  0.74 us (1%)
  local copies, waits for them, and re-layouts  0.73 us (1%)
    all_to_all x1, blocking collectives, local(): lax.all_to_all(blocks.reshape(groups, SUB, LANE), 'depth', split_axis=0,...  29.5 us
    ppermute x4, starting transfers between devices, exchange(): out.append(lax.ppermute(v, axis, p))  14.1 us
    pallas_call x3, Pallas kernels, kernel(): pl.pallas_call(body, in_specs=[VM] * len(operands), out_specs=[VM] * len(...  3.04 us
    ppermute x4, waiting for transfers between devices, exchange(): out.append(lax.ppermute(v, axis, p))  1.58 us
    pallas_call x1, Pallas kernels, local(): pl.pallas_call(pack_depth, in_specs=[pl.BlockSpec(memory_space=pltpu.HBM)...  1.04 us
  transfers between devices with their start and end apart: 4, of which 1 were waited for; matrix products, arithmetic and copies ran while one was open for 0% of the time, Pallas kernels for 5%

profile of v10, /device:TPU:2, one launch (start us, length us, event | category | flops | bytes accessed | tf_op | source)
XLA Modules:
  0.0 51.8 jit_solution(7573668449445836501)
XLA Ops:
  0.0 0.0 copy-start
  0.0 1.0 %pack_depth.1 = (f32[128,2,1,128]{3,2,1,0:T(1,128)S(1)}, f32[128,2,1,128]{3,2,1,0:T(1,128)S(1)}) custom-call(f32[128,8,1,128]{3,2,1,0:T(1,128)} %bitcast.14), custom_call_target="tpu_custom_call" | custom-call | tf_op jit(solution)/shard_map/pack_depth/pallas_call | solution.py:374
  1.1 0.7 %collective-permute-start.1 = (f32[256,128]{1,0:T(8,128)S(1)}, f32[256,128]{1,0:T(8,128)S(1)}, u32[]{:S(2)}, u32[]{:S(2)}) collective-permute-start(f32[256,128]{1,0:T(8,128)S(1)} %bitcast.22), channel_id=1, source_target_pairs={{8,16},{24,32},{40,48},{56,64},{72,80},{88,96},{104,112},{120,128}... | collective-permute-start | bytes 393224 | tf_op jit(solution)/shard_map/ppermute | solution.py:371
  1.7 0.0 copy-start.1
  1.7 6.3 %collective-permute-start = (f32[256,128]{1,0:T(8,128)S(1)}, f32[256,128]{1,0:T(8,128)S(1)}, u32[]{:S(2)}, u32[]{:S(2)}) collective-permute-start(f32[256,128]{1,0:T(8,128)S(1)} %bitcast.20), channel_id=1, source_target_pairs={{0,8},{16,24},{32,40},{48,56},{64,72},{80,88},{96,104},{112,120},{... | collective-permute-start | bytes 393224 | tf_op jit(solution)/shard_map/ppermute | solution.py:371
  8.1 0.0 copy-done.1
  8.7 0.0 copy-start.2
  8.7 0.1 mul.11
  8.8 0.6 %copy-done.2 = f32[3]{0:T(128)S(1)} copy-done((f32[3]{0:T(128)S(1)}, f32[3]{0:T(128)}, u32[]{:S(2)}) %copy-start.2) | copy-done | bytes 36
  9.4 0.1 pad_maximum_fusion
  9.5 0.1 broadcast_in_dim.2.splat_ref
  9.5 0.0 copy-done
  9.5 1.7 %shard_map.46 = (f32[16,6,8,128]{3,2,1,0:T(8,128)S(1)}, f32[16,4,8,128]{3,2,1,0:T(8,128)S(1)}, f32[16,4,8,128]{3,2,1,0:T(8,128)S(1)}, f32[16,4,8,128]{3,2,1,0:T(...) custom-call(f32[10,8,128]{2,1,0:T(8,128)S(1)} %broadcast_in_dim.2.sp, ...), custom_call_target="tpu_custom_call" | custom-call | tf_op jit(solution)/shard_map/pallas_call | solution.py:387
  11.2 0.0 collective-permute-done.1.from_second_ref.depth_second_ref
  11.2 0.0 collective-permute-done.from_first_ref.depth_first_ref
  11.3 1.9 %collective-permute-start.2 = (f32[12,2,8,128]{3,2,1,0:T(8,128)S(1)}, f32[12,2,8,128]{3,2,1,0:T(8,128)S(1)}, u32[]{:S(2)}, u32[]{:S(2)}) collective-permute-start(f32[12,2,8,128]{3,2,1,0:T(8,128)S(1)} %get-tuple-element.26), channel_id=1, source_target_pairs={{0,1},{2,3},{4,5},{6,7},{1,0},{3,2},{5,4},{7,6},{8,9},{10,11},{12,... | collective-permute-start | bytes 294920 | tf_op jit(solution)/shard_map/ppermute | solution.py:371
  13.2 5.2 %collective-permute-start.3 = (f32[12,2,8,128]{3,2,1,0:T(8,128)S(1)}, f32[12,2,8,128]{3,2,1,0:T(8,128)S(1)}, u32[]{:S(2)}, u32[]{:S(2)}) collective-permute-start(f32[12,2,8,128]{3,2,1,0:T(8,128)S(1)} %get-tuple-element.27), channel_id=1, source_target_pairs={{1,2},{3,4},{5,6},{2,1},{4,3},{6,5},{9,10},{11,12},{13,14},{10,9},... | collective-permute-start | bytes 294920 | tf_op jit(solution)/shard_map/ppermute | solution.py:371
  18.5 0.7 %shard_map.47 = (f32[512,128]{1,0:T(8,128)S(1)}, f32[4,10,8,128]{3,2,1,0:T(8,128)S(1)}, f32[4,8,8,128]{3,2,1,0:T(8,128)S(1)}, f32[4,2,8,8,128]{4,3,2,1,0:T(8,128)S(1)}) custom-call(f32[10,8,128]{2,1,0:T(8,128)S(1)} %broadcast_in_dim.2.splat_ref, f32[1024,128]{1,0:T(8,128)S(1)} %bitcast.17, ...), custom_call_target="tpu_custom_call" | custom-call | tf_op jit(solution)/shard_map/pallas_call | solution.py:387
  19.2 0.0 collective-permute-done.2.strip_first_ref
  19.2 1.5 %collective-permute-done.3.strip_second_ref = f32[12,2,8,128]{3,2,1,0:T(8,128)S(1)} collective-permute-done((f32[12,2,8,128]{3,2,1,0:T(8,128)S(1)}, f32[12,2,8,128]{3,2,1,0:T(8,128)S(1)}, u32[]{:S(2)}, u32[]{:S(2)}) %collective-permute-start.3) | collective-permute-done | bytes 98336 | tf_op jit(solution)/shard_map/ppermute | solution.py:371
  20.8 0.6 %shard_map.48 = (f32[512,128]{1,0:T(8,128)S(1)}, f32[512,128]{1,0:T(8,128)S(1)}) custom-call(f32[10,8,128]{2,1,0:T(8,128)S(1)} %broadcast_in_dim.2.splat_ref, f32[12,2,8,128]{3,2,1,0:T(8,128)S(1)} %collective-permute-done.2.strip_first_ref, f32[12,2,8,128]{3,2,1,0:T(8,128)S(1)} %collective-permute-done.3.strip_second_ref, ...), custom_call_target="tpu_custom_call", output_to_operand_aliasing={{1}: (3, {})} | custom-call | tf_op jit(solution)/shard_map/pallas_call | solution.py:387
  21.4 29.5 %all_to_all.5 = f32[64,8,128]{2,1,0:T(8,128)S(1)} all-to-all(f32[64,8,128]{2,1,0:T(8,128)S(1)} %bitcast.19), channel_id=1, replica_groups=mesh['depth'=64,'strip'=8] {'depth'}, dimensions={0} | all-to-all | bytes 524288 | tf_op jit(solution)/shard_map/all_to_all | solution.py:415
  50.8 0.9 %composite.1 = f32[64,16]{1,0:T(8,128)} custom-call(f32[512,128]{1,0:T(8,128)S(1)} %bitcast.18), custom_call_target="tpu_custom_call" | custom-call | tf_op jit(solution)/shard_map/composite/pallas_call | solution.py:418
  (2 shorter events, 0.0 us)
Async XLA Ops:
  0.0 9.5 %copy-start = (f32[16,8,1024]{2,1,0:T(8,128)S(1)}, f32[16,8,1024]{2,1,0:T(8,128)}, u32[]{:S(2)}) copy-start(f32[16,8,1024]{2,1,0:T(8,128)} %param.4) | copy-start | bytes 1572868
  1.1 10.2 %collective-permute-start.1 = (f32[256,128]{1,0:T(8,128)S(1)}, f32[256,128]{1,0:T(8,128)S(1)}, u32[]{:S(2)}, u32[]{:S(2)}) collective-permute-start(f32[256,128]{1,0:T(8,128)S(1)} %bitcast.22), channel_id=1, source_target_pairs={{8,16},{24,32},{40,48},{56,64},{72,80},{88,96},{104,112},{120,128}... | collective-permute-start | bytes 393224 | tf_op jit(solution)/shard_map/ppermute | solution.py:371
  1.7 6.3 %copy-start.1 = (f32[3,2]{0,1:T(2,128)S(1)}, f32[3,2]{0,1:T(2,128)}, u32[]{:S(2)}) copy-start(f32[3,2]{0,1:T(2,128)} %param.6) | copy-start | bytes 76
  1.7 9.5 %collective-permute-start = (f32[256,128]{1,0:T(8,128)S(1)}, f32[256,128]{1,0:T(8,128)S(1)}, u32[]{:S(2)}, u32[]{:S(2)}) collective-permute-start(f32[256,128]{1,0:T(8,128)S(1)} %bitcast.20), channel_id=1, source_target_pairs={{0,8},{16,24},{32,40},{48,56},{64,72},{80,88},{96,104},{112,120},{... | collective-permute-start | bytes 393224 | tf_op jit(solution)/shard_map/ppermute | solution.py:371
  8.7 0.7 %copy-start.2 = (f32[3]{0:T(128)S(1)}, f32[3]{0:T(128)}, u32[]{:S(2)}) copy-start(f32[3]{0:T(128)} %param.7) | copy-start | bytes 40
  11.3 7.9 %collective-permute-start.2 = (f32[12,2,8,128]{3,2,1,0:T(8,128)S(1)}, f32[12,2,8,128]{3,2,1,0:T(8,128)S(1)}, u32[]{:S(2)}, u32[]{:S(2)}) collective-permute-start(f32[12,2,8,128]{3,2,1,0:T(8,128)S(1)} %get-tuple-element.26), channel_id=1, source_target_pairs={{0,1},{2,3},{4,5},{6,7},{1,0},{3,2},{5,4},{7,6},{8,9},{10,11},{12,... | collective-permute-start | bytes 294920 | tf_op jit(solution)/shard_map/ppermute | solution.py:371
  13.2 7.5 %collective-permute-start.3 = (f32[12,2,8,128]{3,2,1,0:T(8,128)S(1)}, f32[12,2,8,128]{3,2,1,0:T(8,128)S(1)}, u32[]{:S(2)}, u32[]{:S(2)}) collective-permute-start(f32[12,2,8,128]{3,2,1,0:T(8,128)S(1)} %get-tuple-element.27), channel_id=1, source_target_pairs={{1,2},{3,4},{5,6},{2,1},{4,3},{6,5},{9,10},{11,12},{13,14},{10,9},... | collective-permute-start | bytes 294920 | tf_op jit(solution)/shard_map/ppermute | solution.py:371
